TPU v7x, 32 devices: a whole 2x2x4 slice. The times are simulated.
32 devices in a mesh: seq: 8 (over z, y), head: 4 (over x, core).
Axes of the slice: x: 2, y: 2, z: 4, core: 2. Of those that a mesh axis runs over, the one named last changes fastest.
Arguments:
- block_input: bfloat16 [16384, 1024], P('seq'), may hold values from -6 to 6
- first_gain: bfloat16 [1024], P('seq'), may hold values from 0.5 to 1.5
- query_weight: bfloat16 [1024, 1024], P('seq', 'head'), may hold values from -0.1875 to 0.1875
- key_weight: bfloat16 [1024, 1024], P('seq', 'head'), may hold values from -0.1875 to 0.1875
- value_weight: bfloat16 [1024, 1024], P('seq', 'head'), may hold values from -0.1875 to 0.1875
- beta_weight: bfloat16 [1024, 8], P('seq', 'head'), may hold values from -0.1875 to 0.1875
- conv_weight: bfloat16 [3, 4, 1024], P(None, None, 'head'), may hold values from -2.5 to 2.5
- head_gain: bfloat16 [128], replicated, may hold values from 0.5 to 1.5
- output_weight: bfloat16 [1024, 1024], P('seq', 'head'), may hold values from -0.1875 to 0.1875
- second_gain: bfloat16 [1024], P('seq'), may hold values from 0.5 to 1.5
- gate_weight: bfloat16 [1024, 2816], P('seq', 'head'), may hold values from -0.1875 to 0.1875
- up_weight: bfloat16 [1024, 2816], P('seq', 'head'), may hold values from -0.1875 to 0.1875
- down_weight: bfloat16 [1024, 2816], P('seq', 'head'), may hold values from -0.109375 to 0.109375
- lengths: int32 [4], replicated, may hold values from 64 to 8192, as said below
- cotangent: bfloat16 [16384, 1024], P('seq'), may hold values from -6 to 6
Outputs:
- block_output: bfloat16 [16384, 1024], P('seq', 'head')
- input_gradient: float32 [16384, 1024], P('seq', 'head')
- first_gradient: float32 [1024], P('seq')
- query_gradient: float32 [1024, 1024], P('seq', 'head')
- key_gradient: float32 [1024, 1024], P('seq', 'head')
- value_gradient: float32 [1024, 1024], P('seq', 'head')
- beta_gradient: float32 [1024, 8], P('seq', 'head')
- conv_gradient: float32 [3, 4, 1024], P(None, None, 'head')
- headnorm_gradient: float32 [128], replicated
- output_gradient: float32 [1024, 1024], P('seq', 'head')
- second_gradient: float32 [1024], P('seq')
- gate_gradient: float32 [1024, 2816], P('seq', 'head')
- up_gradient: float32 [1024, 2816], P('seq', 'head')
- down_gradient: float32 [1024, 2816], P('seq', 'head')
Inputs may be any that keep to these rules, and one draw needn't show every extreme that they name: `lengths`: 4 sequences packed one after another; each length is a multiple of 64, they sum to 16384, and one of them is exactly 8192 tokens long.
All inputs are finite; a program needn't handle non-finite values.
Results may differ from a plain program's by a relative error of at most 0.015.
Values may be sent and summed in bfloat16 or wider, within the bound.
A program may use at most 320 MiB of HBM per device.

v0:
```python
import jax
import jax.numpy as jnp
from jax import lax
from jax.sharding import PartitionSpec as P

GROUP = 64


HIGHEST = lax.Precision.HIGHEST


def from_behind(block, axis, distance):
    devices = range(lax.axis_size(axis))
    route = [(i - distance, i) for i in devices if i - distance in devices]
    return lax.ppermute(block, axis, route)


def entering(part, axis, combine, identity, reverse):
    count = lax.axis_size(axis)
    place = lax.axis_index(axis)
    ahead = count - 1 - place if reverse else place
    gathered = jax.tree.map(lambda a: lax.all_gather(a, axis), part)
    state = jax.tree.map(lambda a, e: jnp.zeros_like(a) + jnp.asarray(e, a.dtype), part, identity)

    def one(lap, state):
        source = count - 1 - lap if reverse else lap
        return combine(
            state, jax.tree.map(lambda a: lax.dynamic_index_in_dim(a, source, 0, False), gathered)
        )

    return lax.fori_loop(0, ahead, one, state)


def plain_product(left, right):
    return jnp.dot(left, right, preferred_element_type=jnp.float32)


def rows_product(left, right):
    return lax.dot_general(
        left, right, (((0,), (0,)), ((), ())), preferred_element_type=jnp.float32
    )


def cols_product(left, right):
    return lax.dot_general(
        left, right, (((1,), (1,)), ((), ())), preferred_element_type=jnp.float32
    )


def precise_product(spec, left, right):
    return jnp.einsum(spec, left, right, precision=HIGHEST)


def rms_scale(values, gain, epsilon):
    return values * lax.rsqrt(jnp.mean(values * values, axis=-1, keepdims=True) + epsilon) * gain


def head_norm(rows, gain, heads):
    shaped = rows.reshape(rows.shape[0], heads, -1)
    return rms_scale(shaped, gain, 1e-05).reshape(rows.shape)


def unit_heads(rows, heads):
    shaped = rows.reshape(rows.shape[0], heads, -1)
    scaled = shaped * lax.rsqrt(jnp.sum(shaped * shaped, axis=-1, keepdims=True) + 1e-06)
    return scaled.reshape(rows.shape)


def activate(padded, table, distance, heads):
    kernel = table.shape[0]
    count = padded.shape[0] - kernel + 1
    mixed = jnp.zeros((count, padded.shape[1]), jnp.float32)
    for offset in range(kernel):
        usable = (kernel - 1 - offset <= distance).astype(jnp.float32)[:, None]
        mixed = mixed + table[offset][None, :] * padded[offset : offset + count] * usable
    silued = jax.nn.silu(mixed)
    third = silued.shape[1] // 3
    return (
        unit_heads(silued[:, :third], heads),
        unit_heads(silued[:, third : 2 * third], heads),
        silued[:, 2 * third :],
    )


def tri_inverse(strict):
    eye = jnp.eye(strict.shape[-1], dtype=jnp.float32)
    result = eye - strict
    power = strict
    for rounds in range((strict.shape[-1] - 1).bit_length() - 1):
        power = precise_product("...ij,...jk->...ik", power, power)
        result = precise_product("...ij,...jk->...ik", result, eye + power)
    return result


def group_factors(key_rows, values, beta, key_gram):
    weighted_keys = key_rows * beta[..., None]
    inverse = tri_inverse(jnp.tril(beta[..., None] * key_gram, -1))
    weight_factor = precise_product("...ij,...jk->...ik", inverse, weighted_keys)
    update_factor = precise_product("...ij,...jk->...ik", inverse, values * beta[..., None])
    return (weight_factor, update_factor)


def group_apply(running_state, pieces):
    query_rows, key_rows, weight_factor, update_factor, scores, reset = pieces
    running_state = running_state * (1.0 - reset)
    fresh_state = update_factor - precise_product("wzu,wuy->wzy", weight_factor, running_state)
    score_matrix = jnp.tril(scores)
    output_rows = precise_product("wzu,wuy->wzy", query_rows, running_state) + precise_product(
        "dsw,dwo->dso", score_matrix, fresh_state
    )
    running_state = running_state + precise_product("flp,flt->fpt", key_rows, fresh_state)
    return (running_state, output_rows)


def apply_groups(query_rows, key_rows, weight_factor, update_factor, scores, running_state, resets):
    final, output_rows = lax.scan(
        group_apply,
        running_state,
        (query_rows, key_rows, weight_factor, update_factor, scores, resets),
    )
    return (output_rows, final)


def compose_pair(earlier, later):
    first_map, first_shift = earlier
    second_map, second_shift = later
    return (
        precise_product("hij,hjk->hik", second_map, first_map),
        precise_product("hij,hjk->hik", second_map, first_shift) + second_shift,
    )


def group_transforms(key_rows, weight_factor, update_factor, resets):
    eye = jnp.eye(key_rows.shape[-1], dtype=jnp.float32)
    maps = (eye - precise_product("...ck,...cl->...kl", key_rows, weight_factor)) * (1.0 - resets)[
        :, None, None, None
    ]
    shifts = precise_product("...ck,...cl->...kl", key_rows, update_factor)

    def absorb(carry, pieces):
        return (compose_pair(carry, pieces), None)

    start = (jnp.broadcast_to(eye, maps.shape[1:]), jnp.zeros(maps.shape[1:], jnp.float32))
    total, unused = lax.scan(absorb, start, (maps, shifts))
    return total


def to_groups(rows, heads):
    return rows.reshape(rows.shape[0] // GROUP, GROUP, heads, -1).transpose(0, 2, 1, 3)


def from_groups(blocks):
    return blocks.transpose(0, 2, 1, 3).reshape(
        blocks.shape[0] * blocks.shape[2], blocks.shape[1] * blocks.shape[3]
    )


def swiglu(gate_rows, up_rows):
    return jax.nn.silu(gate_rows) * up_rows


def body(
    block_input,
    first_gain,
    query_weight,
    key_weight,
    value_weight,
    beta_weight,
    conv_weight,
    head_gain,
    output_weight,
    second_gain,
    gate_weight,
    up_weight,
    down_weight,
    lengths,
    cotangent,
):
    tok_rows = block_input.shape[0]
    full_width = block_input.shape[1]
    heads = beta_weight.shape[1]
    columns = query_weight.shape[1]
    shard = full_width // lax.axis_size("head")
    column_start = lax.axis_index("head") * shard
    kernel = conv_weight.shape[1]
    pieces = (
        query_weight,
        key_weight,
        value_weight,
        beta_weight,
        output_weight,
        gate_weight,
        up_weight,
        down_weight,
        first_gain,
        second_gain,
    )
    gathered = (
        lax.all_gather(pieces[0], "seq", axis=0, tiled=True),
        lax.all_gather(pieces[1], "seq", axis=0, tiled=True),
        lax.all_gather(pieces[2], "seq", axis=0, tiled=True),
        lax.all_gather(pieces[3], "seq", axis=0, tiled=True),
        lax.all_gather(pieces[4], "seq", axis=0, tiled=True),
        lax.all_gather(pieces[5], "seq", axis=0, tiled=True),
        lax.all_gather(pieces[6], "seq", axis=0, tiled=True),
        lax.all_gather(pieces[7], "seq", axis=0, tiled=True),
        lax.all_gather(pieces[8], "seq", axis=0, tiled=True),
        lax.all_gather(pieces[9], "seq", axis=0, tiled=True),
    )
    (
        full_query,
        full_key,
        full_value,
        full_beta,
        full_output,
        full_gate,
        full_up,
        full_down,
        full_first,
        full_second,
    ) = gathered
    positions = lax.axis_index("seq") * tok_rows + jnp.arange(tok_rows, dtype=jnp.int32)
    ends = jnp.cumsum(lengths)
    starts = ends - lengths
    begun = starts[None, :] <= positions[:, None]
    distance = positions - jnp.max(jnp.where(begun, starts[None, :], 0), axis=1)
    resets = jnp.any(starts[None, :] == positions[::GROUP][:, None], axis=1).astype(jnp.float32)
    inputs = block_input.astype(jnp.float32)

    def first_norm(rows, gain):
        return rms_scale(rows, gain, 1e-06)

    first_normed, first_back = jax.vjp(first_norm, inputs, full_first.astype(jnp.float32))
    first_rows = first_normed.astype(jnp.bfloat16)
    projection = jnp.concatenate([full_query, full_key, full_value], 1)
    pre_conv = plain_product(first_rows, projection).astype(jnp.bfloat16)
    beta = jax.nn.sigmoid(plain_product(first_rows, full_beta))
    tails = from_behind(pre_conv[tok_rows - kernel + 1 :], "seq", 1)
    padded = jnp.concatenate([tails, pre_conv], 0).astype(jnp.float32)
    table = conv_weight.astype(jnp.float32).transpose(1, 0, 2).reshape(kernel, -1)

    def mixer_inputs(grid, taps):
        return activate(grid, taps, distance, heads)

    activated, activate_back = jax.vjp(mixer_inputs, padded, table)
    query_low = to_groups(activated[0].astype(jnp.bfloat16), heads)
    key_low = to_groups(activated[1].astype(jnp.bfloat16), heads)
    value_low = to_groups(activated[2].astype(jnp.bfloat16), heads)
    query_blocks = query_low.astype(jnp.float32)
    key_blocks = key_low.astype(jnp.float32)
    value_blocks = value_low.astype(jnp.float32)
    key_gram = jnp.einsum("ghik,ghjk->ghij", key_low, key_low, preferred_element_type=jnp.float32)
    scores = jnp.einsum("ghik,ghjk->ghij", query_low, key_low, preferred_element_type=jnp.float32)
    beta_blocks = beta.reshape(tok_rows // GROUP, GROUP, heads).transpose(0, 2, 1)
    (weight_factor, update_factor), factor_back = jax.vjp(
        group_factors, key_blocks, value_blocks, beta_blocks, key_gram
    )
    dev_map, dev_shift = group_transforms(key_blocks, weight_factor, update_factor, resets)
    eye_stack = jnp.broadcast_to(jnp.eye(dev_map.shape[-1], dtype=jnp.float32), dev_map.shape)
    empty_shift = jnp.zeros_like(dev_shift)
    prefix = entering((dev_map, dev_shift), "seq", compose_pair, (eye_stack, empty_shift), False)

    def run_groups(query_rows, key_rows, w_blocks, u_blocks, score_blocks, running_state):
        return apply_groups(
            query_rows, key_rows, w_blocks, u_blocks, score_blocks, running_state, resets
        )

    (delta_blocks, state_out), apply_back = jax.vjp(
        run_groups, query_blocks, key_blocks, weight_factor, update_factor, scores, prefix[1]
    )

    def output_norm(rows, gain):
        return head_norm(rows, gain, heads)

    normed_heads, head_back = jax.vjp(
        output_norm, from_groups(delta_blocks), head_gain.astype(jnp.float32)
    )
    head_rows = normed_heads.astype(jnp.bfloat16)
    branch = lax.psum(cols_product(head_rows, full_output), "head")
    middle = inputs + branch
    second_normed, second_back = jax.vjp(first_norm, middle, full_second.astype(jnp.float32))
    second_rows = second_normed.astype(jnp.bfloat16)
    gate = plain_product(second_rows, full_gate)
    up_rows = plain_product(second_rows, full_up)
    hidden_values, swish_back = jax.vjp(swiglu, gate, up_rows)
    hidden = hidden_values.astype(jnp.bfloat16)
    update = lax.psum_scatter(
        cols_product(hidden, full_down), "head", scatter_dimension=1, tiled=True
    )
    middle_shard = lax.dynamic_slice_in_dim(middle, column_start, shard, 1)
    block_output = (middle_shard + update).astype(jnp.bfloat16)
    down_grad = rows_product(cotangent, hidden)
    d_hidden = plain_product(cotangent, full_down)
    d_gate_values, d_up_values = swish_back(d_hidden)
    d_gate = d_gate_values.astype(jnp.bfloat16)
    d_up = d_up_values.astype(jnp.bfloat16)
    gate_grad = rows_product(second_rows, d_gate)
    up_grad = rows_product(second_rows, d_up)
    d_second = lax.psum(cols_product(d_gate, full_gate) + cols_product(d_up, full_up), "head")
    d_middle_norm, second_grad = second_back(d_second)
    d_middle = cotangent.astype(jnp.float32) + d_middle_norm
    d_branch = d_middle.astype(jnp.bfloat16)
    output_grad = rows_product(d_branch, head_rows)
    d_heads = plain_product(d_branch, full_output)
    d_delta, head_gain_part = head_back(d_heads)
    d_blocks = to_groups(d_delta, heads)
    local_part = apply_back((d_blocks, jnp.zeros_like(state_out)))
    back_prefix = entering(
        (jnp.swapaxes(dev_map, 1, 2), local_part[5]),
        "seq",
        compose_pair,
        (eye_stack, empty_shift),
        True,
    )
    carried_part = apply_back((jnp.zeros_like(delta_blocks), back_prefix[1]))
    d_w = local_part[2] + carried_part[2]
    d_u = local_part[3] + carried_part[3]
    d_scores = local_part[4] + carried_part[4]
    d_key_more, d_value_blocks, d_beta_blocks, d_gram = factor_back((d_w, d_u))
    d_gram_both = d_gram + jnp.swapaxes(d_gram, 2, 3)
    d_query_blocks = (
        local_part[0] + carried_part[0] + precise_product("ghij,ghjk->ghik", d_scores, key_blocks)
    )
    d_key_blocks = (
        local_part[1]
        + carried_part[1]
        + d_key_more
        + precise_product("ghji,ghjk->ghik", d_scores, query_blocks)
        + precise_product("ghij,ghjk->ghik", d_gram_both, key_blocks)
    )
    d_padded, table_grad = activate_back(
        (from_groups(d_query_blocks), from_groups(d_key_blocks), from_groups(d_value_blocks))
    )
    received = from_behind(d_padded[: kernel - 1], "seq", -1)
    d_local = d_padded[kernel - 1 :]
    d_pre = jnp.concatenate(
        [d_local[: tok_rows - kernel + 1], d_local[tok_rows - kernel + 1 :] + received], 0
    ).astype(jnp.bfloat16)
    d_beta = d_beta_blocks.transpose(0, 2, 1).reshape(tok_rows, heads)
    d_logits = (d_beta * beta * (1.0 - beta)).astype(jnp.bfloat16)
    qkv_grad = rows_product(first_rows, d_pre)
    beta_grad = rows_product(first_rows, d_logits)
    d_first_part = cols_product(d_pre, projection) + cols_product(d_logits, full_beta)
    first_scale = lax.rsqrt(jnp.mean(inputs * inputs, axis=-1, keepdims=True) + 1e-06)
    first_unit = inputs * first_scale
    first_partial = jnp.sum(d_first_part * first_unit, 0)
    d_first = lax.psum(d_first_part, "head")
    d_input_norm, unused_gain = first_back(d_first)
    input_gradient = lax.dynamic_slice_in_dim(d_middle + d_input_norm, column_start, shard, 1)
    conv_grad = table_grad.reshape(kernel, 3, -1).transpose(1, 0, 2)
    conv_empty = jnp.zeros((3, kernel, columns * lax.axis_size("head")), jnp.float32)
    conv_full = lax.dynamic_update_slice_in_dim(
        conv_empty, conv_grad, lax.axis_index("head") * columns, 2
    )
    conv_sum, headnorm_gradient, first_sum = lax.psum(
        (conv_full, head_gain_part, first_partial), ("seq", "head")
    )
    conv_gradient = lax.dynamic_slice_in_dim(conv_sum, lax.axis_index("head") * columns, columns, 2)
    first_piece = full_width // lax.axis_size("seq")
    first_gradient = lax.dynamic_slice_in_dim(
        first_sum, lax.axis_index("seq") * first_piece, first_piece, 0
    )
    query_grad = qkv_grad[:, :columns]
    key_grad = qkv_grad[:, columns : 2 * columns]
    value_grad = qkv_grad[:, 2 * columns :]
    summed = (
        lax.psum_scatter(query_grad, "seq", scatter_dimension=0, tiled=True),
        lax.psum_scatter(key_grad, "seq", scatter_dimension=0, tiled=True),
        lax.psum_scatter(value_grad, "seq", scatter_dimension=0, tiled=True),
        lax.psum_scatter(beta_grad, "seq", scatter_dimension=0, tiled=True),
        lax.psum_scatter(output_grad, "seq", scatter_dimension=0, tiled=True),
        lax.psum_scatter(gate_grad, "seq", scatter_dimension=0, tiled=True),
        lax.psum_scatter(up_grad, "seq", scatter_dimension=0, tiled=True),
        lax.psum_scatter(down_grad, "seq", scatter_dimension=0, tiled=True),
        lax.psum_scatter(second_grad, "seq", scatter_dimension=0, tiled=True),
    )
    (
        query_gradient,
        key_gradient,
        value_gradient,
        beta_gradient,
        output_gradient,
        gate_gradient,
        up_gradient,
        down_gradient,
        second_gradient,
    ) = summed
    return (
        block_output,
        input_gradient,
        first_gradient,
        query_gradient,
        key_gradient,
        value_gradient,
        beta_gradient,
        conv_gradient,
        headnorm_gradient,
        output_gradient,
        second_gradient,
        gate_gradient,
        up_gradient,
        down_gradient,
    )


def solution(mesh):
    return jax.shard_map(
        body,
        mesh=mesh,
        in_specs=(
            P("seq", None),
            P("seq"),
            P("seq", "head"),
            P("seq", "head"),
            P("seq", "head"),
            P("seq", "head"),
            P(None, None, "head"),
            P(),
            P("seq", "head"),
            P("seq"),
            P("seq", "head"),
            P("seq", "head"),
            P("seq", "head"),
            P(),
            P("seq", None),
        ),
        out_specs=(
            P("seq", "head"),
            P("seq", "head"),
            P("seq"),
            P("seq", "head"),
            P("seq", "head"),
            P("seq", "head"),
            P("seq", "head"),
            P(None, None, "head"),
            P(),
            P("seq", "head"),
            P("seq"),
            P("seq", "head"),
            P("seq", "head"),
            P("seq", "head"),
        ),
        check_vma=False,
    )
```

profile of v0, /device:TPU:0, one launch (start us, length us, event | category | flops | bytes accessed | tf_op | source)
XLA Modules:
  0.0 3240.6 jit_solution(2328518005033439527)
XLA Ops:
  7.2 33.2 %all_gather.55 = bf16[1024,256]{1,0:T(8,128)(2,1)S(1)} all-gather(bf16[128,256]{1,0:T(8,128)(2,1)} %param.29), channel_id=1, replica_groups=mesh['seq'=8,'head'=4] {'seq'}, dimensions={0}, use_global_device_ids=true | all-gather | bytes 589824 | tf_op jit(solution)/shard_map/all_gather | solution.py:199
  40.5 31.5 all_gather.56
  72.0 31.3 all_gather.57
  103.4 20.7 all-gather.4
  133.6 17.4 all_gather.58
  290.9 79.5 %while.122 = (s32[]{:T(128)}, f32[2,128,128]{2,1,0:T(8,128)S(1)}, f32[2,128,128]{2,1,0:T(8,128)S(1)}, f32[32,2,128,128]{3,2,1,0:T(8,128)}, f32[32,2,128,128]{3,2,1,0:T(8,128)}) while((s32[]{:T(128)}, f32[2,128,128]{2,1,0:T(8,128)S(1)}, f32[2,128,128]{2,1,0:T(8,128)S(1)}, f32[32,2,128,128]{3,2,1,0:T(8,128)}, ...), condition=%wide.region_6.7_spmd.clone.clone, body=%wide.region_5.6_spmd.clone.sunk.clone | while | flops 100728832 | bytes 1443410 | solution.py:144
  372.0 33.9 %all_gather.63 = bf16[1024,256]{1,0:T(8,128)(2,1)} all-gather(bf16[128,256]{1,0:T(8,128)(2,1)} %param.35), channel_id=1, replica_groups=mesh['seq'=8,'head'=4] {'seq'}, dimensions={0}, use_global_device_ids=true | all-gather | bytes 589824 | tf_op jit(solution)/shard_map/all_gather | solution.py:203
  413.2 39.0 %all-gather.22.cloned.1.call-done = f32[16,128,128]{2,1,0:T(8,128)} async-done(((f32[2,128,128]{2,1,0:T(8,128)}), f32[16,128,128]{2,1,0:T(8,128)}) %all-gather.22.cloned.1.call-update) | async-done | bytes 1048592 | tf_op jit(solution)/shard_map/all_gather | solution.py:22
  455.3 356.3 %while.121 = (s32[]{:T(128)}, f32[2,128,128]{2,1,0:T(8,128)S(1)}, f32[32,2,64,128]{3,2,1,0:T(8,128)}, f32[32]{0:T(128)S(1)}, f32[32,2,128,128]{3,2,1,0:T(8,128)}...) while((s32[]{:T(128)}, f32[2,128,128]{2,1,0:T(8,128)S(1)}, ...), condition=%wide.region_11.12_spmd.clone.clone.clone, body=%wide.region_10.11_spmd.clone.clone.sunk.clone | while | flops 88293376 | bytes 1815337 | solution.py:116
  832.0 27.2 all-gather.5
  859.2 131.7 %all-reduce.17.cloned.1.call-done = f32[2048,1024]{1,0:T(8,128)} async-done(((f32[2048,1024]{1,0:T(8,128)}), f32[2048,1024]{1,0:T(8,128)}) %all-reduce.17.cloned.1.call-update) | async-done | bytes 8388624 | tf_op jit(solution)/shard_map/psum | solution.py:279
  1002.7 34.2 %all-gather.14.cloned.1.call-done = bf16[1024,704]{0,1:T(8,128)(2,1)} async-done(((bf16[128,704]{0,1:T(8,128)(2,1)}), bf16[1024,704]{0,1:T(8,128)(2,1)}) %all-gather.14.cloned.1.call-update) | async-done | bytes 1441808 | tf_op jit(solution)/shard_map/all_gather | solution.py:204
  1045.2 35.8 %all-gather.16.cloned.1.call-done = bf16[1024,704]{0,1:T(8,128)(2,1)} async-done(((bf16[128,704]{0,1:T(8,128)(2,1)}), bf16[1024,704]{0,1:T(8,128)(2,1)}) %all-gather.16.cloned.1.call-update) | async-done | bytes 1441808 | tf_op jit(solution)/shard_map/all_gather | solution.py:205
  1089.3 35.8 %all-gather.18.cloned.1.call-done = bf16[1024,704]{0,1:T(8,128)(2,1)} async-done(((bf16[128,704]{0,1:T(8,128)(2,1)}), bf16[1024,704]{0,1:T(8,128)(2,1)}) %all-gather.18.cloned.1.call-update) | async-done | bytes 1441808 | tf_op jit(solution)/shard_map/all_gather | solution.py:206
  1125.1 11.9 multiply_convert_fusion.2
  1148.4 149.7 %all-reduce.19.cloned.1.call-done = f32[2048,1024]{1,0:T(8,128)} async-done(((f32[2048,1024]{1,0:T(8,128)}), f32[2048,1024]{1,0:T(8,128)}) %all-reduce.19.cloned.1.call-update) | async-done | bytes 8388624 | tf_op jit(solution)/shard_map/psum | solution.py:299
  1333.2 444.0 %while.123 = (s32[]{:T(128)}, f32[2,128,128]{2,1,0:T(8,128)S(1)}, f32[32,2,64,128]{3,2,1,0:T(8,128)}, f32[32,2,64,128]{3,2,1,0:T(8,128)}, f32[32,2,64,128]{3,2,1...) while((s32[]{:T(128)}, f32[2,128,128]{2,1,0:T(8,128)S(1)}, ...), condition=%wide.region_20.21_spmd.clone.clone, body=%wide.region_19.20_spmd.clone.sunk.clone | while | flops 176414720 | bytes 2372807 | solution.py:116
  1778.1 40.3 %all-gather.26.cloned.1.call-done = f32[16,128,128]{2,1,0:T(8,128)} async-done(((f32[2,128,128]{2,1,0:T(8,128)}), f32[16,128,128]{2,1,0:T(8,128)}) %all-gather.26.cloned.1.call-update) | async-done | bytes 1048592 | tf_op jit(solution)/shard_map/all_gather | solution.py:22
  1835.3 439.5 %while.120 = (s32[]{:T(128)}, f32[2,128,128]{2,1,0:T(8,128)S(1)}, f32[32,2,64,128]{3,2,1,0:T(8,128)}, f32[32,2,64,128]{3,2,1,0:T(8,128)}, f32[32,2,64,128]{3,2,1...) while((s32[]{:T(128)}, f32[2,128,128]{2,1,0:T(8,128)S(1)}, ...), condition=%wide.region_24.25_spmd.clone.clone, body=%wide.region_23.24_spmd.clone.sunk.clone | while | flops 176316416 | bytes 2107065 | solution.py:116
  2406.6 10.8 multiply_reduce_fusion.9
  2519.3 19.8 all-reduce.11
  2541.3 123.8 %all-reduce.21.cloned.1.call-done = f32[2048,1024]{1,0:T(8,128)} async-done(((f32[2048,1024]{1,0:T(8,128)}), f32[2048,1024]{1,0:T(8,128)}) %all-reduce.21.cloned.1.call-update) | async-done | bytes 8388624 | tf_op jit(solution)/shard_map/psum | solution.py:347
  2665.1 12.6 multiply_reduce_fusion.1
  2677.7 40.0 %all-reduce.12 = (f32[1024]{0:T(1024)S(1)}, f32[3,4,1024]{2,1,0:T(4,128)S(1)}, f32[128]{0:T(128)}) all-reduce(f32[1024]{0:T(1024)S(1)} %get-tuple-element.1384, f32[3,4,1024]{2,1,0:T(4,128)S(1)} %constant_dynamic-update-slice_fusion.4, f32[128]{0:T(128)S(1)} %bitcast_reduce_fusion), channel_id=1, replica_groups=mesh['seq'=8,'head'=4] {'seq','head'}, use_global_device_ids=true, to_apply=%region_33.34 | all-reduce | flops 13440 | bytes 107520 | tf_op jit(solution)/shard_map/psum | solution.py:355
  2723.1 17.4 reduce-scatter.12.cloned.1.call-done
  2743.8 72.9 %reduce-scatter.22.cloned.1.call-done = f32[128,704]{0,1:T(8,128)} async-done(((f32[1024,704]{0,1:T(8,128)}), f32[128,704]{0,1:T(8,128)}) %reduce-scatter.22.cloned.1.call-update) | async-done | bytes 360464 | tf_op jit(solution)/shard_map/reduce_scatter | solution.py:372
  2816.8 75.5 %reduce-scatter.24.cloned.1.call-done = f32[128,704]{0,1:T(8,128)} async-done(((f32[1024,704]{0,1:T(8,128)}), f32[128,704]{0,1:T(8,128)}) %reduce-scatter.24.cloned.1.call-update) | async-done | bytes 360464 | tf_op jit(solution)/shard_map/reduce_scatter | solution.py:373
  2892.3 75.5 %reduce-scatter.26.cloned.1.call-done = f32[128,704]{0,1:T(8,128)} async-done(((f32[1024,704]{0,1:T(8,128)}), f32[128,704]{0,1:T(8,128)}) %reduce-scatter.26.cloned.1.call-update) | async-done | bytes 360464 | tf_op jit(solution)/shard_map/reduce_scatter | solution.py:374
  2967.8 66.4 %reduce-scatter.20.cloned.1.call-done = f32[128,256]{1,0:T(8,128)} async-done(((f32[1024,256]{1,0:T(8,128)}), f32[128,256]{1,0:T(8,128)}) %reduce-scatter.20.cloned.1.call-update) | async-done | bytes 131088 | tf_op jit(solution)/shard_map/reduce_scatter | solution.py:371
  3034.2 66.7 %reduce-scatter.14.cloned.1.call-done = f32[128,256]{1,0:T(8,128)} async-done(((f32[1024,256]{1,0:T(8,128)}), f32[128,256]{1,0:T(8,128)}) %reduce-scatter.14.cloned.1.call-update) | async-done | bytes 131088 | tf_op jit(solution)/shard_map/reduce_scatter | solution.py:367
  3100.9 66.2 %reduce-scatter.16.cloned.1.call-done = f32[128,256]{1,0:T(8,128)} async-done(((f32[1024,256]{1,0:T(8,128)}), f32[128,256]{1,0:T(8,128)}) %reduce-scatter.16.cloned.1.call-update) | async-done | bytes 131088 | tf_op jit(solution)/shard_map/reduce_scatter | solution.py:368
  3167.1 66.8 %reduce-scatter.18.cloned.1.call-done = f32[128,256]{1,0:T(8,128)} async-done(((f32[1024,256]{1,0:T(8,128)}), f32[128,256]{1,0:T(8,128)}) %reduce-scatter.18.cloned.1.call-update) | async-done | bytes 131088 | tf_op jit(solution)/shard_map/reduce_scatter | solution.py:369
  (1528 shorter events, 1839.7 us)
Async XLA Ops:
  7.2 64.9 %copy-start.101 = (bf16[128,256]{1,0:T(8,128)(2,1)S(1)}, bf16[128,256]{1,0:T(8,128)(2,1)}, u32[]{:S(2)}) copy-start(bf16[128,256]{1,0:T(8,128)(2,1)} %param.31) | copy-start | bytes 196612
  7.2 96.2 %copy-start.118 = (bf16[128]{0:T(256)(128)(2,1)S(1)}, bf16[128]{0:T(256)(128)(2,1)}, u32[]{:S(2)}) copy-start(bf16[128]{0:T(256)(128)(2,1)} %param.28) | copy-start | bytes 772
  7.2 406.0 %all-gather.20.cloned.1.call-start = ((), (), s32[]{:S(2)}) async-start(), calls=%async_computation.23 | async-start | bytes 1179648 | tf_op jit(solution)/shard_map/all_gather | solution.py:22
  131.7 23.8 collective-permute-start
  133.0 153.1 %copy-start.76 = (f32[128,128]{1,0:T(8,128)}, f32[128,128]{1,0:T(8,128)S(1)}, u32[]{:S(2)}) copy-start(f32[128,128]{1,0:T(8,128)S(1)} %fusion.261) | copy-start | bytes 196612
  155.2 96.7 %copy-start.77 = (pred[64,64]{0,1:T(8,128)(4,1)}, pred[64,64]{0,1:T(8,128)(4,1)S(1)}, u32[]{:S(2)}) copy-start(pred[64,64]{0,1:T(8,128)(4,1)S(1)} %get-tuple-element.1550) | copy-start | bytes 12292
  155.3 112.5 %copy-start.67 = (f32[64,64]{0,1:T(8,128)}, f32[64,64]{0,1:T(8,128)S(1)}, u32[]{:S(2)}) copy-start(f32[64,64]{0,1:T(8,128)S(1)} %fusion.264) | copy-start | bytes 49156
  155.5 123.1 %copy-start.65 = (f32[32,2,64]{2,1,0:T(2,128)}, f32[32,2,64]{2,1,0:T(2,128)S(1)}, u32[]{:S(2)}) copy-start(f32[32,2,64]{2,1,0:T(2,128)S(1)} %copy.352) | copy-start | bytes 49156
  207.9 44.0 %copy-start.3 = (f32[32,2,64,64]{2,3,1,0:T(8,128)}, f32[32,2,64,64]{2,3,1,0:T(8,128)S(1)}, u32[]{:S(2)}) copy-start(f32[32,2,64,64]{2,3,1,0:T(8,128)S(1)} %fusion.214) | copy-start | bytes 3145732
  290.9 81.0 %copy-start.125 = (bf16[128]{0:T(256)(128)(2,1)S(1)}, bf16[128]{0:T(256)(128)(2,1)}, u32[]{:S(2)}) copy-start(bf16[128]{0:T(256)(128)(2,1)} %param.34) | copy-start | bytes 772
  371.1 81.0 %all-gather.22.cloned.1.call-start = ((), (), s32[]{:S(2)}) async-start(), calls=%async_computation.24 | async-start | bytes 1179648 | tf_op jit(solution)/shard_map/all_gather | solution.py:22
  371.9 619.1 %all-reduce.17.cloned.1.call-start = ((), (), s32[]{:S(2)}) async-start(), calls=%async_computation.9 | async-start | bytes 16777216 | tf_op jit(solution)/shard_map/psum | solution.py:279
  830.2 206.7 %all-gather.14.cloned.1.call-start = ((), (), s32[]{:S(2)}) async-start(), calls=%async_computation.10 | async-start | bytes 1622016 | tf_op jit(solution)/shard_map/all_gather | solution.py:204
  830.8 250.2 %all-gather.16.cloned.1.call-start = ((), (), s32[]{:S(2)}) async-start(), calls=%async_computation.11 | async-start | bytes 1622016 | tf_op jit(solution)/shard_map/all_gather | solution.py:205
  831.4 293.7 %all-gather.18.cloned.1.call-start = ((), (), s32[]{:S(2)}) async-start(), calls=%async_computation.12 | async-start | bytes 1622016 | tf_op jit(solution)/shard_map/all_gather | solution.py:206
  832.0 466.1 %all-reduce.19.cloned.1.call-start = ((), (), s32[]{:S(2)}) async-start(), calls=%async_computation.14 | async-start | bytes 16777216 | tf_op jit(solution)/shard_map/psum | solution.py:299
  1146.6 631.5 %all-gather.24.cloned.1.call-start = ((), (), s32[]{:S(2)}) async-start(), calls=%async_computation.25 | async-start | bytes 1179648 | tf_op jit(solution)/shard_map/all_gather | solution.py:22
  1148.3 670.1 %all-gather.26.cloned.1.call-start = ((), (), s32[]{:S(2)}) async-start(), calls=%async_computation.26 | async-start | bytes 1179648 | tf_op jit(solution)/shard_map/all_gather | solution.py:22
  1333.2 444.8 %copy-start.80 = (f32[32,64,2]{1,0,2:T(8,128)S(1)}, f32[32,64,2]{1,0,2:T(8,128)}, u32[]{:S(2)}) copy-start(f32[32,64,2]{1,0,2:T(8,128)} %copy-done.79) | copy-start | bytes 49156
  1778.0 761.9 %reduce-scatter.28.cloned.1.call-start = ((), (), s32[]{:S(2)}) async-start(), calls=%async_computation.27 | async-start | bytes 589824
  2436.1 13.2 collective-permute-start.1
  2449.3 215.9 %all-reduce.21.cloned.1.call-start = ((), (), s32[]{:S(2)}) async-start(), calls=%async_computation.15 | async-start | bytes 16777216 | tf_op jit(solution)/shard_map/psum | solution.py:347
  2459.7 280.8 %reduce-scatter.12.cloned.1.call-start = ((), (), s32[]{:S(2)}) async-start(), calls=%async_computation.13 | async-start | bytes 10485760 | tf_op jit(solution)/shard_map/reduce_scatter | solution.py:287
  2468.6 348.2 %reduce-scatter.22.cloned.1.call-start = ((), (), s32[]{:S(2)}) async-start(), calls=%async_computation.20 | async-start | bytes 3244032 | tf_op jit(solution)/shard_map/reduce_scatter | solution.py:372
  2477.3 415.0 %reduce-scatter.24.cloned.1.call-start = ((), (), s32[]{:S(2)}) async-start(), calls=%async_computation.21 | async-start | bytes 3244032 | tf_op jit(solution)/shard_map/reduce_scatter | solution.py:373
  2486.0 481.8 %reduce-scatter.26.cloned.1.call-start = ((), (), s32[]{:S(2)}) async-start(), calls=%async_computation.22 | async-start | bytes 3244032 | tf_op jit(solution)/shard_map/reduce_scatter | solution.py:374
  2494.8 539.5 %reduce-scatter.20.cloned.1.call-start = ((), (), s32[]{:S(2)}) async-start(), calls=%async_computation.19 | async-start | bytes 1179648 | tf_op jit(solution)/shard_map/reduce_scatter | solution.py:371
  2501.7 599.2 %reduce-scatter.14.cloned.1.call-start = ((), (), s32[]{:S(2)}) async-start(), calls=%async_computation.16 | async-start | bytes 1179648 | tf_op jit(solution)/shard_map/reduce_scatter | solution.py:367
  2510.6 656.5 %reduce-scatter.16.cloned.1.call-start = ((), (), s32[]{:S(2)}) async-start(), calls=%async_computation.17 | async-start | bytes 1179648 | tf_op jit(solution)/shard_map/reduce_scatter | solution.py:368
  2511.2 28.4 copy-start.117
  2511.3 722.6 %reduce-scatter.18.cloned.1.call-start = ((), (), s32[]{:S(2)}) async-start(), calls=%async_computation.18 | async-start | bytes 1179648 | tf_op jit(solution)/shard_map/reduce_scatter | solution.py:369
  2541.3 177.6 %copy-start.98 = (f32[2048]{0:T(1024)S(1)}, f32[2048]{0:T(1024)}, u32[]{:S(2)}) copy-start(f32[2048]{0:T(1024)} %copy-done.97) | copy-start | bytes 24580
  (125 other events, 666.5 us)
Sparse Core Ops, SparseCore 0:
  371.2 38.6 all-gather.19
  412.6 39.4 all-gather.21
  830.3 160.5 all-reduce.16
  992.9 43.9 all-gather.13
  1038.8 42.1 all-gather.15
  1082.9 42.1 all-gather.17
  1146.7 151.2 all-reduce.18
  1300.7 40.2 all-gather.23
  1778.1 40.2 all-gather.25
  2449.4 61.2 reduce-scatter.27
  2513.3 151.8 all-reduce.20
  2667.7 72.6 reduce-scatter.11
  2744.6 72.1 reduce-scatter.21
  2820.8 71.4 reduce-scatter.23
  2896.3 71.4 reduce-scatter.25
  2971.6 62.5 reduce-scatter.19
  3038.4 62.4 reduce-scatter.13
  3104.7 62.3 reduce-scatter.15
  3171.5 62.3 reduce-scatter.17
where the time goes:
time: 3280 us; the launch traced here: 3240 us
  matrix products  1440 us (44%)
  waiting for transfers between devices  1100 us (34%)
  blocking collectives  255 us (8%)
  other arithmetic  215 us (7%)
  local copies, waits for them, and re-layouts  202 us (6%)
    dot_general x752, matrix products, precise_product(): return jnp.einsum(spec, left, right, precision=HIGHEST)  1330 us
    psum x1, waiting for transfers between devices, body(): lax.psum(cols_product(d_gate, full_gate) + cols_product(d_up, full_up), '...  150 us
    psum x1, waiting for transfers between devices, body(): branch = lax.psum(cols_product(head_rows, full_output), 'head')  132 us
    psum x1, waiting for transfers between devices, body(): d_first = lax.psum(d_first_part, 'head')  124 us
    all_gather x4, waiting for transfers between devices, entering(): gathered = jax.tree.map(lambda a: lax.all_gather(a, axis), part)  79.3 us
    reduce_scatter x1, waiting for transfers between devices, body(): lax.psum_scatter(up_grad, 'seq', scatter_dimension=0, tiled=True)  75.5 us
    reduce_scatter x1, waiting for transfers between devices, body(): lax.psum_scatter(down_grad, 'seq', scatter_dimension=0, tiled=True)  75.5 us
    reduce_scatter x1, waiting for transfers between devices, body(): lax.psum_scatter(gate_grad, 'seq', scatter_dimension=0, tiled=True)  72.9 us
  transfers between devices with their start and end apart: 21, of which 16 were waited for; matrix products, arithmetic and copies ran while one was open for 19% of the time, Pallas kernels for 0%

commit v1 on v0

v1 whole, which is shorter than its diff:
```python
import functools

import jax
import jax.numpy as jnp
from jax import lax
from jax.experimental import pallas as pl
from jax.experimental.pallas import tpu as pltpu
from jax.sharding import PartitionSpec as P

GROUP = 64
CHUNK = 128
MESH = pl.DeviceIdType.MESH
BF = jnp.bfloat16
F32 = jnp.float32
VMEM_LIMIT = 56 << 20


def nn(left, right):
    return jnp.dot(left.astype(BF), right.astype(BF), preferred_element_type=F32)


def tn(left, right):
    return lax.dot_general(
        left.astype(BF), right.astype(BF), (((0,), (0,)), ((), ())), preferred_element_type=F32
    )


def nt(left, right):
    return lax.dot_general(
        left.astype(BF), right.astype(BF), (((1,), (1,)), ((), ())), preferred_element_type=F32
    )


def sigmoid(v):
    return 0.5 * jnp.tanh(0.5 * v) + 0.5


def side(left, right):
    return jnp.concatenate([left, right], 1)


def stack(top, bottom):
    return jnp.concatenate([top, bottom], 0)


def grid_indices():
    rows = lax.broadcasted_iota(jnp.int32, (CHUNK, CHUNK), 0)
    cols = lax.broadcasted_iota(jnp.int32, (CHUNK, CHUNK), 1)
    return rows, cols


def load_padded(pad_ref, pre_ref, halo_ref, chunk, resets_ref):
    start = pl.multiple_of(chunk * CHUNK, CHUNK)
    before = pl.multiple_of(jnp.maximum(start - 16, 0), 16)
    own = pre_ref[pl.ds(start, CHUNK), :].astype(F32)
    earlier = pre_ref[pl.ds(before, 16), :].astype(F32)[8:]
    halo = halo_ref[...].astype(F32)[8:]
    first = jnp.where(chunk == 0, halo, earlier)
    keep0 = 1.0 - resets_ref[2 * chunk]
    keep1 = 1.0 - resets_ref[2 * chunk + 1]
    pad_ref[0:8] = first * keep0
    pad_ref[8:72] = own[:GROUP]
    pad_ref[72:80] = own[GROUP - 8 : GROUP] * keep1
    pad_ref[80:144] = own[GROUP:]


def tap_rows(pad_ref, tap):
    return stack(pad_ref[5 + tap : 69 + tap], pad_ref[77 + tap : 141 + tap])


def convolve(pad_ref, taps_ref):
    mixed = None
    for tap in range(4):
        term = taps_ref[tap : tap + 1] * tap_rows(pad_ref, tap)
        mixed = term if mixed is None else mixed + term
    return mixed


def inverse_levels(strict, rows, cols, keep1):
    eye = jnp.where(rows == cols, 1.0, 0.0)
    pair = (rows // 2) == (cols // 2)
    results = [eye - jnp.where(pair, a, 0.0) for a in strict]
    width = 2
    while width < CHUNK:
        off = ((rows // (2 * width)) == (cols // (2 * width))) & ((rows // width) != (cols // width))
        lows = [r.astype(BF) for r in results]
        parts = [jnp.where(off, a, 0.0).astype(BF) for a in strict]
        if width == GROUP:
            parts = [jnp.where(off, a * k, 0.0).astype(BF) for a, k in zip(strict, keep1)]
        steps = [nn(r, p) for r, p in zip(lows, parts)]
        results = [r - nn(s, low) for r, s, low in zip(results, steps, lows)]
        width *= 2
    return results


def mixer_forward_kernel(
    heads,
    resets_ref,
    pre_ref,
    halo_ref,
    taps_ref,
    logits_ref,
    qkv_ref,
    inv_ref,
    wu_ref,
    mq_ref,
    start_ref,
    out0_ref,
    total_ref,
    pad_ref,
):
    columns = heads * CHUNK
    rows, cols = grid_indices()
    eye = jnp.where(rows == cols, 1.0, 0.0)
    top = lax.broadcasted_iota(jnp.int32, (CHUNK, 1), 0) < GROUP
    for head in range(heads):
        total_ref[head] = side(eye, jnp.zeros_like(eye))
    batch = pad_ref.shape[0]

    def one(step, carry):
        units = []
        for lane in range(batch):
            chunk = step * batch + lane
            pad = pad_ref.at[lane]
            load_padded(pad, pre_ref, halo_ref, chunk, resets_ref)
            mixed = convolve(pad, taps_ref)
            silued = mixed * sigmoid(mixed)
            keep0 = 1.0 - resets_ref[2 * chunk]
            keep1 = 1.0 - resets_ref[2 * chunk + 1]
            both = keep0 * keep1
            enter = jnp.where(top, keep0, both)
            leave = jnp.where(top, keep1, 1.0)
            at = pl.ds(pl.multiple_of(chunk * CHUNK, CHUNK), CHUNK)
            beta_rows = sigmoid(logits_ref[at, :])
            for head in range(heads):
                window = slice(head * CHUNK, (head + 1) * CHUNK)
                parts = []
                for kind in range(3):
                    part = silued[:, kind * columns + head * CHUNK : kind * columns + (head + 1) * CHUNK]
                    if kind < 2:
                        part = part * lax.rsqrt(jnp.sum(part * part, axis=-1, keepdims=True) + 1e-06)
                    part = part.astype(BF)
                    qkv_ref[at, kind * columns + head * CHUNK : kind * columns + (head + 1) * CHUNK] = part
                    parts.append(part)
                units.append((chunk, head, *parts, beta_rows[:, head : head + 1], keep1, both, enter, leave))
        turned = [u[3].T for u in units]
        strict = [
            jnp.where(rows > cols, u[5] * nn(u[3], t), 0.0) for u, t in zip(units, turned)
        ]
        inverses = [r.astype(BF) for r in inverse_levels(strict, rows, cols, [u[6] for u in units])]
        factors = []
        for u, inverse in zip(units, inverses):
            beta = u[5]
            factors.append(nn(inverse, side(u[3].astype(F32) * beta, u[4].astype(F32) * beta)))
        for u, inverse, factor, t in zip(units, inverses, factors, turned):
            chunk, head, query, key, value, beta, keep1, both, enter, leave = u
            weight, update = factor[:, :CHUNK], factor[:, CHUNK:]
            entering_weight = weight * enter
            inv_ref[chunk, head] = inverse
            wu_ref[chunk, head] = side(entering_weight, update).astype(BF)
            gathered = nn(t, side(weight, update * leave))
            device_map = (both * (eye - gathered[:, :CHUNK])).astype(BF)
            shift = gathered[:, CHUNK:]
            scores = jnp.where(rows >= cols, nn(query, t), 0.0)
            scores = jnp.where((rows >= GROUP) & (cols < GROUP), scores * keep1, scores)
            seen = nn(scores, side(entering_weight, update))
            effective = query.astype(F32) * enter - seen[:, :CHUNK]
            mq_ref[chunk, head] = stack(device_map, effective.astype(BF))
            out0_ref[chunk, head] = seen[:, CHUNK:]
            running = total_ref[head]
            start_ref[chunk, head] = running.astype(BF)
            total_ref[head] = nn(device_map, running) + side(jnp.zeros_like(shift), shift)
        return carry

    lax.fori_loop(0, resets_ref.shape[0] // 2 // batch, one, 0)


def mixer_forward(resets, pre, halo, taps, logits, heads):
    tokens = pre.shape[0]
    chunks = tokens // CHUNK
    columns = heads * CHUNK

    def units(width, kind):
        return jax.ShapeDtypeStruct((chunks, heads, *width), kind)

    return pl.pallas_call(
        functools.partial(mixer_forward_kernel, heads),
        name="mixer_forward",
        out_shape=(
            jax.ShapeDtypeStruct((tokens, 3 * columns), BF),
            units((CHUNK, CHUNK), BF),
            units((CHUNK, 2 * CHUNK), BF),
            units((2 * CHUNK, CHUNK), BF),
            units((CHUNK, 2 * CHUNK), BF),
            units((CHUNK, CHUNK), F32),
            jax.ShapeDtypeStruct((heads, CHUNK, 2 * CHUNK), F32),
        ),
        in_specs=[pl.BlockSpec(memory_space=pltpu.SMEM)] + [pl.BlockSpec(memory_space=pltpu.VMEM)] * 4,
        out_specs=tuple([pl.BlockSpec(memory_space=pltpu.VMEM)] * 7),
        scratch_shapes=[pltpu.VMEM((2, 144, 3 * columns), F32)],
        compiler_params=pltpu.CompilerParams(vmem_limit_bytes=VMEM_LIMIT),
        cost_estimate=pl.CostEstimate(flops=3 * 10**9, bytes_accessed=20 << 20, transcendentals=2 << 20),
    )(resets, pre, halo, taps, logits)


def exchange_kernel(axis, count, window, backward, part_ref, state_ref, slots_ref, send_sem, recv_sem):
    place = lax.axis_index(axis)
    ahead = count - 1 - place if backward else place
    behind = count - 1 - ahead
    sign = -1 if backward else 1
    barrier = pltpu.get_barrier_semaphore()
    for hop in range(1, window + 1):

        @pl.when(ahead >= hop)
        def _():
            pl.semaphore_signal(
                barrier, inc=1, device_id={axis: place - sign * hop}, device_id_type=MESH
            )

    @pl.when(behind > 0)
    def _():
        pl.semaphore_wait(barrier, jnp.minimum(behind, window))

    def copy(hop):
        return pltpu.make_async_remote_copy(
            src_ref=part_ref,
            dst_ref=slots_ref.at[hop - 1],
            send_sem=send_sem.at[hop - 1],
            recv_sem=recv_sem.at[hop - 1],
            device_id={axis: place + sign * hop},
            device_id_type=MESH,
        )

    for hop in range(1, window + 1):

        @pl.when(behind >= hop)
        def _():
            copy(hop).start()

    heads = state_ref.shape[0]
    state_ref[...] = jnp.zeros_like(state_ref)
    for hop in range(window, 0, -1):

        @pl.when(ahead >= hop)
        def _():
            copy(hop).wait_recv()
            for head in range(heads):
                part = slots_ref[hop - 1, head]
                state_ref[head] = nn(part[:, :CHUNK], state_ref[head]) + part[:, CHUNK:].astype(F32)

    for hop in range(1, window + 1):

        @pl.when(behind >= hop)
        def _():
            copy(hop).wait_send()


def exchange(part, axis, backward, collective):
    count = lax.axis_size(axis)
    window = min(count - 1, count // 2)
    heads = part.shape[0]
    return pl.pallas_call(
        functools.partial(exchange_kernel, axis, count, window, backward),
        name="state_backward" if backward else "state_forward",
        out_shape=jax.ShapeDtypeStruct((heads, CHUNK, CHUNK), F32),
        in_specs=[pl.BlockSpec(memory_space=pltpu.VMEM)],
        out_specs=pl.BlockSpec(memory_space=pltpu.VMEM),
        scratch_shapes=[
            pltpu.VMEM((window, heads, CHUNK, 2 * CHUNK), BF),
            pltpu.SemaphoreType.DMA((window,)),
            pltpu.SemaphoreType.DMA((window,)),
        ],
        compiler_params=pltpu.CompilerParams(
            collective_id=collective, has_side_effects=True, vmem_limit_bytes=VMEM_LIMIT
        ),
    )(part)


def mixer_output_kernel(heads, state_ref, start_ref, mq_ref, out0_ref, gain_ref, delta_ref, rows_ref, states_ref):
    batch = 4

    def one(step, carry):
        for lane in range(batch):
            chunk = step * batch + lane
            at = pl.ds(pl.multiple_of(chunk * CHUNK, CHUNK), CHUNK)
            for head in range(heads):
                window = slice(head * CHUNK, (head + 1) * CHUNK)
                begin = start_ref[chunk, head]
                state = nn(begin[:, :CHUNK], state_ref[head]) + begin[:, CHUNK:].astype(F32)
                state = state.astype(BF)
                states_ref[chunk, head] = state
                out = out0_ref[chunk, head] + nn(mq_ref[chunk, head, CHUNK:], state)
                delta_ref[at, window] = out
                scale = lax.rsqrt(jnp.mean(out * out, axis=-1, keepdims=True) + 1e-05)
                rows_ref[at, window] = (out * scale * gain_ref[...]).astype(BF)
        return carry

    lax.fori_loop(0, start_ref.shape[0] // batch, one, 0)


def mixer_output(state, start, mq, out0, gain):
    chunks, heads = start.shape[:2]
    tokens = chunks * CHUNK
    return pl.pallas_call(
        functools.partial(mixer_output_kernel, heads),
        name="mixer_output",
        out_shape=(
            jax.ShapeDtypeStruct((tokens, heads * CHUNK), F32),
            jax.ShapeDtypeStruct((tokens, heads * CHUNK), BF),
            jax.ShapeDtypeStruct((chunks, heads, CHUNK, CHUNK), BF),
        ),
        compiler_params=pltpu.CompilerParams(vmem_limit_bytes=VMEM_LIMIT),
        cost_estimate=pl.CostEstimate(flops=3 * 10**8, bytes_accessed=10 << 20, transcendentals=1 << 14),
    )(state, start, mq, out0, gain)


def mixer_back_state_kernel(heads, dheads_ref, delta_ref, gain_ref, mq_ref, ddelta_ref, gain_grad_ref, shift_ref):
    chunks = mq_ref.shape[0]
    shift_ref[...] = jnp.zeros_like(shift_ref)
    gain_grad_ref[...] = jnp.zeros_like(gain_grad_ref)

    def one(step, carry):
        chunk = chunks - 1 - step
        at = pl.ds(pl.multiple_of(chunk * CHUNK, CHUNK), CHUNK)
        for head in range(heads):
            window = slice(head * CHUNK, (head + 1) * CHUNK)
            out = delta_ref[at, window]
            grad = dheads_ref[at, window].astype(F32)
            scale = lax.rsqrt(jnp.mean(out * out, axis=-1, keepdims=True) + 1e-05)
            unit = out * scale
            gain_grad_ref[...] += jnp.sum((grad * unit).reshape(CHUNK // 8, 8, CHUNK), 0)
            scaled = grad * gain_ref[...]
            back = scale * (scaled - unit * jnp.mean(scaled * unit, axis=-1, keepdims=True))
            back = back.astype(BF)
            ddelta_ref[at, window] = back
            shift_ref[head] = tn(mq_ref[chunk, head], stack(shift_ref[head].astype(BF), back))
        return carry

    lax.fori_loop(0, chunks, one, 0)


def mixer_back_state(dheads, delta, gain, mq):
    chunks, heads = mq.shape[:2]
    tokens = chunks * CHUNK
    return pl.pallas_call(
        functools.partial(mixer_back_state_kernel, heads),
        name="mixer_back_state",
        out_shape=(
            jax.ShapeDtypeStruct((tokens, heads * CHUNK), BF),
            jax.ShapeDtypeStruct((8, CHUNK), F32),
            jax.ShapeDtypeStruct((heads, CHUNK, CHUNK), F32),
        ),
        compiler_params=pltpu.CompilerParams(vmem_limit_bytes=VMEM_LIMIT),
        cost_estimate=pl.CostEstimate(flops=3 * 10**8, bytes_accessed=10 << 20, transcendentals=1 << 14),
    )(dheads, delta, gain, mq)


def mixer_backward_kernel(
    heads,
    resets_ref,
    pre_ref,
    halo_ref,
    taps_ref,
    logits_ref,
    qkv_ref,
    inv_ref,
    wu_ref,
    mq_ref,
    states_ref,
    ddelta_ref,
    arrive_ref,
    dpre_ref,
    tail_ref,
    lead_ref,
    taps_grad_ref,
    dlogits_ref,
    carry_ref,
    pad_ref,
    dpad_ref,
):
    columns = heads * CHUNK
    chunks = mq_ref.shape[0]
    rows, cols = grid_indices()
    top = lax.broadcasted_iota(jnp.int32, (CHUNK, 1), 0) < GROUP
    carry_ref[...] = arrive_ref[...]
    taps_grad_ref[...] = jnp.zeros_like(taps_grad_ref)
    dpad_ref[136:144] = jnp.zeros_like(dpad_ref[136:144])

    def one(step, carry):
        chunk = chunks - 1 - step
        at = pl.ds(pl.multiple_of(chunk * CHUNK, CHUNK), CHUNK)
        keep0 = 1.0 - resets_ref[2 * chunk]
        keep1 = 1.0 - resets_ref[2 * chunk + 1]
        both = keep0 * keep1
        enter = jnp.where(top, keep0, both)
        leave = jnp.where(top, keep1, 1.0)
        load_padded(pad_ref, pre_ref, halo_ref, chunk, resets_ref)
        mixed = convolve(pad_ref, taps_ref)
        gate = sigmoid(mixed)
        slope = gate * (1.0 + mixed * (1.0 - gate))
        silued = mixed * gate
        beta_rows = sigmoid(logits_ref[at, :])
        grads = [[None] * heads for _ in range(3)]
        dlogits = []
        for head in range(heads):
            def part(kind):
                return slice(kind * columns + head * CHUNK, kind * columns + (head + 1) * CHUNK)

            query, key, value = (qkv_ref[at, part(kind)] for kind in range(3))
            beta = beta_rows[:, head : head + 1]
            inverse = inv_ref[chunk, head]
            factors = wu_ref[chunk, head]
            weight, update = factors[:, :CHUNK], factors[:, CHUNK:]
            state = states_ref[chunk, head]
            out_grad = ddelta_ref[at, head * CHUNK : (head + 1) * CHUNK]
            later = carry_ref[head].astype(BF)
            carry_ref[head] = tn(mq_ref[chunk, head], stack(later, out_grad))
            cross = (rows >= GROUP) & (cols < GROUP)
            scores = jnp.where(rows >= cols, nt(query, key), 0.0)
            scores = jnp.where(cross, scores * keep1, scores).astype(BF)
            fresh = (update.astype(F32) - nn(weight, state)).astype(BF)
            fresh_grad = tn(scores, out_grad) + leave * nn(key, later)
            fresh_low = fresh_grad.astype(BF)
            score_grad = jnp.where(rows >= cols, nt(out_grad, fresh), 0.0)
            score_grad = jnp.where(cross, score_grad * keep1, score_grad).astype(BF)
            through = nt(stack(out_grad, fresh_low), state)
            query_grad = enter * through[:CHUNK] + nn(score_grad, key)
            weight_grad = -enter * through[CHUNK:]
            key_grad = tn(score_grad, query) + leave * nt(fresh, later)
            back = tn(inverse, side(weight_grad.astype(BF), fresh_low))
            back_low = back.astype(BF)
            strict = -jnp.where(rows > cols, nt(back_low, side(weight, update)), 0.0)
            strict = jnp.where(cross, strict * keep1, strict).astype(BF)
            yk, zv = back[:, :CHUNK], back[:, CHUNK:]
            key32 = key.astype(F32)
            strict_key = nn(strict, key)
            key_grad = key_grad + beta * (yk + strict_key) + tn(strict, (beta * key32).astype(BF))
            value_grad = beta * zv
            beta_grad = jnp.sum((yk + strict_key) * key32 + zv * value.astype(F32), axis=-1, keepdims=True)
            dlogits.append(beta_grad * beta * (1.0 - beta))
            for kind, grad in ((0, query_grad), (1, key_grad)):
                raw = silued[:, part(kind)]
                inv = lax.rsqrt(jnp.sum(raw * raw, axis=-1, keepdims=True) + 1e-06)
                unit = raw * inv
                grads[kind][head] = (grad - unit * jnp.sum(unit * grad, axis=-1, keepdims=True)) * inv
            grads[2][head] = value_grad
        dlogits_ref[at, :] = jnp.concatenate(dlogits, 1)
        dmixed = jnp.concatenate([g for kind in grads for g in kind], 1) * slope
        dpad_ref[0:GROUP] = dmixed[:GROUP]
        dpad_ref[GROUP : GROUP + 8] = dmixed[GROUP : GROUP + 8] * keep1
        dpad_ref[72 : 72 + GROUP] = dmixed[GROUP:]
        dpre = None
        for tap in range(4):
            back = 3 - tap
            shifted = stack(dpad_ref[back : back + GROUP], dpad_ref[72 + back : 72 + back + GROUP])
            term = taps_ref[tap : tap + 1] * shifted
            dpre = term if dpre is None else dpre + term
            seen = (dmixed * tap_rows(pad_ref, tap)).reshape(CHUNK // 8, 8, 3 * columns)
            taps_grad_ref[tap] += jnp.sum(seen, 0)
        dpre_ref[at, :] = dpre.astype(BF)

        @pl.when(step == 0)
        def _():
            tail_ref[...] = dpre[CHUNK - 8 :]

        dpad_ref[136:144] = dmixed[:8] * keep0
        return carry

    lax.fori_loop(0, chunks, one, 0)
    index = lax.broadcasted_iota(jnp.int32, (8, 1), 0)
    lead = jnp.zeros((8, 3 * columns), F32)
    dpad_ref[0:128] = jnp.zeros_like(dpad_ref[0:128])
    dpad_ref[8:16] = dpad_ref[136:144]
    for tap in range(3):
        back = 3 - tap
        lead = lead + taps_ref[tap : tap + 1] * dpad_ref[back : back + 8]
    lead_ref[...] = lead


def mixer_backward(resets, pre, halo, taps, logits, qkv, inv, wu, mq, states, ddelta, arrive):
    chunks, heads = mq.shape[:2]
    tokens = chunks * CHUNK
    columns = heads * CHUNK
    return pl.pallas_call(
        functools.partial(mixer_backward_kernel, heads),
        name="mixer_backward",
        out_shape=(
            jax.ShapeDtypeStruct((tokens, 3 * columns), BF),
            jax.ShapeDtypeStruct((8, 3 * columns), F32),
            jax.ShapeDtypeStruct((8, 3 * columns), F32),
            jax.ShapeDtypeStruct((4, 8, 3 * columns), F32),
            jax.ShapeDtypeStruct((tokens, heads), F32),
        ),
        in_specs=[pl.BlockSpec(memory_space=pltpu.SMEM)] + [pl.BlockSpec(memory_space=pltpu.VMEM)] * 11,
        out_specs=tuple([pl.BlockSpec(memory_space=pltpu.VMEM)] * 5),
        scratch_shapes=[
            pltpu.VMEM((heads, CHUNK, CHUNK), F32),
            pltpu.VMEM((144, 3 * columns), F32),
            pltpu.VMEM((144, 3 * columns), F32),
        ],
        compiler_params=pltpu.CompilerParams(vmem_limit_bytes=VMEM_LIMIT),
        cost_estimate=pl.CostEstimate(flops=3 * 10**9, bytes_accessed=20 << 20, transcendentals=2 << 20),
    )(resets, pre, halo, taps, logits, qkv, inv, wu, mq, states, ddelta, arrive)


def from_behind(block, axis, distance):
    devices = range(lax.axis_size(axis))
    route = [(i - distance, i) for i in devices if i - distance in devices]
    return lax.ppermute(block, axis, route)


def dot(left, right):
    return jnp.dot(left, right, preferred_element_type=F32)


def dot_rows(left, right):
    return lax.dot_general(left, right, (((0,), (0,)), ((), ())), preferred_element_type=F32)


def dot_cols(left, right):
    return lax.dot_general(left, right, (((1,), (1,)), ((), ())), preferred_element_type=F32)


def gather_seq(block):
    return lax.all_gather(block, "seq", axis=0, tiled=True)


def body(
    block_input,
    first_gain,
    query_weight,
    key_weight,
    value_weight,
    beta_weight,
    conv_weight,
    head_gain,
    output_weight,
    second_gain,
    gate_weight,
    up_weight,
    down_weight,
    lengths,
    cotangent,
):
    tokens, width = block_input.shape
    heads = beta_weight.shape[1]
    columns = query_weight.shape[1]
    hidden_columns = gate_weight.shape[1]
    members = lax.axis_size("seq")
    piece = width // members
    column_start = lax.axis_index("head") * columns
    seq_place = lax.axis_index("seq")

    mixer_pack = gather_seq(
        jnp.concatenate(
            [query_weight, key_weight, value_weight, beta_weight, first_gain[:, None], second_gain[:, None]], 1
        )
    )
    projection = mixer_pack[:, : 3 * columns]
    full_beta = mixer_pack[:, 3 * columns : 3 * columns + heads]
    gain_one = mixer_pack[:, 3 * columns + heads].astype(F32)
    gain_two = mixer_pack[:, 3 * columns + heads + 1].astype(F32)
    full_output = gather_seq(output_weight)
    forward_pack = lax.all_gather(jnp.stack([gate_weight, up_weight, down_weight]), "seq", axis=0)
    full_gate, full_up, full_down = (forward_pack[:, i].reshape(width, hidden_columns) for i in range(3))

    ends = jnp.sum(jnp.where(jnp.arange(4)[:, None] >= jnp.arange(4)[None, :], lengths[None, :], 0), axis=1)
    starts = ends - lengths
    block_starts = seq_place * tokens + GROUP * jnp.arange(tokens // GROUP, dtype=jnp.int32)
    resets = jnp.any(starts[None, :] == block_starts[:, None], axis=1).astype(F32)

    inputs = block_input.astype(F32)
    halo_rows = from_behind(block_input[tokens - 16 :], "seq", 1)
    scale_one = lax.rsqrt(jnp.mean(inputs * inputs, axis=-1, keepdims=True) + 1e-06)
    first_rows = (inputs * scale_one * gain_one).astype(BF)
    halo_in = halo_rows.astype(F32)
    halo_first = (
        halo_in * lax.rsqrt(jnp.mean(halo_in * halo_in, axis=-1, keepdims=True) + 1e-06) * gain_one
    ).astype(BF)
    pre = dot(first_rows, projection).astype(BF)
    halo = dot(halo_first, projection).astype(BF)
    logits = dot(first_rows, full_beta)
    taps = conv_weight.astype(F32).transpose(1, 0, 2).reshape(4, -1)
    qkv, inv, wu, mq, start, out0, total = mixer_forward(resets, pre, halo, taps, logits, heads)
    total_low = total.astype(BF)
    state = exchange(total_low, "seq", False, 0)
    gain_head = head_gain.astype(F32)[None, :]
    delta, head_rows, states = mixer_output(state, start, mq, out0, gain_head)

    branch = lax.psum(dot_cols(head_rows, full_output).astype(BF), "head").astype(F32)
    middle = inputs + branch
    scale_two = lax.rsqrt(jnp.mean(middle * middle, axis=-1, keepdims=True) + 1e-06)
    unit_two = middle * scale_two
    second_rows = (unit_two * gain_two).astype(BF)
    gate = dot(second_rows, full_gate)
    up = dot(second_rows, full_up)
    sig = jax.nn.sigmoid(gate)
    hidden = (gate * sig * up).astype(BF)
    update = lax.psum_scatter(
        dot_cols(hidden, full_down).astype(BF), "head", scatter_dimension=1, tiled=True
    )
    middle_shard = lax.dynamic_slice_in_dim(middle, column_start, columns, 1)
    block_output = (middle_shard + update.astype(F32)).astype(BF)
    down_grad = dot_rows(cotangent, hidden)
    d_hidden = dot(cotangent, full_down)
    d_gate = (d_hidden * up * sig * (1.0 + gate * (1.0 - sig))).astype(BF)
    d_up = (d_hidden * gate * sig).astype(BF)
    gate_grad = dot_rows(second_rows, d_gate)
    up_grad = dot_rows(second_rows, d_up)
    forward_grads = jnp.stack(
        [g.astype(BF).reshape(members, piece, hidden_columns) for g in (gate_grad, up_grad, down_grad)], 1
    )
    forward_sum = lax.psum_scatter(forward_grads, "seq", scatter_dimension=0, tiled=False).astype(F32)
    d_second = lax.psum((dot_cols(d_gate, full_gate) + dot_cols(d_up, full_up)).astype(BF), "head").astype(F32)
    second_part = jnp.sum(d_second * unit_two, 0)
    scaled_two = gain_two * d_second
    d_middle = cotangent.astype(F32) + scale_two * (
        scaled_two - unit_two * jnp.mean(scaled_two * unit_two, axis=-1, keepdims=True)
    )
    d_branch = d_middle.astype(BF)
    output_grad = dot_rows(d_branch, head_rows)
    d_heads = dot(d_branch, full_output).astype(BF)
    ddelta, gain_part, shift = mixer_back_state(d_heads, delta, gain_head, mq)
    back_part = jnp.concatenate([total_low[:, :, :CHUNK].transpose(0, 2, 1), shift.astype(BF)], 2)
    arrive = exchange(back_part, "seq", True, 1)
    d_pre_own, tail, lead, taps_part, d_logits32 = mixer_backward(
        resets, pre, halo, taps, logits, qkv, inv, wu, mq, states, ddelta, arrive
    )
    received = from_behind(lead, "seq", -1)
    d_pre = lax.dynamic_update_slice_in_dim(d_pre_own, (tail + received).astype(BF), tokens - 8, 0)
    d_logits = d_logits32.astype(BF)
    mixer_grads = jnp.concatenate([dot_rows(first_rows, d_pre), dot_rows(d_branch, head_rows)], 1).astype(BF)
    mixer_sum = lax.psum_scatter(mixer_grads, "seq", scatter_dimension=0, tiled=True).astype(F32)
    beta_part = dot_rows(first_rows, d_logits)
    d_first_part = dot_cols(d_pre, projection) + dot_cols(d_logits, full_beta)
    d_first = lax.psum(d_first_part.astype(BF), "head").astype(F32)
    unit_one = inputs * scale_one
    first_part = jnp.sum(d_first * unit_one, 0)
    scaled_one = gain_one * d_first
    d_input = d_middle + scale_one * (
        scaled_one - unit_one * jnp.mean(scaled_one * unit_one, axis=-1, keepdims=True)
    )
    input_gradient = lax.dynamic_slice_in_dim(d_input, column_start, columns, 1)

    seq_small = jnp.concatenate(
        [
            jnp.sum(taps_part, 1).reshape(-1),
            beta_part.reshape(-1),
            first_part,
            second_part,
        ]
    )
    gain_sum = lax.psum(jnp.sum(gain_part, 0), ("seq", "head"))
    small = lax.psum(seq_small, "seq")
    edge = 12 * columns
    conv_gradient = small[:edge].reshape(4, 3, columns).transpose(1, 0, 2)
    row_start = seq_place * piece
    beta_all = small[edge : edge + width * heads].reshape(width, heads)
    beta_gradient = lax.dynamic_slice_in_dim(beta_all, row_start, piece, 0)
    edge += width * heads
    first_gradient = lax.dynamic_slice_in_dim(small, edge + row_start, piece, 0)
    second_gradient = lax.dynamic_slice_in_dim(small, edge + width + row_start, piece, 0)
    return (
        block_output,
        input_gradient,
        first_gradient,
        mixer_sum[:, :columns],
        mixer_sum[:, columns : 2 * columns],
        mixer_sum[:, 2 * columns : 3 * columns],
        beta_gradient,
        conv_gradient,
        gain_sum,
        mixer_sum[:, 3 * columns :],
        second_gradient,
        forward_sum[0],
        forward_sum[1],
        forward_sum[2],
    )


def solution(mesh):
    return jax.shard_map(
        body,
        mesh=mesh,
        in_specs=(
            P("seq", None),
            P("seq"),
            P("seq", "head"),
            P("seq", "head"),
            P("seq", "head"),
            P("seq", "head"),
            P(None, None, "head"),
            P(),
            P("seq", "head"),
            P("seq"),
            P("seq", "head"),
            P("seq", "head"),
            P("seq", "head"),
            P(),
            P("seq", None),
        ),
        out_specs=(
            P("seq", "head"),
            P("seq", "head"),
            P("seq"),
            P("seq", "head"),
            P("seq", "head"),
            P("seq", "head"),
            P("seq", "head"),
            P(None, None, "head"),
            P(),
            P("seq", "head"),
            P("seq"),
            P("seq", "head"),
            P("seq", "head"),
            P("seq", "head"),
        ),
        check_vma=False,
    )
```

time: 3280 us -> 839 us (0.26)
  matrix products: 1440 us -> 84.1 us
  waiting for transfers between devices: 1100 us -> 404 us
  local copies, waits for them, and re-layouts: 202 us -> 36.9 us
  other arithmetic: 215 us -> 53.9 us
  blocking collectives: 255 us -> 108 us
  Pallas kernels: 0 us -> 121 us
    dot_general x771 -> x19, matrix products: 1440 us -> 84.1 us  [the longest x6 30.2 us: dot_cols(): lax.dot_general(left, right, (((1,), (1,)), ((), ())), preferred_element_...]
    reduce_scatter x8 -> x2, waiting for transfers between devices: 507 us -> 132 us  [the longest x1 90.4 us: body(): lax.psum_scatter(forward_grads, 'seq', scatter_dimension=0, tiled=False)]
    psum x3, waiting for transfers between devices: 405 us -> 177 us  [the longest x1 93.5 us: body(): lax.psum(dot_cols(head_rows, full_output).astype(BF), 'head').astype(F32)]
    all_gather x7 -> x1, blocking collectives: 195 us -> 32.7 us  [gather_seq(): return lax.all_gather(block, 'seq', axis=0, tiled=True)]
    pallas_call x0 -> x6, Pallas kernels: none -> 121 us  [the longest x1 39.1 us: mixer_backward(): pl.pallas_call(functools.partial(mixer_backward_kernel, heads), name='mix...]
    all_gather x7 -> x2, waiting for transfers between devices: 185 us -> 75.6 us  [the longest x1 68.6 us: body(): lax.all_gather(jnp.stack([gate_weight, up_weight, down_weight]), 'seq', a...]
    dynamic_update_slice x64 -> x1, other arithmetic: 60.6 us -> 0.01 us  [body(): lax.dynamic_update_slice_in_dim(d_pre_own, (tail + received).astype(BF),...]
    dynamic_slice x66 -> x2, local copies, waits for them, and re-layouts: 38.9 us -> 0.6 us  [the longest x1 0.59 us: body(): lax.dynamic_slice_in_dim(small, edge + width + row_start, piece, 0)]
  transfers between devices with their start and end apart: 21 -> 10, of which waited for: 16 -> 8; matrix products, arithmetic and copies ran while one was open for 19% -> 10% of each run, Pallas kernels for 0% -> 0%
where the time goes in v1:
time: 839 us; the launch traced here: 830 us
  waiting for transfers between devices  404 us (48%)
  Pallas kernels  121 us (14%)
  blocking collectives  108 us (13%)
  matrix products  84.1 us (10%)
  other arithmetic  53.9 us (6%)
  local copies, waits for them, and re-layouts  36.9 us (4%)
  between operations  15.1 us (2%)
    psum x1, waiting for transfers between devices, body(): lax.psum(dot_cols(head_rows, full_output).astype(BF), 'head').astype(F32)  93.5 us
    reduce_scatter x1, waiting for transfers between devices, body(): lax.psum_scatter(forward_grads, 'seq', scatter_dimension=0, tiled=False)  90.4 us
    psum x1, waiting for transfers between devices, body(): lax.psum((dot_cols(d_gate, full_gate) + dot_cols(d_up, full_up)).astype(B...  83.8 us
    all_gather x1, waiting for transfers between devices, body(): lax.all_gather(jnp.stack([gate_weight, up_weight, down_weight]), 'seq', a...  68.6 us
    reduce_scatter x1, waiting for transfers between devices, body(): lax.psum_scatter(dot_cols(hidden, full_down).astype(BF), 'head', scatter_...  42 us
    pallas_call x1, Pallas kernels, mixer_backward(): pl.pallas_call(functools.partial(mixer_backward_kernel, heads), name='mix...  39.1 us
    psum x1, blocking collectives, body(): gain_sum = lax.psum(jnp.sum(gain_part, 0), ('seq', 'head'))  38.5 us
    psum x1, blocking collectives, body(): small = lax.psum(seq_small, 'seq')  36.4 us
  transfers between devices with their start and end apart: 10, of which 8 were waited for; matrix products, arithmetic and copies ran while one was open for 10% of the time, Pallas kernels for 0%

profile of v1, /device:TPU:0, one launch (start us, length us, event | category | flops | bytes accessed | tf_op | source)
XLA Modules:
  0.0 830.0 jit_solution(15843159853588191143)
XLA Ops:
  12.1 4.9 collective-permute-start
  22.8 32.7 %all_gather.13 = bf16[1024,256]{1,0:T(8,128)(2,1)S(1)} all-gather(bf16[128,256]{1,0:T(8,128)(2,1)S(1)} %copy-done.22), channel_id=1, replica_groups=mesh['seq'=8,'head'=4] {'seq'}, dimensions={0}, use_global_device_ids=true | all-gather | bytes 589824 | tf_op jit(solution)/shard_map/all_gather | solution.py:525
  56.9 7.0 all-gather.4.cloned.1.call-done
  65.3 4.7 fusion.51.logits_ref
  70.0 4.9 convolution_convert_fusion.2.pre_ref
  75.8 30.6 %mixer_forward.1 = (bf16[2048,768]{1,0:T(8,128)(2,1)}, bf16[16,2,128,128]{3,2,1,0:T(8,128)(2,1)}, bf16[16,2,128,256]{3,2,1,0:T(8,128)(2,1)}, bf16[16,2,256,128]{...) custom-call(f32[32]{0:T(128)} %convert_element_type.124.resets_ref, ...), custom_call_target="tpu_custom_call" | custom-call | flops 3000000000 | bytes 20971520 | tf_op jit(solution)/shard_map/mixer_forward/pallas_call | solution.py:186
  108.3 12.3 %state_forward.1.state_ref = f32[2,128,128]{2,1,0:T(8,128)} custom-call(bf16[2,128,256]{2,1,0:T(8,128)(2,1)} %copy.88.part_ref), custom_call_target="tpu_custom_call" | custom-call | tf_op jit(solution)/shard_map/state_forward/pallas_call | solution.py:262
  120.6 6.8 mixer_output.1
  127.4 4.5 convolution_convert_fusion.1
  133.9 93.5 %all-reduce.4.cloned.1.call-done = bf16[2048,1024]{1,0:T(8,128)(2,1)} async-done(((bf16[2048,1024]{1,0:T(8,128)(2,1)}), bf16[2048,1024]{1,0:T(8,128)(2,1)}) %all-reduce.4.cloned.1.call-update) | async-done | bytes 4194320 | tf_op jit(solution)/shard_map/psum | solution.py:590
  227.5 5.0 multiply_reduce_fusion.1
  236.4 68.6 %all-gather.6.cloned.1.call-done = bf16[24,128,704]{1,2,0:T(8,128)(2,1)} async-done(((bf16[3,128,704]{1,2,0:T(8,128)(2,1)}), bf16[24,128,704]{1,2,0:T(8,128)(2,1)}) %all-gather.6.cloned.1.call-update) | async-done | bytes 4325392 | tf_op jit(solution)/shard_map/all_gather | solution.py:564
  316.9 8.4 %fusion.12 = (bf16[2048,704]{0,1:T(8,128)(2,1)}, bf16[2048,704]{0,1:T(8,128)(2,1)}, bf16[2048,704]{0,1:T(8,128)(2,1)}) fusion(f32[704,2048]{1,0:T(8,128)S(1)} %fusion.27, f32[2048,704]{0,1:T(8,128)S(1)} %fusion.25, bf16[2048,1024]{1,0:T(8,128)(2,1)S(1)} %copy-done.9, bf16[88,8,8,128]{3,2,1,0:T(8,128)(2,1)S(1)} %bitcast.109), kind=kOutput, calls=%fused_computation.27 | convolution fusion | flops 2975858688 | bytes 25821184 | tf_op jit(solution)/shard_map/dot_general | solution.py:513
  325.3 5.5 fusion.20
  330.8 5.5 add_convert_fusion.1
  336.4 83.8 %all-reduce.6.cloned.1.call-done = bf16[2048,1024]{1,0:T(8,128)(2,1)} async-done(((bf16[2048,1024]{1,0:T(8,128)(2,1)}), bf16[2048,1024]{1,0:T(8,128)(2,1)}) %all-reduce.6.cloned.1.call-update) | async-done | bytes 4194320 | tf_op jit(solution)/shard_map/psum | solution.py:614
  420.2 7.6 fusion.5
  428.5 6.8 fusion.4
  439.0 9.4 %mixer_back_state.1 = (bf16[2048,256]{1,0:T(8,128)(2,1)}, f32[8,128]{1,0:T(8,128)}, f32[2,128,128]{2,1,0:T(8,128)}) custom-call(bf16[2048,256]{1,0:T(8,128)(2,1)} %convolution_convert_fusion.3.dheads_ref, f32[2048,256]{1,0:T(8,128)} %get-tuple-element.41.delta_ref, f32[1,128]{1,0:T(1,128)} %bitcast_convert_fusion.gain_ref, ...), custom_call_target="tpu_custom_call" | custom-call | flops 300000000 | bytes 10485760 | tf_op jit(solution)/shard_map/mixer_back_state/pallas_call | solution.py:345
  450.0 23.2 %state_backward.1.arrive_ref = f32[2,128,128]{2,1,0:T(8,128)} custom-call(bf16[2,128,256]{2,1,0:T(8,128)(2,1)} %pad_maximum_fusion.3.part_ref), custom_call_target="tpu_custom_call" | custom-call | tf_op jit(solution)/shard_map/state_backward/pallas_call | solution.py:262
  473.2 39.1 %mixer_backward.1 = (bf16[2048,768]{1,0:T(8,128)(2,1)}, f32[8,768]{1,0:T(8,128)}, f32[8,768]{1,0:T(8,128)}, f32[4,8,768]{2,1,0:T(8,128)}, f32[2048,2]{1,0:T(8,128)}) custom-call(f32[32]{0:T(128)} %convert_element_type.124.resets_ref, bf16[2048,768]{1,0:T(8,128)(2,1)} %convolution_convert_fusion.2.pre_ref, bf16[16,768]{1,0:T(8,128)(2,1)} %fusion.43.halo_ref, ...), custom_call_target="tpu_custom_call" | custom-call | flops 3000000000 | bytes 20971520 | tf_op jit(solution)/shard_map/mixer_backward/pallas_call | solution.py:484
  520.0 5.1 add_convert_fusion
  526.3 5.6 fusion.30
  539.6 7.0 convolution_convert_fusion
  548.5 5.5 fusion.18
  569.0 4.2 fusion.46
  573.4 38.5 %psum.39 = f32[128]{0:T(128)} all-reduce(f32[128]{0:T(128)S(1)} %reduce_sum.99), channel_id=1, replica_groups=mesh['seq'=8,'head'=4] {'seq','head'}, use_global_device_ids=true, to_apply=%region_17.18 | all-reduce | flops 128 | bytes 1024 | tf_op jit(solution)/shard_map/psum | solution.py:653
  611.9 9.4 %fusion.6 = (f32[1024]{0:T(1024)S(1)}, f32[2048]{0:T(1024)S(1)}, f32[2048,1024]{1,0:T(8,128)}, f32[2048,1024]{1,0:T(8,128)}) fusion(bf16[2048,1024]{1,0:T(8,128)(2,1)} %all-reduce.8.cloned.1.call-done, bf16[2048,1024]{1,0:T(8,128)(2,1)} %param.15, f32[2048]{0:T(1024)S(1)} %add_rsqrt_fusion.1, f32[1024]{0:T(1024)S(1)} %get-tuple-element.110), kind=kLoop, calls=%fused_computation.13 | loop fusion | flops 16774144 | bytes 25190400 | tf_op jit(solution)/shard_map/reduce_sum | solution.py:638
  621.3 36.4 %psum.38 = f32[7168]{0:T(1024)S(1)} all-reduce(f32[7168]{0:T(1024)S(1)} %pad_maximum_fusion.4), channel_id=1, replica_groups=mesh['seq'=8,'head'=4] {'seq'}, use_global_device_ids=true, to_apply=%region_14.15 | all-reduce | flops 7168 | bytes 57344 | tf_op jit(solution)/shard_map/psum | solution.py:654
  664.2 16.6 %reduce-scatter.10.cloned.1.call-done = bf16[128,1024]{1,0:T(8,128)(2,1)} async-done(((bf16[1024,1024]{1,0:T(8,128)(2,1)}), bf16[128,1024]{1,0:T(8,128)(2,1)}) %reduce-scatter.10.cloned.1.call-update) | async-done | bytes 262160
  685.0 42.0 %reduce-scatter.6.cloned.1.call-done = bf16[2048,256]{1,0:T(8,128)(2,1)} async-done(((bf16[2048,1024]{1,0:T(8,128)(2,1)}), bf16[2048,256]{1,0:T(8,128)(2,1)}) %reduce-scatter.6.cloned.1.call-update) | async-done | bytes 1048592 | tf_op jit(solution)/shard_map/reduce_scatter | solution.py:599
  730.2 90.4 %reduce-scatter.8.cloned.1.call-done = bf16[1,3,128,704]{2,3,1,0:T(8,128)(2,1)} async-done(((bf16[8,3,128,704]{2,3,1,0:T(8,128)(2,1)}), bf16[1,3,128,704]{2,3,1,0:T(8,128)(2,1)}) %reduce-scatter.8.cloned.1.call-update) | async-done | bytes 540688 | tf_op jit(solution)/shard_map/reduce_scatter | solution.py:613
  (158 shorter events, 89.2 us)
Async XLA Ops:
  7.2 15.6 %copy-start.22 = (bf16[128,256]{1,0:T(8,128)(2,1)S(1)}, bf16[128,256]{1,0:T(8,128)(2,1)}, u32[]{:S(2)}) copy-start(bf16[128,256]{1,0:T(8,128)(2,1)} %param.23) | copy-start | bytes 196612
  7.2 48.9 %copy-start.24 = (bf16[3,4,256]{2,1,0:T(4,128)(2,1)S(1)}, bf16[3,4,256]{2,1,0:T(4,128)(2,1)}, u32[]{:S(2)}) copy-start(bf16[3,4,256]{2,1,0:T(4,128)(2,1)} %param.21) | copy-start | bytes 18436
  7.2 56.7 %all-gather.4.cloned.1.call-start = ((), (), s32[]{:S(2)}) async-start(), calls=%async_computation.3 | async-start | bytes 2064384 | tf_op jit(solution)/shard_map/all_gather | solution.py:525
  11.3 216.1 %all-reduce.4.cloned.1.call-start = ((), (), s32[]{:S(2)}) async-start(), calls=%async_computation.4 | async-start | bytes 8388608 | tf_op jit(solution)/shard_map/psum | solution.py:590
  12.1 44.6 %collective-permute-start = (bf16[16,1024]{1,0:T(8,128)(2,1)S(1)}, bf16[16,1024]{1,0:T(8,128)(2,1)S(1)}, u32[]{:S(2)}, u32[]{:S(2)}) collective-permute-start(bf16[16,1024]{1,0:T(8,128)(2,1)S(1)} %slice.69), channel_id=1, source_target_pairs={{0,4},{4,8},{8,12},{12,16},{16,20},{20,24},{24,28},{1,5},{5,9},{9,... | collective-permute-start | bytes 98312 | tf_op jit(solution)/shard_map/ppermute | solution.py:509
  65.3 4.7 copy-start.1
  65.3 4.7 copy-start.16
  131.9 173.2 %all-gather.6.cloned.1.call-start = ((), (), s32[]{:S(2)}) async-start(), calls=%async_computation.9 | async-start | bytes 4866048 | tf_op jit(solution)/shard_map/all_gather | solution.py:564
  133.8 286.4 %all-reduce.6.cloned.1.call-start = ((), (), s32[]{:S(2)}) async-start(), calls=%async_computation.6 | async-start | bytes 8388608 | tf_op jit(solution)/shard_map/psum | solution.py:614
  227.5 5.0 copy-start.2
  227.5 5.9 copy-start.5
  307.6 2.8 copy-start.11
  308.5 5.1 copy-start.14
  310.4 3.2 copy-start.9
  325.3 5.5 copy-start.30
  336.3 275.5 %all-reduce.8.cloned.1.call-start = ((), (), s32[]{:S(2)}) async-start(), calls=%async_computation.7 | async-start | bytes 8388608 | tf_op jit(solution)/shard_map/psum | solution.py:636
  420.2 7.7 copy-start.3
  420.2 7.7 copy-start.6
  420.2 8.3 %copy-start.7 = (bf16[2048,1024]{1,0:T(8,128)(2,1)S(1)}, bf16[2048,1024]{1,0:T(8,128)(2,1)}, u32[]{:S(2)}) copy-start(bf16[2048,1024]{1,0:T(8,128)(2,1)} %all-reduce.6.cloned.1.call-done) | copy-start | bytes 12582916
  435.3 3.7 copy-start
  473.2 40.6 %copy-start.17 = (bf16[1024,772]{1,0:T(8,128)(2,1)S(1)}, bf16[1024,772]{1,0:T(8,128)(2,1)}, u32[]{:S(2)}) copy-start(bf16[1024,772]{1,0:T(8,128)(2,1)} %all-gather.4.cloned.1.call-done) | copy-start | bytes 4743172
  512.3 5.9 collective-permute-start.1
  513.8 4.5 copy-start.23
  513.8 4.4 copy-start.26
  525.1 155.7 %reduce-scatter.10.cloned.1.call-start = ((), (), s32[]{:S(2)}) async-start(), calls=%async_computation.10 | async-start | bytes 2359296
  526.3 5.6 copy-start.4
  526.3 6.3 copy-start.28
  536.9 2.7 copy-start.15
  539.5 187.5 %reduce-scatter.6.cloned.1.call-start = ((), (), s32[]{:S(2)}) async-start(), calls=%async_computation.5 | async-start | bytes 5242880 | tf_op jit(solution)/shard_map/reduce_scatter | solution.py:599
  546.7 273.9 %reduce-scatter.8.cloned.1.call-start = ((), (), s32[]{:S(2)}) async-start(), calls=%async_computation.8 | async-start | bytes 4866048 | tf_op jit(solution)/shard_map/reduce_scatter | solution.py:613
  548.5 6.1 copy-start.31
  556.1 3.8 copy-start.32
  (11 other events, 15.1 us)
Sparse Core Ops, SparseCore 0:
  11.4 52.3 all-gather.3
  132.0 95.3 all-reduce.3
  229.9 75.1 all-gather.5
  336.5 83.7 all-reduce.5
  525.2 83.4 all-reduce.7
  612.5 68.2 reduce-scatter.9
  683.5 43.4 reduce-scatter.5
  730.6 89.9 reduce-scatter.7

commit v2 on v1

--- a/solution.py
+++ b/solution.py
@@ -203,7 +203,12 @@
     )(resets, pre, halo, taps, logits)
 
 
-def exchange_kernel(axis, count, window, backward, part_ref, state_ref, slots_ref, send_sem, recv_sem):
+def exchange_kernel(axis, count, window, backward, gathers, *refs):
+    if gathers:
+        part_ref, own_ref, state_ref, others_ref, slots_ref, send_sem, recv_sem, head_send, head_recv = refs
+        _, _, near, far = head_peers()
+    else:
+        part_ref, state_ref, slots_ref, send_sem, recv_sem = refs
     place = lax.axis_index(axis)
     ahead = count - 1 - place if backward else place
     behind = count - 1 - ahead
@@ -217,18 +222,37 @@
                 barrier, inc=1, device_id={axis: place - sign * hop}, device_id_type=MESH
             )
 
-    @pl.when(behind > 0)
-    def _():
-        pl.semaphore_wait(barrier, jnp.minimum(behind, window))
+    extra = 0
+    if gathers:
+        extra = 2
+        for target in (near, far):
+            pl.semaphore_signal(barrier, inc=1, device_id={"head": target}, device_id_type=MESH)
+
+        def near_copy():
+            return push(own_ref, others_ref.at[0], head_send.at[0], head_recv.at[0], "head", near)
+
+        def far_copy():
+            return push(own_ref, others_ref.at[1], head_send.at[1], head_recv.at[1], "head", far)
+
+        def pass_copy():
+            return push(others_ref.at[1], others_ref.at[2], head_send.at[2], head_recv.at[2], "head", near)
+
+    if gathers:
+        pl.semaphore_wait(barrier, jnp.minimum(behind, window) + extra)
+    else:
+
+        @pl.when(behind > 0)
+        def _():
+            pl.semaphore_wait(barrier, jnp.minimum(behind, window))
 
     def copy(hop):
-        return pltpu.make_async_remote_copy(
-            src_ref=part_ref,
-            dst_ref=slots_ref.at[hop - 1],
-            send_sem=send_sem.at[hop - 1],
-            recv_sem=recv_sem.at[hop - 1],
-            device_id={axis: place + sign * hop},
-            device_id_type=MESH,
+        return push(
+            part_ref,
+            slots_ref.at[hop - 1],
+            send_sem.at[hop - 1],
+            recv_sem.at[hop - 1],
+            axis,
+            place + sign * hop,
         )
 
     for hop in range(1, window + 1):
@@ -237,6 +261,9 @@
         def _():
             copy(hop).start()
 
+    if gathers:
+        far_copy().start()
+        near_copy().start()
     heads = state_ref.shape[0]
     state_ref[...] = jnp.zeros_like(state_ref)
     for hop in range(window, 0, -1):
@@ -248,6 +275,12 @@
                 part = slots_ref[hop - 1, head]
                 state_ref[head] = nn(part[:, :CHUNK], state_ref[head]) + part[:, CHUNK:].astype(F32)
 
+    if gathers:
+        far_copy().wait_recv()
+        pass_copy().start()
+        near_copy().wait()
+        far_copy().wait_send()
+        pass_copy().wait()
     for hop in range(1, window + 1):
 
         @pl.when(behind >= hop)
@@ -255,25 +288,33 @@
             copy(hop).wait_send()
 
 
-def exchange(part, axis, backward, collective):
+def exchange(part, own, axis, backward, collective):
     count = lax.axis_size(axis)
     window = min(count - 1, count // 2)
     heads = part.shape[0]
+    whole = pl.BlockSpec(memory_space=pltpu.VMEM)
+    gathers = own is not None
+    out_shape = [jax.ShapeDtypeStruct((heads, CHUNK, CHUNK), F32)]
+    scratch = [
+        pltpu.VMEM((window, heads, CHUNK, 2 * CHUNK), BF),
+        pltpu.SemaphoreType.DMA((window,)),
+        pltpu.SemaphoreType.DMA((window,)),
+    ]
+    if gathers:
+        out_shape.append(jax.ShapeDtypeStruct((3, *own.shape), own.dtype))
+        scratch += [pltpu.SemaphoreType.DMA((3,))] * 2
     return pl.pallas_call(
-        functools.partial(exchange_kernel, axis, count, window, backward),
+        functools.partial(exchange_kernel, axis, count, window, backward, gathers),
         name="state_backward" if backward else "state_forward",
-        out_shape=jax.ShapeDtypeStruct((heads, CHUNK, CHUNK), F32),
-        in_specs=[pl.BlockSpec(memory_space=pltpu.VMEM)],
-        out_specs=pl.BlockSpec(memory_space=pltpu.VMEM),
-        scratch_shapes=[
-            pltpu.VMEM((window, heads, CHUNK, 2 * CHUNK), BF),
-            pltpu.SemaphoreType.DMA((window,)),
-            pltpu.SemaphoreType.DMA((window,)),
-        ],
+        out_shape=out_shape,
+        in_specs=[whole] * (2 if gathers else 1),
+        out_specs=[whole] * len(out_shape),
+        scratch_shapes=scratch,
         compiler_params=pltpu.CompilerParams(
             collective_id=collective, has_side_effects=True, vmem_limit_bytes=VMEM_LIMIT
         ),
-    )(part)
+        cost_estimate=pl.CostEstimate(flops=10**9, bytes_accessed=20 << 20, transcendentals=0),
+    )(*((part, own) if gathers else (part,)))
 
 
 def mixer_output_kernel(heads, state_ref, start_ref, mq_ref, out0_ref, gain_ref, delta_ref, rows_ref, states_ref):
@@ -503,6 +544,268 @@
     )(resets, pre, halo, taps, logits, qkv, inv, wu, mq, states, ddelta, arrive)
 
 
+def head_peers():
+    place = lax.axis_index("head")
+    low = lax.rem(place, 2)
+    high = lax.rem(lax.div(place, 2), 2)
+    return place, low, place + 1 - 2 * low, place + 2 - 4 * high
+
+
+def push(src, dst, send_sem, recv_sem, axis, target):
+    return pltpu.make_async_remote_copy(
+        src_ref=src,
+        dst_ref=dst,
+        send_sem=send_sem,
+        recv_sem=recv_sem,
+        device_id={axis: target},
+        device_id_type=MESH,
+    )
+
+
+def greet(axis, targets):
+    barrier = pltpu.get_barrier_semaphore()
+    for target in targets:
+        pl.semaphore_signal(barrier, inc=1, device_id={axis: target}, device_id_type=MESH)
+    pl.semaphore_wait(barrier, len(targets))
+
+
+def middle_kernel(
+    steps,
+    hidden,
+    rows_ref,
+    weights_ref,
+    others_ref,
+    input_ref,
+    ct_ref,
+    late_ct_ref,
+    gain_ref,
+    dheads_ref,
+    update_ref,
+    mid_ref,
+    dmid_ref,
+    grads_ref,
+    gain_grad_ref,
+    full_ref,
+    acc_ref,
+    part_ref,
+    pair_ref,
+    far_ref,
+    sum_ref,
+    keep_ref,
+    scale_ref,
+    shard_ref,
+    row_near_send,
+    row_near_recv,
+    row_far_send,
+    row_far_recv,
+    row_pass_send,
+    row_pass_recv,
+    pair_send,
+    pair_recv,
+    far_send,
+    far_recv,
+    last_send,
+    last_recv,
+):
+    step = pl.program_id(0)
+    place, low, near, far = head_peers()
+    chunk, width = input_ref.shape
+    columns = rows_ref.shape[1]
+    half = width // 2
+    mine = pl.ds(pl.multiple_of(low * half, 128), half)
+    theirs = pl.ds(pl.multiple_of((1 - low) * half, 128), half)
+    own_columns = pl.ds(pl.multiple_of(place * columns, 128), columns)
+
+    def at(index):
+        return pl.ds(pl.multiple_of(index * chunk, chunk), chunk)
+
+    def near_rows(index):
+        return push(
+            rows_ref.at[at(index)], full_ref.at[0, at(index)], row_near_send.at[index], row_near_recv.at[index], "head", near
+        )
+
+    def far_rows(index):
+        return push(
+            rows_ref.at[at(index)], full_ref.at[1, at(index)], row_far_send.at[index], row_far_recv.at[index], "head", far
+        )
+
+    def pass_rows(index):
+        return push(
+            full_ref.at[1, at(index)], full_ref.at[2, at(index)], row_pass_send.at[index], row_pass_recv.at[index], "head", near
+        )
+
+    def pair(index):
+        return push(
+            part_ref.at[lax.rem(index, 2), :, theirs], pair_ref.at[index], pair_send.at[index], pair_recv.at[index], "head", near
+        )
+
+    def across(index):
+        return push(pair_ref.at[index], far_ref.at[index], far_send.at[index], far_recv.at[index], "head", far)
+
+    def last(index):
+        return push(
+            sum_ref.at[index, :, mine], sum_ref.at[index, :, mine], last_send.at[index], last_recv.at[index], "head", near
+        )
+
+    @pl.when(step == 0)
+    def _():
+        greet("head", (near, far))
+
+        @pl.loop(0, steps)
+        def _(index):
+            far_rows(index).start()
+            near_rows(index).start()
+
+        acc_ref[...] = jnp.zeros_like(acc_ref)
+        gain_grad_ref[...] = jnp.zeros_like(gain_grad_ref)
+
+    @pl.when(step < steps)
+    def _():
+        ct = ct_ref[...]
+        d_hidden = nn(ct, weights_ref[:, columns + 2 * hidden :])
+
+        @pl.when(step == 0)
+        def _():
+            far_rows(step).wait_recv()
+            pass_rows(step).start()
+
+        near_rows(step).wait_recv()
+        pass_rows(step).wait_recv()
+        rows = jnp.concatenate(
+            [rows_ref[at(step)], full_ref[0, at(step)], full_ref[1, at(step)], full_ref[2, at(step)]], 1
+        )
+        output = jnp.concatenate([weights_ref[:, :columns], others_ref[0], others_ref[1], others_ref[2]], 1)
+        middle = input_ref[...].astype(F32) + nt(rows, output)
+        keep_ref[lax.rem(step, 2)] = middle
+        mid_ref[...] = keep_ref[lax.rem(step, 2), :, own_columns]
+        scale = lax.rsqrt(jnp.mean(middle * middle, axis=-1, keepdims=True) + 1e-06)
+        scale_ref[lax.rem(step, 2)] = scale
+        second = (middle * scale * gain_ref[...]).astype(BF)
+        both = nn(second, weights_ref[:, columns : columns + 2 * hidden])
+        gate, up = both[:, :hidden], both[:, hidden:]
+        sig = sigmoid(gate)
+        silu = gate * sig
+        active = (silu * up).astype(BF)
+        d_gate = (d_hidden * up * (sig + silu * (1.0 - sig))).astype(BF)
+        d_up = (d_hidden * silu).astype(BF)
+        d_both = jnp.concatenate([d_gate, d_up], 1)
+
+        @pl.when(step >= 2)
+        def _():
+            pair(step - 2).wait_send()
+
+        part_ref[lax.rem(step, 2)] = nt(d_both, weights_ref[:, columns : columns + 2 * hidden]).astype(BF)
+        pair(step).start()
+
+        @pl.when(step + 1 < steps)
+        def _():
+            far_rows(step + 1).wait_recv()
+            pass_rows(step + 1).start()
+
+        update_ref[...] = nt(active, weights_ref[:, columns + 2 * hidden :]).astype(BF)
+        acc_ref[:, columns : columns + 2 * hidden] += tn(second, d_both)
+        acc_ref[:, columns + 2 * hidden :] += tn(ct, active)
+
+    @pl.when(step > 0)
+    def _():
+        done = step - 1
+        across(done).wait_recv()
+        across(done).wait_send()
+        total = pair_ref[done].astype(F32) + far_ref[done].astype(F32)
+        sum_ref[done, :, mine] = total.astype(BF)
+        last(done).start()
+
+    @pl.when(step < steps)
+    def _():
+        pair(step).wait_recv()
+        both = part_ref[lax.rem(step, 2), :, mine].astype(F32) + pair_ref[step].astype(F32)
+        pair_ref[step] = both.astype(BF)
+        across(step).start()
+
+    @pl.when(step > 0)
+    def _():
+        done = step - 1
+        last(done).wait_recv()
+        grad = sum_ref[done].astype(F32)
+        middle = keep_ref[lax.rem(done, 2)]
+        scale = scale_ref[lax.rem(done, 2)]
+        unit = middle * scale
+        gain_grad_ref[...] += jnp.sum((grad * unit).reshape(chunk // 8, 8, width), 0)
+        scaled = grad * gain_ref[...]
+        d_middle = late_ct_ref[...].astype(F32) + scale * (
+            scaled - unit * jnp.mean(scaled * unit, axis=-1, keepdims=True)
+        )
+        shard_ref[...] = d_middle
+        dmid_ref[...] = shard_ref[:, own_columns]
+        d_branch = d_middle.astype(BF)
+        dheads_ref[...] = nn(d_branch, weights_ref[:, :columns]).astype(BF)
+        acc_ref[:, :columns] += tn(d_branch, rows_ref[at(done)])
+
+    @pl.when(step == steps)
+    def _():
+        grads_ref[...] = acc_ref[...].astype(BF)
+
+        @pl.loop(0, steps)
+        def _(index):
+            near_rows(index).wait_send()
+            far_rows(index).wait_send()
+            pass_rows(index).wait_send()
+            last(index).wait_send()
+
+        for index in range(max(steps - 2, 0), steps):
+            pair(index).wait_send()
+
+
+def middle_stage(head_rows, weights, others, inputs, cotangent, gain, hidden, collective):
+    tokens, width = inputs.shape
+    columns = head_rows.shape[1]
+    chunk = min(256, tokens // 2)
+    steps = tokens // chunk
+    whole = pl.BlockSpec(memory_space=pltpu.VMEM)
+
+    def early(wide):
+        return pl.BlockSpec((chunk, wide), lambda s: (jnp.minimum(s, steps - 1), 0))
+
+    def late(wide):
+        return pl.BlockSpec((chunk, wide), lambda s: (jnp.maximum(s - 1, 0), 0))
+
+    dma = pltpu.SemaphoreType.DMA((steps,))
+    return pl.pallas_call(
+        functools.partial(middle_kernel, steps, hidden),
+        name="middle",
+        grid=(steps + 1,),
+        out_shape=(
+            jax.ShapeDtypeStruct((tokens, columns), BF),
+            jax.ShapeDtypeStruct((tokens, width), BF),
+            jax.ShapeDtypeStruct((tokens, columns), F32),
+            jax.ShapeDtypeStruct((tokens, columns), F32),
+            jax.ShapeDtypeStruct(weights.shape, BF),
+            jax.ShapeDtypeStruct((8, width), F32),
+        ),
+        in_specs=[whole, whole, whole, early(width), early(width), late(width), whole],
+        out_specs=(late(columns), early(width), early(columns), late(columns), whole, whole),
+        scratch_shapes=[
+            pltpu.VMEM((3, tokens, columns), BF),
+            pltpu.VMEM(weights.shape, F32),
+            pltpu.VMEM((2, chunk, width), BF),
+            pltpu.VMEM((steps, chunk, width // 2), BF),
+            pltpu.VMEM((steps, chunk, width // 2), BF),
+            pltpu.VMEM((steps, chunk, width), BF),
+            pltpu.VMEM((2, chunk, width), F32),
+            pltpu.VMEM((2, chunk, 1), F32),
+            pltpu.VMEM((chunk, width), F32),
+        ]
+        + [dma] * 12,
+        compiler_params=pltpu.CompilerParams(
+            collective_id=collective,
+            has_side_effects=True,
+            vmem_limit_bytes=VMEM_LIMIT,
+            dimension_semantics=("arbitrary",),
+        ),
+        cost_estimate=pl.CostEstimate(flops=30 * 10**9, bytes_accessed=30 << 20, transcendentals=2 << 20),
+    )(head_rows, weights, others, inputs, cotangent, cotangent, gain)
+
+
 def from_behind(block, axis, distance):
     devices = range(lax.axis_size(axis))
     route = [(i - distance, i) for i in devices if i - distance in devices]
@@ -560,9 +863,15 @@
     full_beta = mixer_pack[:, 3 * columns : 3 * columns + heads]
     gain_one = mixer_pack[:, 3 * columns + heads].astype(F32)
     gain_two = mixer_pack[:, 3 * columns + heads + 1].astype(F32)
-    full_output = gather_seq(output_weight)
-    forward_pack = lax.all_gather(jnp.stack([gate_weight, up_weight, down_weight]), "seq", axis=0)
-    full_gate, full_up, full_down = (forward_pack[:, i].reshape(width, hidden_columns) for i in range(3))
+    spare = -hidden_columns % 128
+    hidden_wide = hidden_columns + spare
+
+    def widen(block):
+        return jnp.pad(block, ((0, 0), (0, spare)))
+
+    weights = gather_seq(
+        jnp.concatenate([output_weight, widen(gate_weight), widen(up_weight), widen(down_weight)], 1)
+    )
 
     ends = jnp.sum(jnp.where(jnp.arange(4)[:, None] >= jnp.arange(4)[None, :], lengths[None, :], 0), axis=1)
     starts = ends - lengths
@@ -583,83 +892,51 @@
     taps = conv_weight.astype(F32).transpose(1, 0, 2).reshape(4, -1)
     qkv, inv, wu, mq, start, out0, total = mixer_forward(resets, pre, halo, taps, logits, heads)
     total_low = total.astype(BF)
-    state = exchange(total_low, "seq", False, 0)
+    state, others = exchange(total_low, weights[:, :columns], "seq", False, 0)
     gain_head = head_gain.astype(F32)[None, :]
     delta, head_rows, states = mixer_output(state, start, mq, out0, gain_head)
 
-    branch = lax.psum(dot_cols(head_rows, full_output).astype(BF), "head").astype(F32)
-    middle = inputs + branch
-    scale_two = lax.rsqrt(jnp.mean(middle * middle, axis=-1, keepdims=True) + 1e-06)
-    unit_two = middle * scale_two
-    second_rows = (unit_two * gain_two).astype(BF)
-    gate = dot(second_rows, full_gate)
-    up = dot(second_rows, full_up)
-    sig = jax.nn.sigmoid(gate)
-    hidden = (gate * sig * up).astype(BF)
-    update = lax.psum_scatter(
-        dot_cols(hidden, full_down).astype(BF), "head", scatter_dimension=1, tiled=True
+    d_heads, update_part, middle_shard, d_middle_shard, grads, second_grad = middle_stage(
+        head_rows, weights, others, block_input, cotangent, gain_two[None, :], hidden_wide, 2
     )
-    middle_shard = lax.dynamic_slice_in_dim(middle, column_start, columns, 1)
+    update = lax.psum_scatter(update_part, "head", scatter_dimension=1, tiled=True)
     block_output = (middle_shard + update.astype(F32)).astype(BF)
-    down_grad = dot_rows(cotangent, hidden)
-    d_hidden = dot(cotangent, full_down)
-    d_gate = (d_hidden * up * sig * (1.0 + gate * (1.0 - sig))).astype(BF)
-    d_up = (d_hidden * gate * sig).astype(BF)
-    gate_grad = dot_rows(second_rows, d_gate)
-    up_grad = dot_rows(second_rows, d_up)
-    forward_grads = jnp.stack(
-        [g.astype(BF).reshape(members, piece, hidden_columns) for g in (gate_grad, up_grad, down_grad)], 1
-    )
-    forward_sum = lax.psum_scatter(forward_grads, "seq", scatter_dimension=0, tiled=False).astype(F32)
-    d_second = lax.psum((dot_cols(d_gate, full_gate) + dot_cols(d_up, full_up)).astype(BF), "head").astype(F32)
-    second_part = jnp.sum(d_second * unit_two, 0)
-    scaled_two = gain_two * d_second
-    d_middle = cotangent.astype(F32) + scale_two * (
-        scaled_two - unit_two * jnp.mean(scaled_two * unit_two, axis=-1, keepdims=True)
-    )
-    d_branch = d_middle.astype(BF)
-    output_grad = dot_rows(d_branch, head_rows)
-    d_heads = dot(d_branch, full_output).astype(BF)
+    forward_sum = lax.psum_scatter(grads, "seq", scatter_dimension=0, tiled=True).astype(F32)
+    second_part = jnp.sum(second_grad, 0)
     ddelta, gain_part, shift = mixer_back_state(d_heads, delta, gain_head, mq)
     back_part = jnp.concatenate([total_low[:, :, :CHUNK].transpose(0, 2, 1), shift.astype(BF)], 2)
-    arrive = exchange(back_part, "seq", True, 1)
+    (arrive,) = exchange(back_part, None, "seq", True, 1)
     d_pre_own, tail, lead, taps_part, d_logits32 = mixer_backward(
         resets, pre, halo, taps, logits, qkv, inv, wu, mq, states, ddelta, arrive
     )
     received = from_behind(lead, "seq", -1)
     d_pre = lax.dynamic_update_slice_in_dim(d_pre_own, (tail + received).astype(BF), tokens - 8, 0)
     d_logits = d_logits32.astype(BF)
-    mixer_grads = jnp.concatenate([dot_rows(first_rows, d_pre), dot_rows(d_branch, head_rows)], 1).astype(BF)
+    mixer_grads = dot_rows(first_rows, d_pre).astype(BF)
     mixer_sum = lax.psum_scatter(mixer_grads, "seq", scatter_dimension=0, tiled=True).astype(F32)
     beta_part = dot_rows(first_rows, d_logits)
     d_first_part = dot_cols(d_pre, projection) + dot_cols(d_logits, full_beta)
-    d_first = lax.psum(d_first_part.astype(BF), "head").astype(F32)
+    d_first = lax.psum_scatter(d_first_part.astype(BF), "head", scatter_dimension=1, tiled=True).astype(F32)
     unit_one = inputs * scale_one
-    first_part = jnp.sum(d_first * unit_one, 0)
-    scaled_one = gain_one * d_first
-    d_input = d_middle + scale_one * (
-        scaled_one - unit_one * jnp.mean(scaled_one * unit_one, axis=-1, keepdims=True)
-    )
-    input_gradient = lax.dynamic_slice_in_dim(d_input, column_start, columns, 1)
-
-    seq_small = jnp.concatenate(
-        [
-            jnp.sum(taps_part, 1).reshape(-1),
-            beta_part.reshape(-1),
-            first_part,
-            second_part,
-        ]
-    )
-    gain_sum = lax.psum(jnp.sum(gain_part, 0), ("seq", "head"))
-    small = lax.psum(seq_small, "seq")
+    row_part = jnp.sum(d_first_part * gain_one * unit_one, axis=-1)
+    row_mean = lax.psum(row_part, "head") / width
+    unit_shard = lax.dynamic_slice_in_dim(unit_one, column_start, columns, 1)
+    gain_shard = lax.dynamic_slice_in_dim(gain_one, column_start, columns, 0)
+    first_shard = jnp.sum(d_first * unit_shard, 0)
+    first_part = lax.dynamic_update_slice_in_dim(jnp.zeros((width,), F32), first_shard, column_start, 0)
+    input_gradient = d_middle_shard + scale_one * (d_first * gain_shard - unit_shard * row_mean[:, None])
+
+    first_gathered = lax.psum(jnp.concatenate([first_part, jnp.sum(gain_part, 0)]), ("seq", "head"))
+    gain_sum = first_gathered[width:]
+    small = lax.psum(jnp.concatenate([jnp.sum(taps_part, 1).reshape(-1), beta_part.reshape(-1), second_part]), "seq")
     edge = 12 * columns
     conv_gradient = small[:edge].reshape(4, 3, columns).transpose(1, 0, 2)
     row_start = seq_place * piece
     beta_all = small[edge : edge + width * heads].reshape(width, heads)
     beta_gradient = lax.dynamic_slice_in_dim(beta_all, row_start, piece, 0)
     edge += width * heads
-    first_gradient = lax.dynamic_slice_in_dim(small, edge + row_start, piece, 0)
-    second_gradient = lax.dynamic_slice_in_dim(small, edge + width + row_start, piece, 0)
+    first_gradient = lax.dynamic_slice_in_dim(first_gathered, row_start, piece, 0)
+    second_gradient = lax.dynamic_slice_in_dim(small, edge + row_start, piece, 0)
     return (
         block_output,
         input_gradient,
@@ -670,11 +947,12 @@
         beta_gradient,
         conv_gradient,
         gain_sum,
-        mixer_sum[:, 3 * columns :],
+        forward_sum[:, :columns],
         second_gradient,
-        forward_sum[0],
-        forward_sum[1],
-        forward_sum[2],
+        *(
+            forward_sum[:, columns + i * hidden_wide : columns + i * hidden_wide + hidden_columns]
+            for i in range(3)
+        ),
     )
 
 

time: 839 us -> 636 us (0.76)
  waiting for transfers between devices: 404 us -> 234 us
  Pallas kernels: 121 us -> 225 us
  matrix products: 84.1 us -> 31.2 us
  other arithmetic: 53.9 us -> 18.3 us
  blocking collectives: 108 us -> 81.5 us
  local copies, waits for them, and re-layouts: 36.9 us -> 24.6 us
    psum x3 -> x0, waiting for transfers between devices: 177 us -> none  [the longest x1 93.5 us: body(): lax.psum(dot_cols(head_rows, full_output).astype(BF), 'head').astype(F32)]
    pallas_call x0 -> x1, Pallas kernels: none -> 94.9 us  [middle_stage(): pl.pallas_call(functools.partial(middle_kernel, steps, hidden), name='mid...]
    all_gather x1 -> x0, waiting for transfers between devices: 68.6 us -> none  [body(): lax.all_gather(jnp.stack([gate_weight, up_weight, down_weight]), 'seq', a...]
    all_gather x1 -> x2, waiting for transfers between devices: 7 us -> 74.5 us  [gather_seq(): return lax.all_gather(block, 'seq', axis=0, tiled=True)]
    all_gather x1 -> x0, blocking collectives: 32.7 us -> none  [gather_seq(): return lax.all_gather(block, 'seq', axis=0, tiled=True)]
    dot_general x6 -> x2, matrix products: 30.2 us -> 8.43 us  [dot_cols(): lax.dot_general(left, right, (((1,), (1,)), ((), ())), preferred_element_...]
    reduce_scatter x2 -> x4, waiting for transfers between devices: 132 us -> 153 us  [the longest x1 60.8 us: body(): lax.psum_scatter(grads, 'seq', scatter_dimension=0, tiled=True).astype(F32)]
    reduce_sum x4 -> x3, other arithmetic: 22.1 us -> 3.89 us  [the longest x1 3.86 us: body(): first_shard = jnp.sum(d_first * unit_shard, 0)]
  transfers between devices with their start and end apart: 10 -> 8, of which waited for: 8 -> 7; matrix products, arithmetic and copies ran while one was open for 10% -> 8% of each run, Pallas kernels for 0% -> 5%
where the time goes in v2:
time: 636 us; the launch traced here: 635 us
  waiting for transfers between devices  234 us (37%)
  Pallas kernels  225 us (35%)
  blocking collectives  81.5 us (13%)
  matrix products  31.2 us (5%)
  local copies, waits for them, and re-layouts  24.6 us (4%)
  other arithmetic  18.3 us (3%)
  between operations  14.4 us (2%)
  starting transfers between devices  6.6 us (1%)
    pallas_call x1, Pallas kernels, middle_stage(): pl.pallas_call(functools.partial(middle_kernel, steps, hidden), name='mid...  94.9 us
    all_gather x2, waiting for transfers between devices, gather_seq(): return lax.all_gather(block, 'seq', axis=0, tiled=True)  74.5 us
    reduce_scatter x1, waiting for transfers between devices, body(): lax.psum_scatter(grads, 'seq', scatter_dimension=0, tiled=True).astype(F32)  60.8 us
    reduce_scatter x1, waiting for transfers between devices, body(): lax.psum_scatter(d_first_part.astype(BF), 'head', scatter_dimension=1, ti...  44.5 us
    reduce_scatter x1, waiting for transfers between devices, body(): lax.psum_scatter(update_part, 'head', scatter_dimension=1, tiled=True)  44.3 us
    pallas_call x2, Pallas kernels, exchange(): pl.pallas_call(functools.partial(exchange_kernel, axis, count, window, ba...  44.1 us
    psum x1, blocking collectives, body(): lax.psum(jnp.concatenate([first_part, jnp.sum(gain_part, 0)]), ('seq', 'h...  42.1 us
    pallas_call x1, Pallas kernels, mixer_backward(): pl.pallas_call(functools.partial(mixer_backward_kernel, heads), name='mix...  39.1 us
  transfers between devices with their start and end apart: 8, of which 7 were waited for; matrix products, arithmetic and copies ran while one was open for 8% of the time, Pallas kernels for 5%

profile of v2, /device:TPU:0, one launch (start us, length us, event | category | flops | bytes accessed | tf_op | source)
XLA Modules:
  0.0 635.2 jit_solution(15878006785464767126)
XLA Ops:
  9.6 1.7 concatenate.15
  14.6 1.8 fusion.18
  17.2 4.9 collective-permute-start
  22.7 3.1 fusion
  27.2 33.4 %all-gather.3.cloned.1.call-done = bf16[1024,772]{1,0:T(8,128)(2,1)} async-done(((bf16[128,772]{1,0:T(8,128)(2,1)}), bf16[1024,772]{1,0:T(8,128)(2,1)}) %all-gather.3.cloned.1.call-update) | async-done | bytes 1581072 | tf_op jit(solution)/shard_map/all_gather | solution.py:828
  60.6 2.1 convert_reduce_fusion
  62.7 2.4 fusion.14.halo_ref
  65.0 4.7 fusion.25.logits_ref
  69.7 4.9 convolution_convert_fusion.pre_ref
  74.6 30.6 %mixer_forward.1 = (bf16[2048,768]{1,0:T(8,128)(2,1)}, bf16[16,2,128,128]{3,2,1,0:T(8,128)(2,1)}, bf16[16,2,128,256]{3,2,1,0:T(8,128)(2,1)}, bf16[16,2,256,128]{...) custom-call(f32[32]{0:T(128)} %convert_element_type.83.resets_ref, ...), custom_call_target="tpu_custom_call" | custom-call | flops 3000000000 | bytes 20971520 | tf_op jit(solution)/shard_map/mixer_forward/pallas_call | solution.py:186
  107.0 41.1 %all-gather.5.cloned.1.call-done.weights_ref = bf16[1024,2560]{1,0:T(8,128)(2,1)} async-done(((bf16[128,2560]{1,0:T(8,128)(2,1)}), bf16[1024,2560]{1,0:T(8,128)(2,1)}) %all-gather.5.cloned.1.call-update) | async-done | bytes 5242896 | tf_op jit(solution)/shard_map/all_gather | solution.py:828
  148.1 1.9 slice.93.refs_1_
  150.0 18.2 %state_forward.1 = (f32[2,128,128]{2,1,0:T(8,128)}, bf16[3,1024,256]{2,1,0:T(8,128)(2,1)}) custom-call(bf16[2,128,256]{2,1,0:T(8,128)(2,1)} %copy.70.refs_0_, bf16[1024,256]{1,0:T(8,128)(2,1)} %slice.93.refs_1_), custom_call_target="tpu_custom_call" | custom-call | flops 1000000000 | bytes 20971520 | tf_op jit(solution)/shard_map/state_forward/pallas_call | solution.py:306
  168.2 6.8 %mixer_output.1 = (f32[2048,256]{1,0:T(8,128)}, bf16[2048,256]{1,0:T(8,128)(2,1)}, bf16[16,2,128,128]{3,2,1,0:T(8,128)(2,1)}) custom-call(f32[2,128,128]{2,1,0:T(8,128)} %get-tuple-element.41.state_ref, bf16[16,2,128,256]{3,2,1,0:T(8,128)(2,1)} %get-tuple-element.42.start_ref, bf16[16,2,256,128]{3,2,1,0:T(8,128)(2,1)} %get-tuple-element.43.mq_ref, ...), custom_call_target="tpu_custom_call" | custom-call | flops 300000000 | bytes 10485760 | tf_op jit(solution)/shard_map/mixer_output/pallas_call | solution.py:345
  175.0 94.9 %middle.1 = (bf16[2048,256]{1,0:T(8,128)(2,1)}, bf16[2048,1024]{1,0:T(8,128)(2,1)}, f32[2048,256]{1,0:T(8,128)}, f32[2048,256]{1,0:T(8,128)}, bf16[1024,2560]{1,0:T(8,128)(2,1)}, /*index=5*/f32[8,1024]{1,0:T(8,128)}) custom-call(bf16[2048,256]{1,0:T(8,128)(2,1)} %get-tuple-element.45.rows_ref, bf16[1024,2560]{1,0:T(8,128)(2,1)} %all-gather.5.cloned.1.call-done.weights_ref, ...), custom_call_target="tpu_custom_call" | custom-call | flops 30000001024 | bytes 31457280 | tf_op jit(solution)/shard_map/middle/pallas_call | solution.py:773
  270.0 9.4 %mixer_back_state.1 = (bf16[2048,256]{1,0:T(8,128)(2,1)}, f32[8,128]{1,0:T(8,128)}, f32[2,128,128]{2,1,0:T(8,128)}) custom-call(bf16[2048,256]{1,0:T(8,128)(2,1)} %get-tuple-element.54.dheads_ref, f32[2048,256]{1,0:T(8,128)} %get-tuple-element.55.delta_ref, f32[1,128]{1,0:T(1,128)} %bitcast_convert_fusion.gain_ref, ...), custom_call_target="tpu_custom_call" | custom-call | flops 300000000 | bytes 10485760 | tf_op jit(solution)/shard_map/mixer_back_state/pallas_call | solution.py:386
  281.0 26.0 %state_backward.1.arrive_ref = f32[2,128,128]{2,1,0:T(8,128)} custom-call(bf16[2,128,256]{2,1,0:T(8,128)(2,1)} %pad_maximum_fusion.refs_0_), custom_call_target="tpu_custom_call" | custom-call | flops 1000000000 | bytes 20971520 | tf_op jit(solution)/shard_map/state_backward/pallas_call | solution.py:306
  306.9 39.1 %mixer_backward.1 = (bf16[2048,768]{1,0:T(8,128)(2,1)}, f32[8,768]{1,0:T(8,128)}, f32[8,768]{1,0:T(8,128)}, f32[4,8,768]{2,1,0:T(8,128)}, f32[2048,2]{1,0:T(8,128)}) custom-call(f32[32]{0:T(128)} %convert_element_type.83.resets_ref, bf16[2048,768]{1,0:T(8,128)(2,1)} %convolution_convert_fusion.pre_ref, bf16[16,768]{1,0:T(8,128)(2,1)} %fusion.14.halo_ref, ...), custom_call_target="tpu_custom_call" | custom-call | flops 3000000000 | bytes 20971520 | tf_op jit(solution)/shard_map/mixer_backward/pallas_call | solution.py:525
  347.3 4.6 collective-permute-done.1
  353.3 6.8 %convolution_convert_fusion.1 = bf16[1024,768]{1,0:T(8,128)(2,1)} fusion(bf16[2048,768]{1,0:T(8,128)(2,1)} %fusion.34, f32[1024]{0:T(1024)S(1)} %get-tuple-element.109, f32[2048]{0:T(1024)S(1)} %add_rsqrt_fusion, bf16[2048,1024]{1,0:T(8,128)(2,1)S(1)} %copy-done.1), kind=kOutput, calls=%fused_computation.18 | convolution fusion | flops 3230400512 | bytes 8925184 | tf_op jit(solution)/shard_map/dot_general | solution.py:820
  364.5 7.2 %multiply_reduce_fusion = (f32[2048]{0:T(1024)S(1)}, bf16[2048,1024]{1,0:T(8,128)(2,1)}, f32[2048,1024]{1,0:T(8,128)}) fusion(f32[1024]{0:T(1024)S(1)} %get-tuple-element.109, f32[2048]{0:T(1024)S(1)} %add_rsqrt_fusion, bf16[2048,1024]{1,0:T(8,128)(2,1)S(1)} %copy-done.2, f32[2048,1024]{1,0:T(8,128)S(1)} %fusion.22, bf16[2048,768]{1,0:T(8,128)(2,1)S(1)} %copy-done.5, ...), kind=kOutput, calls=%fused_computation.3 | convolution fusion | flops 3235903488 | bytes 29904896 | tf_op jit(solution)/shard_map/dot_general | solution.py:824
  372.7 4.0 fusion.20
  377.0 33.3 %psum.23 = f32[6144]{0:T(1024)S(1)} all-reduce(f32[6144]{0:T(1024)S(1)} %pad_maximum_fusion.1), channel_id=1, replica_groups=mesh['seq'=8,'head'=4] {'seq'}, use_global_device_ids=true, to_apply=%region_14.15 | all-reduce | flops 6144 | bytes 49152 | tf_op jit(solution)/shard_map/psum | solution.py:931
  412.7 6.1 psum.21
  418.9 3.6 reduce-scatter.9.cloned.1.call-done
  422.5 1.7 fusion.36
  424.1 44.3 %reduce-scatter.5.cloned.1.call-done = bf16[2048,256]{1,0:T(8,128)(2,1)} async-done(((bf16[2048,1024]{1,0:T(8,128)(2,1)}), bf16[2048,256]{1,0:T(8,128)(2,1)}) %reduce-scatter.5.cloned.1.call-update) | async-done | bytes 1048592 | tf_op jit(solution)/shard_map/reduce_scatter | solution.py:902
  468.5 2.4 add_convert_fusion
  470.9 44.5 %reduce-scatter.7.cloned.1.call-done = bf16[2048,256]{1,0:T(8,128)(2,1)} async-done(((bf16[2048,1024]{1,0:T(8,128)(2,1)}), bf16[2048,256]{1,0:T(8,128)(2,1)}) %reduce-scatter.7.cloned.1.call-update) | async-done | bytes 1048592 | tf_op jit(solution)/shard_map/reduce_scatter | solution.py:919
  515.4 3.9 fusion.4
  519.5 42.1 %psum.22 = f32[1152]{0:T(1024)S(1)} all-reduce(f32[1152]{0:T(1024)S(1)} %pad_maximum_fusion.2), channel_id=1, replica_groups=mesh['seq'=8,'head'=4] {'seq','head'}, use_global_device_ids=true, to_apply=%region_10.11 | all-reduce | flops 1152 | bytes 9216 | tf_op jit(solution)/shard_map/psum | solution.py:929
  562.2 60.8 %reduce-scatter.11.cloned.1.call-done = bf16[128,2560]{1,0:T(8,128)(2,1)} async-done(((bf16[1024,2560]{1,0:T(8,128)(2,1)}), bf16[128,2560]{1,0:T(8,128)(2,1)}) %reduce-scatter.11.cloned.1.call-update) | async-done | bytes 655376 | tf_op jit(solution)/shard_map/reduce_scatter | solution.py:904
  (90 shorter events, 28.6 us)
Async XLA Ops:
  7.2 14.9 %copy-start.11 = (s32[4]{0:T(128)S(1)}, s32[4]{0:T(128)}, u32[]{:S(2)}) copy-start(s32[4]{0:T(128)} %param.28) | copy-start | bytes 52
  7.2 15.0 %copy-start.12 = (bf16[128]{0:T(256)(128)(2,1)S(1)}, bf16[128]{0:T(256)(128)(2,1)}, u32[]{:S(2)}) copy-start(bf16[128]{0:T(256)(128)(2,1)} %param.22) | copy-start | bytes 772
  7.2 53.4 %all-gather.3.cloned.1.call-start = ((), (), s32[]{:S(2)}) async-start(), calls=%async_computation.4 | async-start | bytes 2064384 | tf_op jit(solution)/shard_map/all_gather | solution.py:828
  11.3 136.8 %all-gather.5.cloned.1.call-start = ((), (), s32[]{:S(2)}) async-start(), calls=%async_computation.5 | async-start | bytes 5898240 | tf_op jit(solution)/shard_map/all_gather | solution.py:828
  14.6 11.9 %copy-start.9 = (bf16[3,4,256]{2,1,0:T(4,128)(2,1)S(1)}, bf16[3,4,256]{2,1,0:T(4,128)(2,1)}, u32[]{:S(2)}) copy-start(bf16[3,4,256]{2,1,0:T(4,128)(2,1)} %param.21) | copy-start | bytes 18436
  16.4 406.1 %reduce-scatter.9.cloned.1.call-start = ((), (), s32[]{:S(2)}) async-start(), calls=%async_computation.8 | async-start | bytes 1769472 | tf_op jit(solution)/shard_map/reduce_scatter | solution.py:916
  17.2 9.8 %collective-permute-start = (bf16[16,1024]{1,0:T(8,128)(2,1)S(1)}, bf16[16,1024]{1,0:T(8,128)(2,1)S(1)}, u32[]{:S(2)}, u32[]{:S(2)}) collective-permute-start(bf16[16,1024]{1,0:T(8,128)(2,1)S(1)} %slice.73), channel_id=1, source_target_pairs={{0,4},{4,8},{8,12},{12,16},{16,20},{20,24},{24,28},{1,5},{5,9},{9,... | collective-permute-start | bytes 98312 | tf_op jit(solution)/shard_map/ppermute | solution.py:812
  65.0 4.7 copy-start
  65.0 4.7 copy-start.3
  306.9 46.4 %copy-start.1 = (bf16[2048,1024]{1,0:T(8,128)(2,1)S(1)}, bf16[2048,1024]{1,0:T(8,128)(2,1)}, u32[]{:S(2)}) copy-start(bf16[2048,1024]{1,0:T(8,128)(2,1)} %input_ref.1) | copy-start | bytes 12582916
  346.0 5.9 collective-permute-start.1
  360.1 1.2 copy-start.4
  360.2 108.3 %reduce-scatter.5.cloned.1.call-start = ((), (), s32[]{:S(2)}) async-start(), calls=%async_computation.6 | async-start | bytes 5242880 | tf_op jit(solution)/shard_map/reduce_scatter | solution.py:902
  360.7 154.7 %reduce-scatter.7.cloned.1.call-start = ((), (), s32[]{:S(2)}) async-start(), calls=%async_computation.7 | async-start | bytes 5242880 | tf_op jit(solution)/shard_map/reduce_scatter | solution.py:919
  361.4 2.2 copy-start.2
  361.4 3.2 copy-start.5
  371.8 0.9 copy-start.8
  371.8 0.9 copy-start.7
  371.8 251.2 %reduce-scatter.11.cloned.1.call-start = ((), (), s32[]{:S(2)}) async-start(), calls=%async_computation.9 | async-start | bytes 5898240 | tf_op jit(solution)/shard_map/reduce_scatter | solution.py:904
  372.7 37.6 %copy-start.10 = (f32[8,128]{1,0:T(8,128)S(1)}, f32[8,128]{1,0:T(8,128)}, u32[]{:S(2)}) copy-start(f32[8,128]{1,0:T(8,128)} %get-tuple-element.62) | copy-start | bytes 12292
  376.8 91.7 %copy-start.6 = (f32[2048,256]{1,0:T(8,128)S(1)}, f32[2048,256]{1,0:T(8,128)}, u32[]{:S(2)}) copy-start(f32[2048,256]{1,0:T(8,128)} %get-tuple-element.47) | copy-start | bytes 6291460
Sparse Core Ops, SparseCore 0:
  11.4 49.0 all-gather.2
  62.8 85.3 all-gather.4
  360.3 62.1 reduce-scatter.8
  425.0 43.4 reduce-scatter.4
  470.9 44.5 reduce-scatter.6
  519.3 103.5 reduce-scatter.10

commit v3 on v2

--- a/solution.py
+++ b/solution.py
@@ -204,7 +204,18 @@
 
 
 def exchange_kernel(axis, count, window, backward, gathers, *refs):
-    if gathers:
+    if backward:
+        (
+            part_ref, update_ref, mid_ref, state_ref, block_ref, slots_ref, send_sem, recv_sem,
+            near_ref, relay_ref, far_ref, *sems,
+        ) = refs
+        _, _, near, far = head_peers()
+        chunk = 256
+        steps = update_ref.shape[0] // chunk
+        at, _, start_pair, pass_on, own_sum, finish = head_scatter_copies(
+            chunk, update_ref, near_ref, relay_ref, far_ref, sems
+        )
+    elif gathers:
         part_ref, own_ref, state_ref, others_ref, slots_ref, send_sem, recv_sem, head_send, head_recv = refs
         _, _, near, far = head_peers()
     else:
@@ -223,11 +234,13 @@
             )
 
     extra = 0
-    if gathers:
+    if gathers or backward:
         extra = 2
         for target in (near, far):
             pl.semaphore_signal(barrier, inc=1, device_id={"head": target}, device_id_type=MESH)
 
+    if gathers:
+
         def near_copy():
             return push(own_ref, others_ref.at[0], head_send.at[0], head_recv.at[0], "head", near)
 
@@ -237,13 +250,7 @@
         def pass_copy():
             return push(others_ref.at[1], others_ref.at[2], head_send.at[2], head_recv.at[2], "head", near)
 
-    if gathers:
-        pl.semaphore_wait(barrier, jnp.minimum(behind, window) + extra)
-    else:
-
-        @pl.when(behind > 0)
-        def _():
-            pl.semaphore_wait(barrier, jnp.minimum(behind, window))
+    pl.semaphore_wait(barrier, jnp.minimum(behind, window) + extra)
 
     def copy(hop):
         return push(
@@ -264,6 +271,16 @@
     if gathers:
         far_copy().start()
         near_copy().start()
+    if backward:
+
+        @pl.loop(0, steps)
+        def _(index):
+            start_pair(index)
+
+        @pl.loop(0, steps)
+        def _(index):
+            pass_on(index)
+
     heads = state_ref.shape[0]
     state_ref[...] = jnp.zeros_like(state_ref)
     for hop in range(window, 0, -1):
@@ -281,6 +298,13 @@
         near_copy().wait()
         far_copy().wait_send()
         pass_copy().wait()
+    if backward:
+
+        @pl.loop(0, steps)
+        def _(index):
+            block_ref[at(index)] = (mid_ref[at(index)] + own_sum(index)).astype(BF)
+            finish(index)
+
     for hop in range(1, window + 1):
 
         @pl.when(behind >= hop)
@@ -288,12 +312,12 @@
             copy(hop).wait_send()
 
 
-def exchange(part, own, axis, backward, collective):
+def exchange(part, extras, axis, backward, collective):
     count = lax.axis_size(axis)
     window = min(count - 1, count // 2)
     heads = part.shape[0]
     whole = pl.BlockSpec(memory_space=pltpu.VMEM)
-    gathers = own is not None
+    gathers = not backward
     out_shape = [jax.ShapeDtypeStruct((heads, CHUNK, CHUNK), F32)]
     scratch = [
         pltpu.VMEM((window, heads, CHUNK, 2 * CHUNK), BF),
@@ -301,20 +325,24 @@
         pltpu.SemaphoreType.DMA((window,)),
     ]
     if gathers:
-        out_shape.append(jax.ShapeDtypeStruct((3, *own.shape), own.dtype))
+        out_shape.append(jax.ShapeDtypeStruct((3, *extras[0].shape), extras[0].dtype))
         scratch += [pltpu.SemaphoreType.DMA((3,))] * 2
+    else:
+        tokens, columns = extras[1].shape
+        out_shape.append(jax.ShapeDtypeStruct((tokens, columns), BF))
+        scratch += head_scatter_scratch(tokens, columns, tokens // 256)
     return pl.pallas_call(
         functools.partial(exchange_kernel, axis, count, window, backward, gathers),
         name="state_backward" if backward else "state_forward",
         out_shape=out_shape,
-        in_specs=[whole] * (2 if gathers else 1),
+        in_specs=[whole] * (1 + len(extras)),
         out_specs=[whole] * len(out_shape),
         scratch_shapes=scratch,
         compiler_params=pltpu.CompilerParams(
             collective_id=collective, has_side_effects=True, vmem_limit_bytes=VMEM_LIMIT
         ),
         cost_estimate=pl.CostEstimate(flops=10**9, bytes_accessed=20 << 20, transcendentals=0),
-    )(*((part, own) if gathers else (part,)))
+    )(part, *extras)
 
 
 def mixer_output_kernel(heads, state_ref, start_ref, mq_ref, out0_ref, gain_ref, delta_ref, rows_ref, states_ref):
@@ -411,14 +439,23 @@
     ddelta_ref,
     arrive_ref,
     dpre_ref,
-    tail_ref,
-    lead_ref,
     taps_grad_ref,
-    dlogits_ref,
     carry_ref,
     pad_ref,
     dpad_ref,
+    tail_ref,
+    lead_ref,
+    edge_ref,
+    send_sem,
+    recv_sem,
 ):
+    member, members = lax.axis_index("seq"), lax.axis_size("seq")
+    barrier = pltpu.get_barrier_semaphore()
+
+    @pl.when(member + 1 < members)
+    def _():
+        pl.semaphore_signal(barrier, inc=1, device_id={"seq": member + 1}, device_id_type=MESH)
+
     columns = heads * CHUNK
     chunks = mq_ref.shape[0]
     rows, cols = grid_indices()
@@ -485,7 +522,11 @@
                 unit = raw * inv
                 grads[kind][head] = (grad - unit * jnp.sum(unit * grad, axis=-1, keepdims=True)) * inv
             grads[2][head] = value_grad
-        dlogits_ref[at, :] = jnp.concatenate(dlogits, 1)
+        lanes = lax.broadcasted_iota(jnp.int32, (CHUNK, CHUNK), 1)
+        spread = jnp.zeros((CHUNK, CHUNK), F32)
+        for head in range(heads):
+            spread = jnp.where(lanes == head, dlogits[head], spread)
+        dpre_ref[at, 3 * columns :] = spread.astype(BF)
         dmixed = jnp.concatenate([g for kind in grads for g in kind], 1) * slope
         dpad_ref[0:GROUP] = dmixed[:GROUP]
         dpad_ref[GROUP : GROUP + 8] = dmixed[GROUP : GROUP + 8] * keep1
@@ -498,11 +539,11 @@
             dpre = term if dpre is None else dpre + term
             seen = (dmixed * tap_rows(pad_ref, tap)).reshape(CHUNK // 8, 8, 3 * columns)
             taps_grad_ref[tap] += jnp.sum(seen, 0)
-        dpre_ref[at, :] = dpre.astype(BF)
+        dpre_ref[at, : 3 * columns] = dpre.astype(BF)
 
         @pl.when(step == 0)
         def _():
-            tail_ref[...] = dpre[CHUNK - 8 :]
+            tail_ref[...] = dpre[CHUNK - 16 :]
 
         dpad_ref[136:144] = dmixed[:8] * keep0
         return carry
@@ -517,8 +558,27 @@
         lead = lead + taps_ref[tap : tap + 1] * dpad_ref[back : back + 8]
     lead_ref[...] = lead
 
-
-def mixer_backward(resets, pre, halo, taps, logits, qkv, inv, wu, mq, states, ddelta, arrive):
+    def to_previous(target):
+        return push(lead_ref, edge_ref, send_sem, recv_sem, "seq", target)
+
+    @pl.when(member > 0)
+    def _():
+        pl.semaphore_wait(barrier, 1)
+        to_previous(member - 1).start()
+
+    @pl.when(member + 1 < members)
+    def _():
+        to_previous(member).wait_recv()
+        last = pl.ds(dpre_ref.shape[0] - 16, 16)
+        late = stack(tail_ref[0:8], tail_ref[8:16] + edge_ref[...])
+        dpre_ref[last, : 3 * columns] = late.astype(BF)
+
+    @pl.when(member > 0)
+    def _():
+        to_previous(member - 1).wait_send()
+
+
+def mixer_backward(resets, pre, halo, taps, logits, qkv, inv, wu, mq, states, ddelta, arrive, collective):
     chunks, heads = mq.shape[:2]
     tokens = chunks * CHUNK
     columns = heads * CHUNK
@@ -526,20 +586,24 @@
         functools.partial(mixer_backward_kernel, heads),
         name="mixer_backward",
         out_shape=(
-            jax.ShapeDtypeStruct((tokens, 3 * columns), BF),
-            jax.ShapeDtypeStruct((8, 3 * columns), F32),
-            jax.ShapeDtypeStruct((8, 3 * columns), F32),
+            jax.ShapeDtypeStruct((tokens, 3 * columns + CHUNK), BF),
             jax.ShapeDtypeStruct((4, 8, 3 * columns), F32),
-            jax.ShapeDtypeStruct((tokens, heads), F32),
         ),
         in_specs=[pl.BlockSpec(memory_space=pltpu.SMEM)] + [pl.BlockSpec(memory_space=pltpu.VMEM)] * 11,
-        out_specs=tuple([pl.BlockSpec(memory_space=pltpu.VMEM)] * 5),
+        out_specs=tuple([pl.BlockSpec(memory_space=pltpu.VMEM)] * 2),
         scratch_shapes=[
             pltpu.VMEM((heads, CHUNK, CHUNK), F32),
             pltpu.VMEM((144, 3 * columns), F32),
             pltpu.VMEM((144, 3 * columns), F32),
+            pltpu.VMEM((16, 3 * columns), F32),
+            pltpu.VMEM((8, 3 * columns), F32),
+            pltpu.VMEM((8, 3 * columns), F32),
+            pltpu.SemaphoreType.DMA,
+            pltpu.SemaphoreType.DMA,
         ],
-        compiler_params=pltpu.CompilerParams(vmem_limit_bytes=VMEM_LIMIT),
+        compiler_params=pltpu.CompilerParams(
+            collective_id=collective, has_side_effects=True, vmem_limit_bytes=VMEM_LIMIT
+        ),
         cost_estimate=pl.CostEstimate(flops=3 * 10**9, bytes_accessed=20 << 20, transcendentals=2 << 20),
     )(resets, pre, halo, taps, logits, qkv, inv, wu, mq, states, ddelta, arrive)
 
@@ -806,6 +870,343 @@
     )(head_rows, weights, others, inputs, cotangent, cotangent, gain)
 
 
+def zeros_below(value):
+    return (value & -value).bit_length() - 1
+
+
+def flip(place, mask):
+    bit = 1
+    while bit <= mask:
+        if mask & bit:
+            place = place + bit - 2 * bit * lax.rem(lax.div(place, bit), 2)
+        bit *= 2
+    return place
+
+
+def head_scatter_copies(chunk, part_ref, near_ref, send_ref, far_ref, sems):
+    place, low, near, far = head_peers()
+    high = lax.rem(lax.div(place, 2), 2)
+    columns = far_ref.shape[-1]
+    near_send, near_recv, far_send, far_recv = sems
+
+    def at(index):
+        return pl.ds(pl.multiple_of(index * chunk, chunk), chunk)
+
+    def cols(owner):
+        return pl.ds(pl.multiple_of(owner * columns, 128), columns)
+
+    def pair(index, side_):
+        return push(
+            part_ref.at[at(index), cols(2 * side_ + 1 - low)],
+            near_ref.at[side_, at(index)],
+            near_send.at[side_, index],
+            near_recv.at[side_, index],
+            "head",
+            near,
+        )
+
+    def across(index):
+        return push(send_ref.at[at(index)], far_ref.at[at(index)], far_send.at[index], far_recv.at[index], "head", far)
+
+    def start_pair(index):
+        pair(index, 0).start()
+        pair(index, 1).start()
+
+    def pass_on(index):
+        pair(index, 0).wait_recv()
+        pair(index, 1).wait_recv()
+        total = part_ref[at(index), cols(2 * (1 - high) + low)].astype(F32) + near_ref[1 - high, at(index)].astype(F32)
+        send_ref[at(index)] = total.astype(BF)
+        across(index).start()
+
+    def own_sum(index):
+        across(index).wait_recv()
+        near_part = part_ref[at(index), cols(place)].astype(F32) + near_ref[high, at(index)].astype(F32)
+        return near_part + far_ref[at(index)].astype(F32)
+
+    def finish(index):
+        pair(index, 0).wait_send()
+        pair(index, 1).wait_send()
+        across(index).wait_send()
+
+    return at, cols, start_pair, pass_on, own_sum, finish
+
+
+def head_scatter_scratch(tokens, columns, steps):
+    return [
+        pltpu.VMEM((2, tokens, columns), BF),
+        pltpu.VMEM((tokens, columns), BF),
+        pltpu.VMEM((tokens, columns), BF),
+        pltpu.SemaphoreType.DMA((2, steps)),
+        pltpu.SemaphoreType.DMA((2, steps)),
+        pltpu.SemaphoreType.DMA((steps,)),
+        pltpu.SemaphoreType.DMA((steps,)),
+    ]
+
+
+def final_kernel(
+    members,
+    chunk,
+    rows_ref,
+    dpre_ref,
+    pack_ref,
+    input_ref,
+    scale_ref,
+    gain_ref,
+    dmid_ref,
+    small_ref,
+    ingrad_ref,
+    piece_ref,
+    sums_ref,
+    acc_ref,
+    out_ref,
+    slots_ref,
+    part_ref,
+    near_ref,
+    send_ref,
+    far_ref,
+    near_send,
+    near_recv,
+    far_send,
+    far_recv,
+    stat_ref,
+    stat_slots,
+    small_slots,
+    piece_send,
+    piece_recv,
+    stat_send,
+    stat_recv,
+    small_send,
+    small_recv,
+):
+    tokens, width = input_ref.shape
+    steps = tokens // chunk
+    place, low, near, far = head_peers()
+    member = lax.axis_index("seq")
+    rows = width // members
+    stages = (members - 1).bit_length()
+    at, cols, start_pair, pass_on, own_sum, finish = head_scatter_copies(
+        chunk, part_ref, near_ref, send_ref, far_ref, (near_send, near_recv, far_send, far_recv)
+    )
+
+    barrier = pltpu.get_barrier_semaphore()
+    for target in (near, far):
+        pl.semaphore_signal(barrier, inc=1, device_id={"head": target}, device_id_type=MESH)
+    for stage in range(stages):
+        pl.semaphore_signal(barrier, inc=1, device_id={"seq": flip(member, 1 << stage)}, device_id_type=MESH)
+    pl.semaphore_wait(barrier, 2 + stages)
+
+    order = sorted(range(members), key=lambda r: zeros_below(r) if r else stages)
+    sent = [r for r in order if r]
+    events = {}
+    for r in order:
+        for stage in range(zeros_below(r) if r else stages):
+            events[stage, r] = len(events)
+
+    def give(r):
+        stage = zeros_below(r)
+        slot = events[stage, r ^ (1 << stage)]
+        return push(
+            out_ref.at[r],
+            slots_ref.at[slot],
+            piece_send.at[r],
+            piece_recv.at[slot],
+            "seq",
+            flip(member, 1 << stage),
+        )
+
+    def take(stage, r):
+        slot = events[stage, r]
+        return push(
+            out_ref.at[0], slots_ref.at[slot], piece_send.at[0], piece_recv.at[slot], "seq", flip(member, 1 << stage)
+        )
+
+    def send_piece(r):
+        out_ref[r] = acc_ref[flip(member, r)].astype(BF)
+        give(r).start()
+
+    def receive(r):
+        index = flip(member, r)
+        for stage in range(zeros_below(r) if r else stages):
+            take(stage, r).wait_recv()
+            acc_ref[index] += slots_ref[events[stage, r]].astype(F32)
+        if r:
+            send_piece(r)
+
+    first = sorted([r for r in range(members) if r % 2], key=lambda r: order.index(r ^ 1))
+    evens = [r for r in order if r % 2 == 0]
+    if rows % 128 == 0:
+        for r in first + evens:
+            index = flip(member, r)
+            columns = pl.ds(pl.multiple_of(index * rows, 128), rows)
+            acc_ref[index] = tn(rows_ref[:, columns], dpre_ref[...])
+            if r % 2:
+                send_piece(r)
+    else:
+        per = 128 // rows
+        for unit in range(width // 128):
+            block = tn(rows_ref[:, unit * 128 : (unit + 1) * 128], dpre_ref[...])
+            acc_ref[unit * per : (unit + 1) * per] = block.reshape(per, rows, block.shape[1])
+        for r in first:
+            send_piece(r)
+
+    small_slots[0] = small_ref[...]
+    diagonal = lax.broadcasted_iota(jnp.int32, (128, 128), 0) == lax.broadcasted_iota(jnp.int32, (128, 128), 1)
+
+    def project(index):
+        part = nt(dpre_ref[at(index)], pack_ref[...])
+        part_ref[at(index)] = part.astype(BF)
+        start_pair(index)
+        seen = part * (input_ref[at(index)].astype(F32) * scale_ref[at(index)])
+        small_slots[0, 0:1] += jnp.sum(seen, 0, keepdims=True)
+        stat = jnp.sum(seen * gain_ref[...], axis=-1, keepdims=True)
+        for block in range(chunk // 128):
+            line = jnp.where(diagonal, stat[block * 128 : (block + 1) * 128], 0.0)
+            stat_ref[index * (chunk // 128) + block] = jnp.sum(line, 0, keepdims=True)
+
+    receives = list(evens)
+    for group in range(steps // 2):
+
+        @pl.loop(2 * group, 2 * group + 2)
+        def _(index):
+            project(index)
+
+            @pl.when(index > 0)
+            def _():
+                pass_on(index - 1)
+
+        if group and len(receives) > 2:
+            receive(receives.pop(0))
+    pass_on(steps - 1)
+
+    def stat_copy(stage):
+        target = (near, far)[stage]
+        return push(stat_ref, stat_slots.at[stage], stat_send.at[stage], stat_recv.at[stage], "head", target)
+
+    def head_copy(stage):
+        target = (near, far)[stage]
+        return push(
+            small_slots.at[stage, pl.ds(0, 8)],
+            small_slots.at[2 + stage, pl.ds(0, 8)],
+            small_send.at[stage],
+            small_recv.at[stage],
+            "head",
+            target,
+        )
+
+    stat_copy(0).start()
+    head_copy(0).start()
+    stat_copy(0).wait()
+    head_copy(0).wait()
+    stat_ref[...] += stat_slots[0]
+    small_slots[1] = small_slots[0]
+    small_slots[1, 0:8] += small_slots[2, 0:8]
+    stat_copy(1).start()
+    head_copy(1).start()
+    while len(receives) > 1:
+        receive(receives.pop(0))
+    stat_copy(1).wait()
+    head_copy(1).wait()
+    stat_ref[...] += stat_slots[1]
+    small_slots[4] = small_slots[1]
+    small_slots[4, 0:8] += small_slots[3, 0:8]
+
+    bits = list(range(1, stages)) + [0]
+
+    def seq_copy(turn):
+        return push(
+            small_slots.at[4 + 2 * turn],
+            small_slots.at[5 + 2 * turn],
+            small_send.at[2 + turn],
+            small_recv.at[2 + turn],
+            "seq",
+            flip(member, 1 << bits[turn]),
+        )
+
+    def seq_add(turn):
+        seq_copy(turn).wait()
+        small_slots[6 + 2 * turn] = small_slots[4 + 2 * turn] + small_slots[5 + 2 * turn]
+
+    seq_copy(0).start()
+
+    def result(index):
+        grad = own_sum(index)
+        scale = scale_ref[at(index)]
+        unit = input_ref[at(index), cols(place)].astype(F32) * scale
+        means = []
+        for block in range(chunk // 128):
+            line = jnp.where(diagonal, stat_ref[index * (chunk // 128) + block], 0.0)
+            means.append(jnp.sum(line, axis=-1, keepdims=True))
+        mean = jnp.concatenate(means, 0) * (1.0 / width)
+        ingrad_ref[at(index)] = dmid_ref[at(index)] + scale * (grad * gain_ref[:, cols(place)] - unit * mean)
+
+    for turn in range(stages):
+        start, stop = turn * steps // stages, (turn + 1) * steps // stages
+        if stop > start:
+
+            @pl.loop(start, stop)
+            def _(index):
+                result(index)
+
+        seq_add(turn)
+        if turn + 1 < stages:
+            seq_copy(turn + 1).start()
+    receive(0)
+    piece_ref[...] = acc_ref[member]
+    sums_ref[...] = small_slots[4 + 2 * stages]
+
+    @pl.loop(0, steps)
+    def _(index):
+        finish(index)
+
+    for r in sent:
+        give(r).wait_send()
+
+
+def final_stage(first_rows, dpre, pack, inputs, scale, gain, dmid, small, members, collective):
+    tokens, width = inputs.shape
+    columns = dmid.shape[1]
+    chunk = 256
+    steps = tokens // chunk
+    stages = (members - 1).bit_length()
+    rows = width // members
+    wide = dpre.shape[1]
+    whole = pl.BlockSpec(memory_space=pltpu.VMEM)
+    return pl.pallas_call(
+        functools.partial(final_kernel, members, chunk),
+        name="final",
+        out_shape=(
+            jax.ShapeDtypeStruct((tokens, columns), F32),
+            jax.ShapeDtypeStruct((rows, wide), F32),
+            jax.ShapeDtypeStruct(small.shape, F32),
+        ),
+        in_specs=[whole] * 8,
+        out_specs=(whole,) * 3,
+        scratch_shapes=[
+            pltpu.VMEM((members, rows, wide), F32),
+            pltpu.VMEM((members, rows, wide), BF),
+            pltpu.VMEM((members - 1, rows, wide), BF),
+            pltpu.VMEM((tokens, width), BF),
+        ]
+        + head_scatter_scratch(tokens, columns, steps)
+        + [
+            pltpu.VMEM((tokens // 128, 1, 128), F32),
+            pltpu.VMEM((2, tokens // 128, 1, 128), F32),
+            pltpu.VMEM((5 + 2 * stages, *small.shape), F32),
+            pltpu.SemaphoreType.DMA((members,)),
+            pltpu.SemaphoreType.DMA((members - 1,)),
+            pltpu.SemaphoreType.DMA((2,)),
+            pltpu.SemaphoreType.DMA((2,)),
+            pltpu.SemaphoreType.DMA((2 + stages,)),
+            pltpu.SemaphoreType.DMA((2 + stages,)),
+        ],
+        compiler_params=pltpu.CompilerParams(
+            collective_id=collective, has_side_effects=True, vmem_limit_bytes=VMEM_LIMIT
+        ),
+        cost_estimate=pl.CostEstimate(flops=8 * 10**9, bytes_accessed=30 << 20, transcendentals=0),
+    )(first_rows, dpre, pack, inputs, scale, gain, dmid, small)
+
+
 def from_behind(block, axis, distance):
     devices = range(lax.axis_size(axis))
     route = [(i - distance, i) for i in devices if i - distance in devices]
@@ -851,12 +1252,20 @@
     hidden_columns = gate_weight.shape[1]
     members = lax.axis_size("seq")
     piece = width // members
-    column_start = lax.axis_index("head") * columns
     seq_place = lax.axis_index("seq")
 
     mixer_pack = gather_seq(
         jnp.concatenate(
-            [query_weight, key_weight, value_weight, beta_weight, first_gain[:, None], second_gain[:, None]], 1
+            [
+                query_weight,
+                key_weight,
+                value_weight,
+                beta_weight,
+                first_gain[:, None],
+                second_gain[:, None],
+                jnp.zeros((piece, CHUNK - heads - 2), BF),
+            ],
+            1,
         )
     )
     projection = mixer_pack[:, : 3 * columns]
@@ -892,51 +1301,40 @@
     taps = conv_weight.astype(F32).transpose(1, 0, 2).reshape(4, -1)
     qkv, inv, wu, mq, start, out0, total = mixer_forward(resets, pre, halo, taps, logits, heads)
     total_low = total.astype(BF)
-    state, others = exchange(total_low, weights[:, :columns], "seq", False, 0)
+    state, others = exchange(total_low, (weights[:, :columns],), "seq", False, 0)
     gain_head = head_gain.astype(F32)[None, :]
     delta, head_rows, states = mixer_output(state, start, mq, out0, gain_head)
 
     d_heads, update_part, middle_shard, d_middle_shard, grads, second_grad = middle_stage(
         head_rows, weights, others, block_input, cotangent, gain_two[None, :], hidden_wide, 2
     )
-    update = lax.psum_scatter(update_part, "head", scatter_dimension=1, tiled=True)
-    block_output = (middle_shard + update.astype(F32)).astype(BF)
     forward_sum = lax.psum_scatter(grads, "seq", scatter_dimension=0, tiled=True).astype(F32)
     second_part = jnp.sum(second_grad, 0)
     ddelta, gain_part, shift = mixer_back_state(d_heads, delta, gain_head, mq)
     back_part = jnp.concatenate([total_low[:, :, :CHUNK].transpose(0, 2, 1), shift.astype(BF)], 2)
-    (arrive,) = exchange(back_part, None, "seq", True, 1)
-    d_pre_own, tail, lead, taps_part, d_logits32 = mixer_backward(
-        resets, pre, halo, taps, logits, qkv, inv, wu, mq, states, ddelta, arrive
+    arrive, block_output = exchange(back_part, (update_part, middle_shard), "seq", True, 1)
+    d_pre, taps_part = mixer_backward(
+        resets, pre, halo, taps, logits, qkv, inv, wu, mq, states, ddelta, arrive, 3
     )
-    received = from_behind(lead, "seq", -1)
-    d_pre = lax.dynamic_update_slice_in_dim(d_pre_own, (tail + received).astype(BF), tokens - 8, 0)
-    d_logits = d_logits32.astype(BF)
-    mixer_grads = dot_rows(first_rows, d_pre).astype(BF)
-    mixer_sum = lax.psum_scatter(mixer_grads, "seq", scatter_dimension=0, tiled=True).astype(F32)
-    beta_part = dot_rows(first_rows, d_logits)
-    d_first_part = dot_cols(d_pre, projection) + dot_cols(d_logits, full_beta)
-    d_first = lax.psum_scatter(d_first_part.astype(BF), "head", scatter_dimension=1, tiled=True).astype(F32)
-    unit_one = inputs * scale_one
-    row_part = jnp.sum(d_first_part * gain_one * unit_one, axis=-1)
-    row_mean = lax.psum(row_part, "head") / width
-    unit_shard = lax.dynamic_slice_in_dim(unit_one, column_start, columns, 1)
-    gain_shard = lax.dynamic_slice_in_dim(gain_one, column_start, columns, 0)
-    first_shard = jnp.sum(d_first * unit_shard, 0)
-    first_part = lax.dynamic_update_slice_in_dim(jnp.zeros((width,), F32), first_shard, column_start, 0)
-    input_gradient = d_middle_shard + scale_one * (d_first * gain_shard - unit_shard * row_mean[:, None])
-
-    first_gathered = lax.psum(jnp.concatenate([first_part, jnp.sum(gain_part, 0)]), ("seq", "head"))
-    gain_sum = first_gathered[width:]
-    small = lax.psum(jnp.concatenate([jnp.sum(taps_part, 1).reshape(-1), beta_part.reshape(-1), second_part]), "seq")
-    edge = 12 * columns
-    conv_gradient = small[:edge].reshape(4, 3, columns).transpose(1, 0, 2)
+    small = jnp.concatenate(
+        [
+            jnp.zeros((1, width), F32),
+            jnp.pad(jnp.sum(gain_part, 0, keepdims=True), ((0, 0), (0, width - CHUNK))),
+            jnp.zeros((6, width), F32),
+            jnp.sum(second_grad, 0, keepdims=True),
+            jnp.sum(taps_part, 1).reshape(-1, width),
+            jnp.zeros((7 - 12 * columns // width, width), F32),
+        ]
+    )
+    input_gradient, mixer_sum, sums = final_stage(
+        first_rows, d_pre, mixer_pack, block_input, scale_one, gain_one[None, :], d_middle_shard, small, members, 4
+    )
+    gain_sum = sums[1, :CHUNK]
+    conv_gradient = sums[9 : 9 + 12 * columns // width].reshape(4, 3, columns).transpose(1, 0, 2)
     row_start = seq_place * piece
-    beta_all = small[edge : edge + width * heads].reshape(width, heads)
-    beta_gradient = lax.dynamic_slice_in_dim(beta_all, row_start, piece, 0)
-    edge += width * heads
-    first_gradient = lax.dynamic_slice_in_dim(first_gathered, row_start, piece, 0)
-    second_gradient = lax.dynamic_slice_in_dim(small, edge + row_start, piece, 0)
+    first_gradient = lax.dynamic_slice_in_dim(sums[0], row_start, piece, 0)
+    second_gradient = lax.dynamic_slice_in_dim(sums[8], row_start, piece, 0)
+    beta_gradient = mixer_sum[:, 3 * columns : 3 * columns + heads]
     return (
         block_output,
         input_gradient,

time: 636 us -> 455 us (0.72)
  waiting for transfers between devices: 234 us -> 74.5 us
  Pallas kernels: 225 us -> 307 us
  blocking collectives: 81.5 us -> 0 us
  matrix products: 31.2 us -> 9.46 us
    reduce_scatter x3 -> x0, waiting for transfers between devices: 92.5 us -> none  [the longest x1 44.5 us: body(): lax.psum_scatter(d_first_part.astype(BF), 'head', scatter_dimension=1, ti...]
    psum x3 -> x0, blocking collectives: 81.5 us -> none  [the longest x1 42.1 us: body(): lax.psum(jnp.concatenate([first_part, jnp.sum(gain_part, 0)]), ('seq', 'h...]
    reduce_scatter x1, waiting for transfers between devices: 60.8 us -> 0.01 us  [body(): lax.psum_scatter(grads, 'seq', scatter_dimension=0, tiled=True).astype(F32)]
    pallas_call x0 -> x1, Pallas kernels: none -> 52.4 us  [final_stage(): pl.pallas_call(functools.partial(final_kernel, members, chunk), name='fin...]
    pallas_call x2, Pallas kernels: 44.1 us -> 76 us  [exchange(): pl.pallas_call(functools.partial(exchange_kernel, axis, count, window, ba...]
    dot_general x4 -> x0, matrix products: 19.3 us -> none  [the longest x2 10.9 us: dot_rows(): lax.dot_general(left, right, (((0,), (0,)), ((), ())), preferred_element_...]
  transfers between devices with their start and end apart: 8 -> 4, of which waited for: 7 -> 2; matrix products, arithmetic and copies ran while one was open for 8% -> 9% of each run, Pallas kernels for 5% -> 41%
where the time goes in v3:
time: 455 us; the launch traced here: 454 us
  Pallas kernels  307 us (67%)
  waiting for transfers between devices  74.5 us (16%)
  local copies, waits for them, and re-layouts  30.5 us (7%)
  between operations  14 us (3%)
  other arithmetic  13.6 us (3%)
  matrix products  9.46 us (2%)
  starting transfers between devices  4.98 us (1%)
    pallas_call x1, Pallas kernels, middle_stage(): pl.pallas_call(functools.partial(middle_kernel, steps, hidden), name='mid...  94.8 us
    pallas_call x2, Pallas kernels, exchange(): pl.pallas_call(functools.partial(exchange_kernel, axis, count, window, ba...  76 us
    all_gather x2, waiting for transfers between devices, gather_seq(): return lax.all_gather(block, 'seq', axis=0, tiled=True)  74.4 us
    pallas_call x1, Pallas kernels, final_stage(): pl.pallas_call(functools.partial(final_kernel, members, chunk), name='fin...  52.4 us
    pallas_call x1, Pallas kernels, mixer_backward(): pl.pallas_call(functools.partial(mixer_backward_kernel, heads), name='mix...  37.5 us
    pallas_call x1, Pallas kernels, mixer_forward(): pl.pallas_call(functools.partial(mixer_forward_kernel, heads), name='mixe...  30.6 us
    unnamed x31, local copies, waits for them, and re-layouts  11.5 us
    dot_general x3, matrix products, dot(): return jnp.dot(left, right, preferred_element_type=F32)  9.46 us
  transfers between devices with their start and end apart: 4, of which 2 were waited for; matrix products, arithmetic and copies ran while one was open for 9% of the time, Pallas kernels for 41%

profile of v3, /device:TPU:0, one launch (start us, length us, event | category | flops | bytes accessed | tf_op | source)
XLA Modules:
  0.0 454.4 jit_solution(9863224820331542859)
XLA Ops:
  9.6 1.7 concatenate.12
  11.4 1.1 copy.65
  12.5 1.1 copy.66
  13.5 1.1 copy.67
  16.3 4.9 %collective-permute-start = (bf16[16,1024]{1,0:T(8,128)(2,1)S(1)}, bf16[16,1024]{1,0:T(8,128)(2,1)S(1)}, u32[]{:S(2)}, u32[]{:S(2)}) collective-permute-start(bf16[16,1024]{1,0:T(8,128)(2,1)S(1)} %slice.59), channel_id=1, source_target_pairs={{0,4},{4,8},{8,12},{12,16},{16,20},{20,24},{24,28},{1,5},{5,9},{9,... | collective-permute-start | bytes 98312 | tf_op jit(solution)/shard_map/ppermute | solution.py:1213
  21.9 3.2 fusion
  26.4 33.9 %all-gather.3.cloned.1.call-done.pack_ref = bf16[1024,896]{1,0:T(8,128)(2,1)} async-done(((bf16[128,896]{1,0:T(8,128)(2,1)}), bf16[1024,896]{1,0:T(8,128)(2,1)}) %all-gather.3.cloned.1.call-update) | async-done | bytes 1835024 | tf_op jit(solution)/shard_map/all_gather | solution.py:1229
  60.3 2.1 convert_reduce_fusion
  62.4 2.4 fusion.11.halo_ref
  64.7 2.9 fusion.2.rows_ref
  67.7 2.3 fusion.17.logits_ref
  70.0 4.7 %convolution_convert_fusion.pre_ref = bf16[2048,768]{1,0:T(8,128)(2,1)} fusion(bf16[2048,1024]{1,0:T(8,128)(2,1)S(1)} %fusion.2.rows_ref, bf16[1024,896]{1,0:T(8,128)(2,1)S(1)} %copy-done.2), kind=kOutput, calls=%fused_computation.5 | convolution fusion | flops 3222798336 | bytes 8912896 | tf_op jit(solution)/shard_map/dot_general | solution.py:1217
  74.8 30.6 %mixer_forward.1 = (bf16[2048,768]{1,0:T(8,128)(2,1)}, bf16[16,2,128,128]{3,2,1,0:T(8,128)(2,1)}, bf16[16,2,128,256]{3,2,1,0:T(8,128)(2,1)}, bf16[16,2,256,128]{...) custom-call(f32[32]{0:T(128)} %convert_element_type.70.resets_ref, ...), custom_call_target="tpu_custom_call" | custom-call | flops 3000000000 | bytes 20971520 | tf_op jit(solution)/shard_map/mixer_forward/pallas_call | solution.py:186
  105.4 1.1 copy.64
  107.2 40.5 %all-gather.5.cloned.1.call-done.weights_ref = bf16[1024,2560]{1,0:T(8,128)(2,1)} async-done(((bf16[128,2560]{1,0:T(8,128)(2,1)}), bf16[1024,2560]{1,0:T(8,128)(2,1)}) %all-gather.5.cloned.1.call-update) | async-done | bytes 5242896 | tf_op jit(solution)/shard_map/all_gather | solution.py:1229
  147.8 1.9 slice.80.refs_1_
  149.6 18.2 %state_forward.1 = (f32[2,128,128]{2,1,0:T(8,128)}, bf16[3,1024,256]{2,1,0:T(8,128)(2,1)}) custom-call(bf16[2,128,256]{2,1,0:T(8,128)(2,1)} %copy.68.refs_0_, bf16[1024,256]{1,0:T(8,128)(2,1)} %slice.80.refs_1_), custom_call_target="tpu_custom_call" | custom-call | flops 1000000000 | bytes 20971520 | tf_op jit(solution)/shard_map/state_forward/pallas_call | solution.py:334
  167.8 6.8 %mixer_output.1 = (f32[2048,256]{1,0:T(8,128)}, bf16[2048,256]{1,0:T(8,128)(2,1)}, bf16[16,2,128,128]{3,2,1,0:T(8,128)(2,1)}) custom-call(f32[2,128,128]{2,1,0:T(8,128)} %get-tuple-element.43.state_ref, bf16[16,2,128,256]{3,2,1,0:T(8,128)(2,1)} %get-tuple-element.44.start_ref, bf16[16,2,256,128]{3,2,1,0:T(8,128)(2,1)} %get-tuple-element.45.mq_ref, ...), custom_call_target="tpu_custom_call" | custom-call | flops 300000000 | bytes 10485760 | tf_op jit(solution)/shard_map/mixer_output/pallas_call | solution.py:373
  174.6 94.8 %middle.1 = (bf16[2048,256]{1,0:T(8,128)(2,1)}, bf16[2048,1024]{1,0:T(8,128)(2,1)}, f32[2048,256]{1,0:T(8,128)}, f32[2048,256]{1,0:T(8,128)}, bf16[1024,2560]{1,0:T(8,128)(2,1)}, /*index=5*/f32[8,1024]{1,0:T(8,128)}) custom-call(bf16[2048,256]{1,0:T(8,128)(2,1)} %get-tuple-element.47.rows_ref, bf16[1024,2560]{1,0:T(8,128)(2,1)} %all-gather.5.cloned.1.call-done.weights_ref, ...), custom_call_target="tpu_custom_call" | custom-call | flops 30000001024 | bytes 31457280 | tf_op jit(solution)/shard_map/middle/pallas_call | solution.py:837
  269.5 1.3 copy.70.scale_ref
  270.8 9.4 %mixer_back_state.1 = (bf16[2048,256]{1,0:T(8,128)(2,1)}, f32[8,128]{1,0:T(8,128)}, f32[2,128,128]{2,1,0:T(8,128)}) custom-call(bf16[2048,256]{1,0:T(8,128)(2,1)} %get-tuple-element.49.dheads_ref, f32[2048,256]{1,0:T(8,128)} %get-tuple-element.50.delta_ref, f32[1,128]{1,0:T(1,128)} %bitcast_convert_fusion.gain_ref, ...), custom_call_target="tpu_custom_call" | custom-call | flops 300000000 | bytes 10485760 | tf_op jit(solution)/shard_map/mixer_back_state/pallas_call | solution.py:414
  281.8 57.7 %state_backward.1 = (f32[2,128,128]{2,1,0:T(8,128)}, bf16[2048,256]{1,0:T(8,128)(2,1)}) custom-call(bf16[2,128,256]{2,1,0:T(8,128)(2,1)} %pad_maximum_fusion.refs_0_, bf16[2048,1024]{1,0:T(8,128)(2,1)} %get-tuple-element.52.refs_1_, f32[2048,256]{1,0:T(8,128)} %get-tuple-element.53.refs_2_), custom_call_target="tpu_custom_call" | custom-call | flops 1000000000 | bytes 20971520 | tf_op jit(solution)/shard_map/state_backward/pallas_call | solution.py:334
  339.6 37.5 %mixer_backward.1 = (bf16[2048,896]{1,0:T(8,128)(2,1)}, f32[4,8,768]{2,1,0:T(8,128)}) custom-call(f32[32]{0:T(128)} %convert_element_type.70.resets_ref, bf16[2048,768]{1,0:T(8,128)(2,1)} %convolution_convert_fusion.pre_ref, bf16[16,768]{1,0:T(8,128)(2,1)} %fusion.11.halo_ref, f32[4,768]{1,0:T(4,128)} %bitcast.27, f32[2048,2]{1,0:T(8,128)} %fusion.17.logits_ref, ...), custom_call_target="tpu_custom_call" | custom-call | flops 3000000000 | bytes 20971520 | tf_op jit(solution)/shard_map/mixer_backward/pallas_call | solution.py:585
  377.0 0.9 reduce_sum.59
  378.1 1.3 concatenate.15.small_ref
  379.4 52.4 %final.1 = (f32[2048,256]{1,0:T(8,128)}, f32[128,896]{1,0:T(8,128)}, f32[16,1024]{1,0:T(8,128)}) custom-call(bf16[2048,1024]{1,0:T(8,128)(2,1)} %copy-done, bf16[2048,896]{1,0:T(8,128)(2,1)} %get-tuple-element.61.dpre_ref, bf16[1024,896]{1,0:T(8,128)(2,1)} %all-gather.3.cloned.1.call-done.pack_ref, bf16[2048,1024]{1,0:T(8,128)(2,1)} %input_ref.3, ...), custom_call_target="tpu_custom_call" | custom-call | flops 8000000000 | bytes 31457280 | tf_op jit(solution)/shard_map/final/pallas_call | solution.py:1175
  435.9 1.2 slice_bitcast_fusion.1
  437.1 1.8 fusion.26
  438.9 1.2 fusion.25
  442.8 1.5 slice.82
  444.3 2.3 copy.79
  446.6 1.3 copy.80
  (65 shorter events, 15.5 us)
Async XLA Ops:
  7.2 7.4 %copy-start.3 = (bf16[128,256]{1,0:T(8,128)(2,1)S(1)}, bf16[128,256]{1,0:T(8,128)(2,1)}, u32[]{:S(2)}) copy-start(bf16[128,256]{1,0:T(8,128)(2,1)} %param.23) | copy-start | bytes 196612
  7.2 14.0 %copy-start.8 = (s32[4]{0:T(128)S(1)}, s32[4]{0:T(128)}, u32[]{:S(2)}) copy-start(s32[4]{0:T(128)} %param.28) | copy-start | bytes 52
  7.2 14.2 %copy-start.9 = (bf16[128]{0:T(256)(128)(2,1)S(1)}, bf16[128]{0:T(256)(128)(2,1)}, u32[]{:S(2)}) copy-start(bf16[128]{0:T(256)(128)(2,1)} %param.22) | copy-start | bytes 772
  7.2 53.1 %all-gather.3.cloned.1.call-start = ((), (), s32[]{:S(2)}) async-start(), calls=%async_computation.1 | async-start | bytes 2064384 | tf_op jit(solution)/shard_map/all_gather | solution.py:1229
  11.3 136.4 %all-gather.5.cloned.1.call-start = ((), (), s32[]{:S(2)}) async-start(), calls=%async_computation.2 | async-start | bytes 5898240 | tf_op jit(solution)/shard_map/all_gather | solution.py:1229
  15.5 423.4 %reduce-scatter.2.cloned.1.call-start = ((), (), s32[]{:S(2)}) async-start(), calls=%async_computation.3 | async-start | bytes 5898240 | tf_op jit(solution)/shard_map/reduce_scatter | solution.py:1311
  16.3 9.9 %collective-permute-start = (bf16[16,1024]{1,0:T(8,128)(2,1)S(1)}, bf16[16,1024]{1,0:T(8,128)(2,1)S(1)}, u32[]{:S(2)}, u32[]{:S(2)}) collective-permute-start(bf16[16,1024]{1,0:T(8,128)(2,1)S(1)} %slice.59), channel_id=1, source_target_pairs={{0,4},{4,8},{8,12},{12,16},{16,20},{20,24},{24,28},{1,5},{5,9},{9,... | collective-permute-start | bytes 98312 | tf_op jit(solution)/shard_map/ppermute | solution.py:1213
  21.9 3.8 copy-start.6
  62.3 5.3 %copy-start.5 = (f32[1024]{0:T(1024)}, f32[1024]{0:T(1024)S(1)}, u32[]{:S(2)}) copy-start(f32[1024]{0:T(1024)S(1)} %get-tuple-element.113) | copy-start | bytes 12292
  64.7 2.9 copy-start.2
  67.7 2.4 copy-start
  339.6 38.4 %copy-start.7 = (f32[8,128]{1,0:T(8,128)S(1)}, f32[8,128]{1,0:T(8,128)}, u32[]{:S(2)}) copy-start(f32[8,128]{1,0:T(8,128)} %get-tuple-element.63) | copy-start | bytes 12292
  339.6 38.5 %copy-start.4 = (f32[8,1024]{1,0:T(8,128)S(1)}, f32[8,1024]{1,0:T(8,128)}, u32[]{:S(2)}) copy-start(f32[8,1024]{1,0:T(8,128)} %get-tuple-element.64) | copy-start | bytes 98308
  441.0 5.6 %copy-start.1 = (f32[2048,256]{1,0:T(8,128)S(1)}, f32[2048,256]{1,0:T(8,128)}, u32[]{:S(2)}) copy-start(f32[2048,256]{1,0:T(8,128)} %get-tuple-element.139) | copy-start | bytes 6291460
Sparse Core Ops, SparseCore 0:
  11.5 48.7 all-gather.2
  62.5 85.2 all-gather.4
  269.6 127.2 reduce-scatter.1

commit v4 on v3

v4 whole, which is shorter than its diff:
```python
import functools

import jax
import jax.numpy as jnp
from jax import lax
from jax.experimental import pallas as pl
from jax.experimental.pallas import tpu as pltpu
from jax.sharding import PartitionSpec as P

GROUP = 64
CHUNK = 128
MESH = pl.DeviceIdType.MESH
BF = jnp.bfloat16
F32 = jnp.float32
VMEM_LIMIT = 56 << 20


def nn(left, right):
    return jnp.dot(left.astype(BF), right.astype(BF), preferred_element_type=F32)


def tn(left, right):
    return lax.dot_general(
        left.astype(BF), right.astype(BF), (((0,), (0,)), ((), ())), preferred_element_type=F32
    )


def nt(left, right):
    return lax.dot_general(
        left.astype(BF), right.astype(BF), (((1,), (1,)), ((), ())), preferred_element_type=F32
    )


def sigmoid(v):
    return 0.5 * jnp.tanh(0.5 * v) + 0.5


def side(left, right):
    return jnp.concatenate([left, right], 1)


def stack(top, bottom):
    return jnp.concatenate([top, bottom], 0)


def grid_indices():
    rows = lax.broadcasted_iota(jnp.int32, (CHUNK, CHUNK), 0)
    cols = lax.broadcasted_iota(jnp.int32, (CHUNK, CHUNK), 1)
    return rows, cols


def load_padded(pad_ref, pre_ref, halo_ref, chunk, resets_ref):
    start = pl.multiple_of(chunk * CHUNK, CHUNK)
    before = pl.multiple_of(jnp.maximum(start - 16, 0), 16)
    own = pre_ref[pl.ds(start, CHUNK), :].astype(F32)
    earlier = pre_ref[pl.ds(before, 16), :].astype(F32)[8:]
    halo = halo_ref[...].astype(F32)[8:]
    first = jnp.where(chunk == 0, halo, earlier)
    keep0 = 1.0 - resets_ref[2 * chunk]
    keep1 = 1.0 - resets_ref[2 * chunk + 1]
    pad_ref[0:8] = first * keep0
    pad_ref[8:72] = own[:GROUP]
    pad_ref[72:80] = own[GROUP - 8 : GROUP] * keep1
    pad_ref[80:144] = own[GROUP:]


def tap_rows(pad_ref, tap):
    return stack(pad_ref[5 + tap : 69 + tap], pad_ref[77 + tap : 141 + tap])


def convolve(pad_ref, taps_ref):
    mixed = None
    for tap in range(4):
        term = taps_ref[tap : tap + 1] * tap_rows(pad_ref, tap)
        mixed = term if mixed is None else mixed + term
    return mixed


def inverse_levels(strict, rows, cols, keep1):
    eye = jnp.where(rows == cols, 1.0, 0.0)
    pair = (rows // 2) == (cols // 2)
    results = [eye - jnp.where(pair, a, 0.0) for a in strict]
    width = 2
    while width < CHUNK:
        off = ((rows // (2 * width)) == (cols // (2 * width))) & ((rows // width) != (cols // width))
        lows = [r.astype(BF) for r in results]
        parts = [jnp.where(off, a, 0.0).astype(BF) for a in strict]
        if width == GROUP:
            parts = [jnp.where(off, a * k, 0.0).astype(BF) for a, k in zip(strict, keep1)]
        steps = [nn(r, p) for r, p in zip(lows, parts)]
        results = [r - nn(s, low) for r, s, low in zip(results, steps, lows)]
        width *= 2
    return results


def exchange_kernel(axis, count, window, backward, *refs):
    if backward:
        (
            part_ref, update_ref, mid_ref, grads_ref, state_ref, block_ref, total_ref, slots_ref, send_sem, recv_sem,
            near_ref, relay_ref, far_ref, *sems, piece_relay, piece_slots, piece_send, piece_recv,
        ) = refs
        begin, receive, jobs, end = piece_scatter(
            grads_ref, piece_relay, piece_slots, total_ref, piece_send, piece_recv, count
        )
        _, _, near, far = head_peers()
        chunk = 256
        steps = update_ref.shape[0] // chunk
        at, _, start_pair, pass_on, own_sum, finish = head_scatter_copies(
            chunk, update_ref, near_ref, relay_ref, far_ref, sems
        )
    else:
        part_ref, state_ref, slots_ref, send_sem, recv_sem = refs
    place = lax.axis_index(axis)
    ahead = count - 1 - place if backward else place
    behind = count - 1 - ahead
    sign = -1 if backward else 1
    barrier = pltpu.get_barrier_semaphore()
    for hop in range(1, window + 1):

        @pl.when(ahead >= hop)
        def _():
            pl.semaphore_signal(
                barrier, inc=1, device_id={axis: place - sign * hop}, device_id_type=MESH
            )

    extra = 0
    if backward:
        extra = 2 + greet_seq(count)[1]
        for target in (near, far):
            pl.semaphore_signal(barrier, inc=1, device_id={"head": target}, device_id_type=MESH)

    if extra:
        pl.semaphore_wait(barrier, jnp.minimum(behind, window) + extra)
    else:

        @pl.when(behind > 0)
        def _():
            pl.semaphore_wait(barrier, jnp.minimum(behind, window))

    def copy(hop):
        return push(
            part_ref,
            slots_ref.at[hop - 1],
            send_sem.at[hop - 1],
            recv_sem.at[hop - 1],
            axis,
            place + sign * hop,
        )

    for hop in range(1, window + 1):

        @pl.when(behind >= hop)
        def _():
            copy(hop).start()

    if backward:

        @pl.loop(0, steps)
        def _(index):
            start_pair(index)

        begin()

        @pl.loop(0, steps)
        def _(index):
            pass_on(index)

        for job in jobs[: len(jobs) // 2]:
            receive(*job)

    heads = state_ref.shape[0]
    state_ref[...] = jnp.zeros_like(state_ref)
    for hop in range(window, 0, -1):

        @pl.when(ahead >= hop)
        def _():
            copy(hop).wait_recv()
            for head in range(heads):
                part = slots_ref[hop - 1, head]
                state_ref[head] = nn(part[:, :CHUNK], state_ref[head]) + part[:, CHUNK:].astype(F32)

    if backward:
        for job in jobs[len(jobs) // 2 :]:
            receive(*job)

        @pl.loop(0, steps)
        def _(index):
            block_ref[at(index)] = (mid_ref[at(index)] + own_sum(index)).astype(BF)
            finish(index)

        end()

    for hop in range(1, window + 1):

        @pl.when(behind >= hop)
        def _():
            copy(hop).wait_send()


def exchange(part, extras, axis, backward, collective):
    count = lax.axis_size(axis)
    window = min(count - 1, count // 2)
    heads = part.shape[0]
    whole = pl.BlockSpec(memory_space=pltpu.VMEM)
    out_shape = [jax.ShapeDtypeStruct((heads, CHUNK, CHUNK), F32)]
    scratch = [
        pltpu.VMEM((window, heads, CHUNK, 2 * CHUNK), BF),
        pltpu.SemaphoreType.DMA((window,)),
        pltpu.SemaphoreType.DMA((window,)),
    ]
    if backward:
        tokens, columns = extras[1].shape
        out_shape.append(jax.ShapeDtypeStruct((tokens, columns), BF))
        scratch += head_scatter_scratch(tokens, columns, tokens // 256)
        parts, _, *piece = extras[2].shape
        out_shape.append(jax.ShapeDtypeStruct((parts, *piece), F32))
        scratch += piece_scatter_scratch(parts, count, piece)
    return pl.pallas_call(
        functools.partial(exchange_kernel, axis, count, window, backward),
        name="state_backward" if backward else "state_forward",
        out_shape=out_shape,
        in_specs=[whole] * (1 + len(extras)),
        out_specs=[whole] * len(out_shape),
        scratch_shapes=scratch,
        compiler_params=pltpu.CompilerParams(
            collective_id=collective, has_side_effects=True, vmem_limit_bytes=VMEM_LIMIT
        ),
        cost_estimate=pl.CostEstimate(flops=10**9, bytes_accessed=20 << 20, transcendentals=0),
    )(part, *extras)


def mixer_output_kernel(heads, state_ref, start_ref, mq_ref, out0_ref, gain_ref, delta_ref, rows_ref, states_ref):
    batch = 4

    def one(step, carry):
        for lane in range(batch):
            chunk = step * batch + lane
            at = pl.ds(pl.multiple_of(chunk * CHUNK, CHUNK), CHUNK)
            for head in range(heads):
                window = slice(head * CHUNK, (head + 1) * CHUNK)
                begin = start_ref[chunk, head]
                state = nn(begin[:, :CHUNK], state_ref[head]) + begin[:, CHUNK:].astype(F32)
                state = state.astype(BF)
                states_ref[chunk, head] = state
                out = out0_ref[chunk, head] + nn(mq_ref[chunk, head, CHUNK:], state)
                delta_ref[at, window] = out
                scale = lax.rsqrt(jnp.mean(out * out, axis=-1, keepdims=True) + 1e-05)
                rows_ref[at, window] = (out * scale * gain_ref[...]).astype(BF)
        return carry

    lax.fori_loop(0, start_ref.shape[0] // batch, one, 0)


def mixer_output(state, start, mq, out0, gain):
    chunks, heads = start.shape[:2]
    tokens = chunks * CHUNK
    return pl.pallas_call(
        functools.partial(mixer_output_kernel, heads),
        name="mixer_output",
        out_shape=(
            jax.ShapeDtypeStruct((tokens, heads * CHUNK), F32),
            jax.ShapeDtypeStruct((tokens, heads * CHUNK), BF),
            jax.ShapeDtypeStruct((chunks, heads, CHUNK, CHUNK), BF),
        ),
        compiler_params=pltpu.CompilerParams(vmem_limit_bytes=VMEM_LIMIT),
        cost_estimate=pl.CostEstimate(flops=3 * 10**8, bytes_accessed=10 << 20, transcendentals=1 << 14),
    )(state, start, mq, out0, gain)


def mixer_back_state_kernel(heads, dheads_ref, delta_ref, gain_ref, mq_ref, ddelta_ref, gain_grad_ref, shift_ref):
    chunks = mq_ref.shape[0]
    shift_ref[...] = jnp.zeros_like(shift_ref)
    gain_grad_ref[...] = jnp.zeros_like(gain_grad_ref)

    def one(step, carry):
        chunk = chunks - 1 - step
        at = pl.ds(pl.multiple_of(chunk * CHUNK, CHUNK), CHUNK)
        for head in range(heads):
            window = slice(head * CHUNK, (head + 1) * CHUNK)
            out = delta_ref[at, window]
            grad = dheads_ref[at, window].astype(F32)
            scale = lax.rsqrt(jnp.mean(out * out, axis=-1, keepdims=True) + 1e-05)
            unit = out * scale
            gain_grad_ref[...] += jnp.sum((grad * unit).reshape(CHUNK // 8, 8, CHUNK), 0)
            scaled = grad * gain_ref[...]
            back = scale * (scaled - unit * jnp.mean(scaled * unit, axis=-1, keepdims=True))
            back = back.astype(BF)
            ddelta_ref[at, window] = back
            shift_ref[head] = tn(mq_ref[chunk, head], stack(shift_ref[head].astype(BF), back))
        return carry

    lax.fori_loop(0, chunks, one, 0)


def mixer_back_state(dheads, delta, gain, mq):
    chunks, heads = mq.shape[:2]
    tokens = chunks * CHUNK
    return pl.pallas_call(
        functools.partial(mixer_back_state_kernel, heads),
        name="mixer_back_state",
        out_shape=(
            jax.ShapeDtypeStruct((tokens, heads * CHUNK), BF),
            jax.ShapeDtypeStruct((8, CHUNK), F32),
            jax.ShapeDtypeStruct((heads, CHUNK, CHUNK), F32),
        ),
        compiler_params=pltpu.CompilerParams(vmem_limit_bytes=VMEM_LIMIT),
        cost_estimate=pl.CostEstimate(flops=3 * 10**8, bytes_accessed=10 << 20, transcendentals=1 << 14),
    )(dheads, delta, gain, mq)


def piece_scatter_scratch(parts, members, piece):
    return [
        pltpu.VMEM((parts, max(members // 2 - 1, 1), *piece), BF),
        pltpu.VMEM((parts, members - 1, *piece), BF),
        pltpu.SemaphoreType.DMA((parts, members)),
        pltpu.SemaphoreType.DMA((parts, members)),
    ]


def piece_scatter(own_ref, relay_ref, slots_ref, total_ref, send, recv, members):
    member = lax.axis_index("seq")
    parts = own_ref.shape[0]
    stages = (members - 1).bit_length()
    order = sorted(range(members), key=lambda r: zeros_below(r) if r else stages)
    levels = {r: list(range(zeros_below(r) if r else stages)) for r in order}
    events = {}
    for r in order:
        for stage in levels[r]:
            events[r, stage] = len(events)
    kept = [r for r in order if r and r % 2 == 0]

    def source(part, r):
        return own_ref.at[part, flip(member, r)] if r % 2 else relay_ref.at[part, kept.index(r)]

    def give(part, r):
        stage = zeros_below(r)
        slot = events[r ^ (1 << stage), stage]
        return push(
            source(part, r), slots_ref.at[part, slot], send.at[part, r], recv.at[part, slot], "seq", flip(member, 1 << stage)
        )

    def take(part, r, stage):
        slot = events[r, stage]
        return push(
            own_ref.at[part, flip(member, 1)], slots_ref.at[part, slot], send.at[part, 0], recv.at[part, slot], "seq", flip(member, 1 << stage)
        )

    jobs = [(part, r) for r in order if r % 2 == 0 for part in range(parts)]

    def begin():
        for part, r in jobs:
            give(part, r ^ 1).start()

    def receive(part, r):
        total = own_ref[part, flip(member, r)].astype(F32)
        for stage in levels[r]:
            take(part, r, stage).wait_recv()
            total = total + slots_ref[part, events[r, stage]].astype(F32)
        if r:
            relay_ref[part, kept.index(r)] = total.astype(BF)
            give(part, r).start()
        else:
            total_ref[part] = total

    def finish():
        for part in range(parts):
            for r in order:
                if r:
                    give(part, r).wait_send()

    return begin, receive, jobs, finish


def mixer_backward_kernel(
    heads,
    resets_ref,
    pre_ref,
    halo_ref,
    taps_ref,
    logits_ref,
    qkv_ref,
    inv_ref,
    wu_ref,
    mq_ref,
    states_ref,
    ddelta_ref,
    arrive_ref,
    grads_ref,
    dpre_ref,
    taps_grad_ref,
    total_ref,
    carry_ref,
    pad_ref,
    dpad_ref,
    tail_ref,
    lead_ref,
    edge_ref,
    send_sem,
    recv_sem,
    relay_ref,
    slots_ref,
    piece_send,
    piece_recv,
):
    member, members = lax.axis_index("seq"), lax.axis_size("seq")
    barrier, stages = greet_seq(members)
    begin, receive, order, finish = piece_scatter(
        grads_ref, relay_ref, slots_ref, total_ref, piece_send, piece_recv, members
    )

    @pl.when(member + 1 < members)
    def _():
        pl.semaphore_signal(barrier, inc=1, device_id={"seq": member + 1}, device_id_type=MESH)

    columns = heads * CHUNK
    chunks = mq_ref.shape[0]
    rows, cols = grid_indices()
    top = lax.broadcasted_iota(jnp.int32, (CHUNK, 1), 0) < GROUP
    pl.semaphore_wait(barrier, stages + jnp.minimum(member, 1))
    begin()
    carry_ref[...] = arrive_ref[...]
    taps_grad_ref[...] = jnp.zeros_like(taps_grad_ref)
    dpad_ref[136:144] = jnp.zeros_like(dpad_ref[136:144])

    def one(step, carry):
        chunk = chunks - 1 - step
        at = pl.ds(pl.multiple_of(chunk * CHUNK, CHUNK), CHUNK)
        keep0 = 1.0 - resets_ref[2 * chunk]
        keep1 = 1.0 - resets_ref[2 * chunk + 1]
        both = keep0 * keep1
        enter = jnp.where(top, keep0, both)
        leave = jnp.where(top, keep1, 1.0)
        load_padded(pad_ref, pre_ref, halo_ref, chunk, resets_ref)
        mixed = convolve(pad_ref, taps_ref)
        gate = sigmoid(mixed)
        slope = gate * (1.0 + mixed * (1.0 - gate))
        silued = mixed * gate
        beta_rows = sigmoid(logits_ref[at, :])
        grads = [[None] * heads for _ in range(3)]
        dlogits = []
        cross = (rows >= GROUP) & (cols < GROUP)

        def part(kind, head):
            return slice(kind * columns + head * CHUNK, kind * columns + (head + 1) * CHUNK)

        def masked(product, keep):
            lower = jnp.where(keep, product, 0.0)
            return jnp.where(cross, lower * keep1, lower).astype(BF)

        every = range(heads)
        query = [qkv_ref[at, part(0, h)] for h in every]
        key = [qkv_ref[at, part(1, h)] for h in every]
        value = [qkv_ref[at, part(2, h)] for h in every]
        key32 = [k.astype(F32) for k in key]
        beta = [beta_rows[:, h : h + 1] for h in every]
        inverse = [inv_ref[chunk, h] for h in every]
        weight = [wu_ref[chunk, h, :, :CHUNK] for h in every]
        factors = [wu_ref[chunk, h] for h in every]
        update = [wu_ref[chunk, h, :, CHUNK:] for h in every]
        state = [states_ref[chunk, h] for h in every]
        out_grad = [ddelta_ref[at, h * CHUNK : (h + 1) * CHUNK] for h in every]
        later = [carry_ref[h].astype(BF) for h in every]
        carried = [tn(mq_ref[chunk, h], stack(later[h], out_grad[h])) for h in every]
        scores = [masked(nt(query[h], key[h]), rows >= cols) for h in every]
        fresh = [(update[h].astype(F32) - nn(weight[h], state[h])).astype(BF) for h in every]
        fresh_low = [(tn(scores[h], out_grad[h]) + leave * nn(key[h], later[h])).astype(BF) for h in every]
        score_grad = [masked(nt(out_grad[h], fresh[h]), rows >= cols) for h in every]
        through = [nt(stack(out_grad[h], fresh_low[h]), state[h]) for h in every]
        weight_grad = [(-enter * through[h][CHUNK:]).astype(BF) for h in every]
        back = [tn(inverse[h], side(weight_grad[h], fresh_low[h])) for h in every]
        query_grad = [enter * through[h][:CHUNK] + nn(score_grad[h], key[h]) for h in every]
        key_grad = [tn(score_grad[h], query[h]) + leave * nt(fresh[h], later[h]) for h in every]
        strict = [masked(-nt(back[h].astype(BF), factors[h]), rows > cols) for h in every]
        strict_key = [nn(strict[h], key[h]) for h in every]
        turned = [tn(strict[h], (beta[h] * key32[h]).astype(BF)) for h in every]
        for h in every:
            carry_ref[h] = carried[h]
            yk, zv = back[h][:, :CHUNK], back[h][:, CHUNK:]
            both_key = yk + strict_key[h]
            key_grad[h] = key_grad[h] + beta[h] * both_key + turned[h]
            grads[2][h] = beta[h] * zv
            beta_grad = jnp.sum(both_key * key32[h] + zv * value[h].astype(F32), axis=-1, keepdims=True)
            dlogits.append(beta_grad * beta[h] * (1.0 - beta[h]))
        for kind, grad in ((0, query_grad), (1, key_grad)):
            raw = [silued[:, part(kind, h)] for h in every]
            norm = [lax.rsqrt(jnp.sum(raw[h] * raw[h], axis=-1, keepdims=True) + 1e-06) for h in every]
            unit = [raw[h] * norm[h] for h in every]
            inner = [jnp.sum(unit[h] * grad[h], axis=-1, keepdims=True) for h in every]
            grads[kind] = [(grad[h] - unit[h] * inner[h]) * norm[h] for h in every]
        lanes = lax.broadcasted_iota(jnp.int32, (CHUNK, CHUNK), 1)
        spread = jnp.zeros((CHUNK, CHUNK), F32)
        for head in range(heads):
            spread = jnp.where(lanes == head, dlogits[head], spread)
        dpre_ref[at, 3 * columns :] = spread.astype(BF)
        dmixed = jnp.concatenate([g for kind in grads for g in kind], 1) * slope
        dpad_ref[0:GROUP] = dmixed[:GROUP]
        dpad_ref[GROUP : GROUP + 8] = dmixed[GROUP : GROUP + 8] * keep1
        dpad_ref[72 : 72 + GROUP] = dmixed[GROUP:]
        dpre = None
        for tap in range(4):
            back = 3 - tap
            shifted = stack(dpad_ref[back : back + GROUP], dpad_ref[72 + back : 72 + back + GROUP])
            term = taps_ref[tap : tap + 1] * shifted
            dpre = term if dpre is None else dpre + term
            seen = (dmixed * tap_rows(pad_ref, tap)).reshape(CHUNK // 8, 8, 3 * columns)
            taps_grad_ref[tap] += jnp.sum(seen, 0)
        dpre_ref[at, : 3 * columns] = dpre.astype(BF)

        @pl.when(step == 0)
        def _():
            tail_ref[...] = dpre[CHUNK - 16 :]

        dpad_ref[136:144] = dmixed[:8] * keep0
        for place, job in enumerate(order):

            @pl.when(step == (place + 1) * (chunks - 1) // len(order))
            def _():
                receive(*job)

        return carry

    lax.fori_loop(0, chunks, one, 0)
    index = lax.broadcasted_iota(jnp.int32, (8, 1), 0)
    lead = jnp.zeros((8, 3 * columns), F32)
    dpad_ref[0:128] = jnp.zeros_like(dpad_ref[0:128])
    dpad_ref[8:16] = dpad_ref[136:144]
    for tap in range(3):
        back = 3 - tap
        lead = lead + taps_ref[tap : tap + 1] * dpad_ref[back : back + 8]
    lead_ref[...] = lead

    def to_previous(target):
        return push(lead_ref, edge_ref, send_sem, recv_sem, "seq", target)

    @pl.when(member > 0)
    def _():
        to_previous(member - 1).start()

    @pl.when(member + 1 < members)
    def _():
        to_previous(member).wait_recv()
        last = pl.ds(dpre_ref.shape[0] - 16, 16)
        late = stack(tail_ref[0:8], tail_ref[8:16] + edge_ref[...])
        dpre_ref[last, : 3 * columns] = late.astype(BF)

    @pl.when(member > 0)
    def _():
        to_previous(member - 1).wait_send()

    finish()


def mixer_backward(resets, pre, halo, taps, logits, qkv, inv, wu, mq, states, ddelta, arrive, grads, collective):
    chunks, heads = mq.shape[:2]
    tokens = chunks * CHUNK
    columns = heads * CHUNK
    parts, members = grads.shape[:2]
    piece = grads.shape[2:]
    return pl.pallas_call(
        functools.partial(mixer_backward_kernel, heads),
        name="mixer_backward",
        out_shape=(
            jax.ShapeDtypeStruct((tokens, 3 * columns + CHUNK), BF),
            jax.ShapeDtypeStruct((4, 8, 3 * columns), F32),
            jax.ShapeDtypeStruct((parts, *piece), F32),
        ),
        in_specs=[pl.BlockSpec(memory_space=pltpu.SMEM)] + [pl.BlockSpec(memory_space=pltpu.VMEM)] * 12,
        out_specs=tuple([pl.BlockSpec(memory_space=pltpu.VMEM)] * 3),
        scratch_shapes=[
            pltpu.VMEM((heads, CHUNK, CHUNK), F32),
            pltpu.VMEM((144, 3 * columns), F32),
            pltpu.VMEM((144, 3 * columns), F32),
            pltpu.VMEM((16, 3 * columns), F32),
            pltpu.VMEM((8, 3 * columns), F32),
            pltpu.VMEM((8, 3 * columns), F32),
            pltpu.SemaphoreType.DMA,
            pltpu.SemaphoreType.DMA,
        ]
        + piece_scatter_scratch(parts, members, piece),
        compiler_params=pltpu.CompilerParams(
            collective_id=collective, has_side_effects=True, vmem_limit_bytes=VMEM_LIMIT
        ),
        cost_estimate=pl.CostEstimate(flops=3 * 10**9, bytes_accessed=20 << 20, transcendentals=2 << 20),
    )(resets, pre, halo, taps, logits, qkv, inv, wu, mq, states, ddelta, arrive, grads)


def head_peers():
    place = lax.axis_index("head")
    low = lax.rem(place, 2)
    high = lax.rem(lax.div(place, 2), 2)
    return place, low, place + 1 - 2 * low, place + 2 - 4 * high


def push(src, dst, send_sem, recv_sem, axis, target):
    return pltpu.make_async_remote_copy(
        src_ref=src,
        dst_ref=dst,
        send_sem=send_sem,
        recv_sem=recv_sem,
        device_id={axis: target},
        device_id_type=MESH,
    )


def greet(axis, targets):
    barrier = pltpu.get_barrier_semaphore()
    for target in targets:
        pl.semaphore_signal(barrier, inc=1, device_id={axis: target}, device_id_type=MESH)
    pl.semaphore_wait(barrier, len(targets))


def middle_kernel(
    steps,
    rows_ref,
    full_hbm,
    turned_hbm,
    others_hbm,
    input_ref,
    ct_ref,
    late_ct_ref,
    gain_ref,
    dheads_ref,
    update_ref,
    mid_ref,
    dmid_ref,
    first_grads_ref,
    second_grads_ref,
    third_grads_ref,
    gain_grad_ref,
    gate_ref,
    up_ref,
    down_ref,
    turned_ref,
    others_ref,
    load_sem,
    full_ref,
    acc_ref,
    part_ref,
    pair_ref,
    far_ref,
    sum_ref,
    keep_ref,
    scale_ref,
    shard_ref,
    row_near_send,
    row_near_recv,
    row_far_send,
    row_far_recv,
    row_pass_send,
    row_pass_recv,
    pair_send,
    pair_recv,
    far_send,
    far_recv,
    last_send,
    last_recv,
):
    step = pl.program_id(0)
    place, low, near, far = head_peers()
    chunk, width = input_ref.shape
    columns = rows_ref.shape[1]
    hidden = gate_ref.shape[0]
    half = width // 2
    mine = pl.ds(pl.multiple_of(low * half, 128), half)
    theirs = pl.ds(pl.multiple_of((1 - low) * half, 128), half)
    own_columns = pl.ds(pl.multiple_of(place * columns, 128), columns)

    def at(index):
        return pl.ds(pl.multiple_of(index * chunk, chunk), chunk)

    def near_rows(index):
        return push(
            rows_ref.at[at(index)], full_ref.at[0, at(index)], row_near_send.at[index], row_near_recv.at[index], "head", near
        )

    def far_rows(index):
        return push(
            rows_ref.at[at(index)], full_ref.at[1, at(index)], row_far_send.at[index], row_far_recv.at[index], "head", far
        )

    def pass_rows(index):
        return push(
            full_ref.at[1, at(index)], full_ref.at[2, at(index)], row_pass_send.at[index], row_pass_recv.at[index], "head", near
        )

    def pair(index):
        return push(
            part_ref.at[lax.rem(index, 2), :, theirs], pair_ref.at[index], pair_send.at[index], pair_recv.at[index], "head", near
        )

    def across(index):
        return push(pair_ref.at[index], far_ref.at[index], far_send.at[index], far_recv.at[index], "head", far)

    def last(index):
        return push(
            sum_ref.at[index, :, mine], sum_ref.at[index, :, mine], last_send.at[index], last_recv.at[index], "head", near
        )

    def loads():
        targets = [
            (full_hbm.at[0], gate_ref),
            (full_hbm.at[1], up_ref),
            (full_hbm.at[2], down_ref),
            (turned_hbm, turned_ref),
        ] + [(others_hbm.at[other], others_ref.at[other]) for other in range(3)]
        for number, (source, target) in enumerate(targets):
            for piece in range(width // 128):
                yield pltpu.make_async_copy(
                    source.at[piece], target.at[:, piece * 128 : (piece + 1) * 128], load_sem.at[number, piece]
                )

    @pl.when(step == 0)
    def _():
        for load in loads():
            load.start()
        greet("head", (near, far))

        @pl.loop(0, steps)
        def _(index):
            far_rows(index).start()
            near_rows(index).start()

        acc_ref[...] = jnp.zeros_like(acc_ref)
        gain_grad_ref[...] = jnp.zeros_like(gain_grad_ref)
        for load in loads():
            load.wait()

    @pl.when(step < steps)
    def _():
        ct = ct_ref[...]
        d_hidden = nt(ct, down_ref[...])

        @pl.when(step == 0)
        def _():
            far_rows(step).wait_recv()
            pass_rows(step).start()

        near_rows(step).wait_recv()
        pass_rows(step).wait_recv()
        branch = nn(rows_ref[at(step)], turned_ref[...])
        for other in range(3):
            branch = branch + nn(full_ref[other, at(step)], others_ref[other])
        middle = input_ref[...].astype(F32) + branch
        keep_ref[lax.rem(step, 3)] = middle
        mid_ref[...] = keep_ref[lax.rem(step, 3), :, own_columns]
        scale = lax.rsqrt(jnp.mean(middle * middle, axis=-1, keepdims=True) + 1e-06)
        scale_ref[lax.rem(step, 3)] = scale
        second = (middle * scale * gain_ref[...]).astype(BF)
        gate, up = nt(second, gate_ref[...]), nt(second, up_ref[...])
        sig = sigmoid(gate)
        silu = gate * sig
        active = (silu * up).astype(BF)
        d_gate = (d_hidden * up * (sig + silu * (1.0 - sig))).astype(BF)
        d_up = (d_hidden * silu).astype(BF)

        @pl.when(step >= 2)
        def _():
            pair(step - 2).wait_send()

        part_ref[lax.rem(step, 2)] = (nn(d_gate, gate_ref[...]) + nn(d_up, up_ref[...])).astype(BF)
        pair(step).start()

        @pl.when(step + 1 < steps)
        def _():
            far_rows(step + 1).wait_recv()
            pass_rows(step + 1).start()

        update_ref[...] = nn(active, down_ref[...]).astype(BF)
        acc_ref[:hidden] += tn(d_gate, second)
        acc_ref[hidden : 2 * hidden] += tn(d_up, second)
        acc_ref[2 * hidden : 3 * hidden] += tn(active, ct)

    @pl.when(step < steps)
    def _():
        pair(step).wait_recv()
        both = part_ref[lax.rem(step, 2), :, mine].astype(F32) + pair_ref[step].astype(F32)
        pair_ref[step] = both.astype(BF)
        across(step).start()

    @pl.when((step > 0) & (step <= steps))
    def _():
        done = step - 1
        across(done).wait_recv()
        across(done).wait_send()
        total = pair_ref[done].astype(F32) + far_ref[done].astype(F32)
        sum_ref[done, :, mine] = total.astype(BF)
        last(done).start()

    @pl.when(step > 1)
    def _():
        done = step - 2
        last(done).wait_recv()
        grad = sum_ref[done].astype(F32)
        middle = keep_ref[lax.rem(done, 3)]
        scale = scale_ref[lax.rem(done, 3)]
        unit = middle * scale
        gain_grad_ref[...] += jnp.sum((grad * unit).reshape(chunk // 8, 8, width), 0)
        scaled = grad * gain_ref[...]
        d_middle = late_ct_ref[...].astype(F32) + scale * (
            scaled - unit * jnp.mean(scaled * unit, axis=-1, keepdims=True)
        )
        shard_ref[...] = d_middle
        dmid_ref[...] = shard_ref[:, own_columns]
        d_branch = d_middle.astype(BF)
        dheads_ref[...] = nt(d_branch, turned_ref[...]).astype(BF)
        acc_ref[3 * hidden :] += tn(rows_ref[at(done)], d_branch)

    @pl.when(step == steps + 1)
    def _():
        for piece in range(width // 128):
            lanes = slice(piece * 128, (piece + 1) * 128)
            begin = 0
            for grads_ref in (first_grads_ref, second_grads_ref, third_grads_ref):
                rows = grads_ref.shape[2]
                for part in range(2):
                    grads_ref[part, piece] = acc_ref[begin : begin + rows, lanes].astype(BF)
                    begin += rows

        @pl.loop(0, steps)
        def _(index):
            near_rows(index).wait_send()
            far_rows(index).wait_send()
            pass_rows(index).wait_send()
            last(index).wait_send()

        for index in range(max(steps - 2, 0), steps):
            pair(index).wait_send()


def middle_stage(head_rows, full, turned, others, inputs, cotangent, gain, collective):
    tokens, width = inputs.shape
    columns = head_rows.shape[1]
    chunk = min(256, tokens // 2)
    steps = tokens // chunk
    whole = pl.BlockSpec(memory_space=pltpu.VMEM)
    outside = pl.BlockSpec(memory_space=pl.ANY)
    hidden = full.shape[2]
    units = (3 * hidden + columns) // 32
    shares = [16 * (units * 36 // 74), 0, 16 * (units * 25 // 74)]
    shares[1] = 16 * units - sum(shares)

    def early(wide):
        return pl.BlockSpec((chunk, wide), lambda s: (jnp.minimum(s, steps - 1), 0))

    def late(wide):
        return pl.BlockSpec((chunk, wide), lambda s: (jnp.maximum(s - 2, 0), 0))

    dma = pltpu.SemaphoreType.DMA((steps,))
    return pl.pallas_call(
        functools.partial(middle_kernel, steps),
        name="middle",
        grid=(steps + 2,),
        out_shape=(
            jax.ShapeDtypeStruct((tokens, columns), BF),
            jax.ShapeDtypeStruct((tokens, width), BF),
            jax.ShapeDtypeStruct((tokens, columns), F32),
            jax.ShapeDtypeStruct((tokens, columns), F32),
            *(jax.ShapeDtypeStruct((2, width // 128, rows, 128), BF) for rows in shares),
            jax.ShapeDtypeStruct((8, width), F32),
        ),
        in_specs=[whole] + [outside] * 3 + [early(width), early(width), late(width), whole],
        out_specs=(late(columns), early(width), early(columns), late(columns), whole, whole, whole, whole),
        scratch_shapes=[
            pltpu.VMEM((hidden, width), BF),
            pltpu.VMEM((hidden, width), BF),
            pltpu.VMEM((hidden, width), BF),
            pltpu.VMEM((columns, width), BF),
            pltpu.VMEM((3, columns, width), BF),
            pltpu.SemaphoreType.DMA((7, width // 128)),
            pltpu.VMEM((3, tokens, columns), BF),
            pltpu.VMEM((3 * hidden + columns, width), F32),
            pltpu.VMEM((2, chunk, width), BF),
            pltpu.VMEM((steps, chunk, width // 2), BF),
            pltpu.VMEM((steps, chunk, width // 2), BF),
            pltpu.VMEM((steps, chunk, width), BF),
            pltpu.VMEM((3, chunk, width), F32),
            pltpu.VMEM((3, chunk, 1), F32),
            pltpu.VMEM((chunk, width), F32),
        ]
        + [dma] * 12,
        compiler_params=pltpu.CompilerParams(
            collective_id=collective,
            has_side_effects=True,
            vmem_limit_bytes=VMEM_LIMIT,
            dimension_semantics=("arbitrary",),
        ),
        cost_estimate=pl.CostEstimate(flops=30 * 10**9, bytes_accessed=30 << 20, transcendentals=2 << 20),
    )(head_rows, full, turned, others, inputs, cotangent, cotangent, gain)


def zeros_below(value):
    return (value & -value).bit_length() - 1


def flip(place, mask):
    bit = 1
    while bit <= mask:
        if mask & bit:
            place = place + bit - 2 * bit * lax.rem(lax.div(place, bit), 2)
        bit *= 2
    return place


def head_scatter_copies(chunk, part_ref, near_ref, send_ref, far_ref, sems):
    place, low, near, far = head_peers()
    high = lax.rem(lax.div(place, 2), 2)
    columns = far_ref.shape[-1]
    near_send, near_recv, far_send, far_recv = sems

    def at(index):
        return pl.ds(pl.multiple_of(index * chunk, chunk), chunk)

    def cols(owner):
        return pl.ds(pl.multiple_of(owner * columns, 128), columns)

    def pair(index, side_):
        return push(
            part_ref.at[at(index), cols(2 * side_ + 1 - low)],
            near_ref.at[side_, at(index)],
            near_send.at[side_, index],
            near_recv.at[side_, index],
            "head",
            near,
        )

    def across(index):
        return push(send_ref.at[at(index)], far_ref.at[at(index)], far_send.at[index], far_recv.at[index], "head", far)

    def start_pair(index):
        pair(index, 0).start()
        pair(index, 1).start()

    def pass_on(index):
        pair(index, 0).wait_recv()
        pair(index, 1).wait_recv()
        total = part_ref[at(index), cols(2 * (1 - high) + low)].astype(F32) + near_ref[1 - high, at(index)].astype(F32)
        send_ref[at(index)] = total.astype(BF)
        across(index).start()

    def own_sum(index):
        across(index).wait_recv()
        near_part = part_ref[at(index), cols(place)].astype(F32) + near_ref[high, at(index)].astype(F32)
        return near_part + far_ref[at(index)].astype(F32)

    def finish(index):
        pair(index, 0).wait_send()
        pair(index, 1).wait_send()
        across(index).wait_send()

    return at, cols, start_pair, pass_on, own_sum, finish


def head_scatter_scratch(tokens, columns, steps):
    return [
        pltpu.VMEM((2, tokens, columns), BF),
        pltpu.VMEM((tokens, columns), BF),
        pltpu.VMEM((tokens, columns), BF),
        pltpu.SemaphoreType.DMA((2, steps)),
        pltpu.SemaphoreType.DMA((2, steps)),
        pltpu.SemaphoreType.DMA((steps,)),
        pltpu.SemaphoreType.DMA((steps,)),
    ]


def final_kernel(
    members,
    chunk,
    rows_ref,
    dpre_ref,
    pack_ref,
    input_ref,
    scale_ref,
    gain_ref,
    dmid_ref,
    small_ref,
    rest_ref,
    ingrad_ref,
    piece_ref,
    sums_ref,
    total_ref,
    acc_ref,
    out_ref,
    slots_ref,
    part_ref,
    near_ref,
    send_ref,
    far_ref,
    near_send,
    near_recv,
    far_send,
    far_recv,
    stat_ref,
    stat_slots,
    small_slots,
    piece_send,
    piece_recv,
    stat_send,
    stat_recv,
    small_send,
    small_recv,
    rest_relay,
    rest_slots,
    rest_send,
    rest_recv,
):
    tokens, width = input_ref.shape
    steps = tokens // chunk
    place, low, near, far = head_peers()
    member = lax.axis_index("seq")
    rows = width // members
    stages = (members - 1).bit_length()
    at, cols, start_pair, pass_on, own_sum, finish = head_scatter_copies(
        chunk, part_ref, near_ref, send_ref, far_ref, (near_send, near_recv, far_send, far_recv)
    )

    barrier = pltpu.get_barrier_semaphore()
    opposite = near + far - place
    for target in (near, far, opposite):
        pl.semaphore_signal(barrier, inc=1, device_id={"head": target}, device_id_type=MESH)
    for stage in range(stages):
        pl.semaphore_signal(barrier, inc=1, device_id={"seq": flip(member, 1 << stage)}, device_id_type=MESH)
    begin, rest_receive, rest_jobs, rest_end = piece_scatter(
        rest_ref, rest_relay, rest_slots, total_ref, rest_send, rest_recv, members
    )
    pl.semaphore_wait(barrier, 3 + stages)
    order = sorted(range(members), key=lambda r: zeros_below(r) if r else stages)
    sent = [r for r in order if r]
    events = {}
    for r in order:
        for stage in range(zeros_below(r) if r else stages):
            events[stage, r] = len(events)

    def give(r):
        stage = zeros_below(r)
        slot = events[stage, r ^ (1 << stage)]
        return push(
            out_ref.at[r],
            slots_ref.at[slot],
            piece_send.at[r],
            piece_recv.at[slot],
            "seq",
            flip(member, 1 << stage),
        )

    def take(stage, r):
        slot = events[stage, r]
        return push(
            out_ref.at[0], slots_ref.at[slot], piece_send.at[0], piece_recv.at[slot], "seq", flip(member, 1 << stage)
        )

    def send_piece(r):
        out_ref[r] = acc_ref[flip(member, r)].astype(BF)
        give(r).start()

    def receive(r):
        index = flip(member, r)
        for stage in range(zeros_below(r) if r else stages):
            take(stage, r).wait_recv()
            acc_ref[index] += slots_ref[events[stage, r]].astype(F32)
        if r:
            send_piece(r)

    first = sorted([r for r in range(members) if r % 2], key=lambda r: order.index(r ^ 1))
    evens = [r for r in order if r % 2 == 0]
    if rows % 128 == 0:
        for r in first:
            even = 2 * lax.div(flip(member, r), 2)
            columns = pl.ds(pl.multiple_of(even * rows, 128), 2 * rows)
            block = tn(rows_ref[:, columns], dpre_ref[...])
            acc_ref[even] = block[:rows]
            acc_ref[even + 1] = block[rows:]
            send_piece(r)
        begin()
    else:
        per = 128 // rows
        for unit in range(width // 128):
            block = tn(rows_ref[:, unit * 128 : (unit + 1) * 128], dpre_ref[...])
            acc_ref[unit * per : (unit + 1) * per] = block.reshape(per, rows, block.shape[1])
        for r in first:
            send_piece(r)
        begin()

    small_slots[0] = small_ref[...]
    diagonal = lax.broadcasted_iota(jnp.int32, (128, 128), 0) == lax.broadcasted_iota(jnp.int32, (128, 128), 1)

    def project(index):
        part = nt(dpre_ref[at(index)], pack_ref[...])
        part_ref[at(index)] = part.astype(BF)
        start_pair(index)
        seen = part * (input_ref[at(index)].astype(F32) * scale_ref[at(index)])
        small_slots[0, 0:1] += jnp.sum(seen, 0, keepdims=True)
        stat = jnp.sum(seen * gain_ref[...], axis=-1, keepdims=True)
        for block in range(chunk // 128):
            line = jnp.where(diagonal, stat[block * 128 : (block + 1) * 128], 0.0)
            stat_ref[index * (chunk // 128) + block] = jnp.sum(line, 0, keepdims=True)

    early = steps // 2
    receives = list(evens)
    for half in range(2):

        @pl.loop(half * early, (half + 1) * early)
        def _(index):
            project(index)

            @pl.when(lax.rem(index, 2) == 1)
            def _():
                pass_on(lax.div(index, 2))

        if len(receives) > 1:
            receive(receives.pop(0))

    def stat_copy(turn):
        target = (near, far, opposite)[turn]
        return push(stat_ref, stat_slots.at[turn], stat_send.at[turn], stat_recv.at[turn], "head", target)

    def head_copy(turn):
        target = (near, far, opposite)[turn]
        return push(
            small_slots.at[0, pl.ds(0, 8)],
            small_slots.at[1 + turn, pl.ds(0, 8)],
            small_send.at[turn],
            small_recv.at[turn],
            "head",
            target,
        )

    for turn in (1, 2, 0):
        head_copy(turn).start()
        stat_copy(turn).start()
    for index in range(early, steps):
        pass_on(index)
    while len(receives) > 1:
        receive(receives.pop(0))
    for turn in range(3):
        head_copy(turn).wait()
    small_slots[4] = small_slots[0]
    small_slots[4, 0:8] += small_slots[1, 0:8] + small_slots[2, 0:8] + small_slots[3, 0:8]

    bits = list(range(1, stages)) + [0]

    def seq_copy(turn):
        return push(
            small_slots.at[4 + 2 * turn],
            small_slots.at[5 + 2 * turn],
            small_send.at[3 + turn],
            small_recv.at[3 + turn],
            "seq",
            flip(member, 1 << bits[turn]),
        )

    def seq_add(turn):
        seq_copy(turn).wait()
        small_slots[6 + 2 * turn] = small_slots[4 + 2 * turn] + small_slots[5 + 2 * turn]

    seq_copy(0).start()
    for turn in range(3):
        stat_copy(turn).wait()
    stat_ref[...] += stat_slots[0] + stat_slots[1] + stat_slots[2]

    def result(index):
        grad = own_sum(index)
        scale = scale_ref[at(index)]
        unit = input_ref[at(index), cols(place)].astype(F32) * scale
        means = []
        for block in range(chunk // 128):
            line = jnp.where(diagonal, stat_ref[index * (chunk // 128) + block], 0.0)
            means.append(jnp.sum(line, axis=-1, keepdims=True))
        mean = jnp.concatenate(means, 0) * (1.0 / width)
        ingrad_ref[at(index)] = dmid_ref[at(index)] + scale * (grad * gain_ref[:, cols(place)] - unit * mean)

    rests = list(rest_jobs)
    for turn in range(stages):
        start, stop = turn * steps // stages, (turn + 1) * steps // stages
        if stop > start:

            @pl.loop(start, stop)
            def _(index):
                result(index)

        share = (len(rests) - 1) // (stages - turn)
        for job in rests[:share]:
            rest_receive(*job)
        rests = rests[share:]
        seq_add(turn)
        if turn + 1 < stages:
            seq_copy(turn + 1).start()
    receive(0)
    for job in rests:
        rest_receive(*job)
    piece_ref[...] = acc_ref[member]
    sums_ref[...] = small_slots[4 + 2 * stages]

    @pl.loop(0, steps)
    def _(index):
        finish(index)

    for r in sent:
        give(r).wait_send()
    rest_end()


def final_stage(first_rows, dpre, pack, inputs, scale, gain, dmid, small, rest, members, collective):
    tokens, width = inputs.shape
    columns = dmid.shape[1]
    chunk = 256
    steps = tokens // chunk
    stages = (members - 1).bit_length()
    rows = width // members
    wide = dpre.shape[1]
    whole = pl.BlockSpec(memory_space=pltpu.VMEM)
    return pl.pallas_call(
        functools.partial(final_kernel, members, chunk),
        name="final",
        out_shape=(
            jax.ShapeDtypeStruct((tokens, columns), F32),
            jax.ShapeDtypeStruct((rows, wide), F32),
            jax.ShapeDtypeStruct(small.shape, F32),
            jax.ShapeDtypeStruct((rest.shape[0], *rest.shape[2:]), F32),
        ),
        in_specs=[whole] * 9,
        out_specs=(whole,) * 4,
        scratch_shapes=[
            pltpu.VMEM((members, rows, wide), F32),
            pltpu.VMEM((members, rows, wide), BF),
            pltpu.VMEM((members - 1, rows, wide), BF),
            pltpu.VMEM((tokens, width), BF),
        ]
        + head_scatter_scratch(tokens, columns, steps)
        + [
            pltpu.VMEM((tokens // 128, 1, 128), F32),
            pltpu.VMEM((3, tokens // 128, 1, 128), F32),
            pltpu.VMEM((5 + 2 * stages, *small.shape), F32),
            pltpu.SemaphoreType.DMA((members,)),
            pltpu.SemaphoreType.DMA((members - 1,)),
            pltpu.SemaphoreType.DMA((3,)),
            pltpu.SemaphoreType.DMA((3,)),
            pltpu.SemaphoreType.DMA((3 + stages,)),
            pltpu.SemaphoreType.DMA((3 + stages,)),
        ]
        + piece_scatter_scratch(rest.shape[0], members, rest.shape[2:]),
        compiler_params=pltpu.CompilerParams(
            collective_id=collective, has_side_effects=True, vmem_limit_bytes=VMEM_LIMIT
        ),
        cost_estimate=pl.CostEstimate(flops=8 * 10**9, bytes_accessed=30 << 20, transcendentals=0),
    )(first_rows, dpre, pack, inputs, scale, gain, dmid, small, rest)
def turn_column(column):
    diagonal = lax.broadcasted_iota(jnp.int32, (128, 128), 0) == lax.broadcasted_iota(jnp.int32, (128, 128), 1)
    lines = []
    for block in range(column.shape[0] // 128):
        lines.append(jnp.sum(jnp.where(diagonal, column[block * 128 : (block + 1) * 128], 0.0), 0, keepdims=True))
    return jnp.concatenate(lines, 1)


def piece_gather(full_ref, send, recv, members):
    member = lax.axis_index("seq")
    parts = full_ref.shape[0]
    stages = (members - 1).bit_length()

    def give(part, r, stage):
        owner = flip(member, r)
        mark = r ^ (1 << stage)
        return push(
            full_ref.at[part, owner],
            full_ref.at[part, owner],
            send.at[part, mark],
            recv.at[part, mark],
            "seq",
            flip(member, 1 << stage),
        )

    def take(part, r):
        owner = flip(member, r)
        return push(
            full_ref.at[part, owner],
            full_ref.at[part, owner],
            send.at[part, r],
            recv.at[part, r],
            "seq",
            flip(member, r & -r),
        )

    def begin(part=0, levels=None):
        for stage in reversed(range(stages)) if levels is None else levels:
            give(part, 0, stage).start()

    def relay(part, r):
        take(part, r).wait_recv()
        for stage in reversed(range(zeros_below(r))):
            give(part, r, stage).start()
        if r == 1 << (stages - 1) and part + 1 < parts:
            begin(part + 1)

    order = sorted([r for r in range(1, members) if r % 2 == 0], key=lambda r: (-zeros_below(r), r))
    def when(part, r):
        return 2 * part + 3 * (bin(r).count("1") - 1), part, -zeros_below(r), r

    relays = sorted([(part, r) for r in order for part in range(parts)], key=lambda job: when(*job))

    def arrive():
        for part in range(parts):
            for r in range(1, members, 2):
                take(part, r).wait_recv()

    def finish():
        for part in range(parts):
            for r in [0] + order:
                for stage in range(zeros_below(r) if r else stages):
                    give(part, r, stage).wait_send()

    return begin, relay, relays, arrive, finish


def greet_seq(members):
    member = lax.axis_index("seq")
    stages = (members - 1).bit_length()
    barrier = pltpu.get_barrier_semaphore()
    for stage in range(stages):
        pl.semaphore_signal(barrier, inc=1, device_id={"seq": flip(member, 1 << stage)}, device_id_type=MESH)
    return barrier, stages


def front_kernel(
    members,
    heads,
    resets_ref,
    input_ref,
    query_ref,
    key_ref,
    value_ref,
    extra_ref,
    out_weight_ref,
    own_ref,
    taps_ref,
    pack_ref,
    first_ref,
    pre_ref,
    logits_ref,
    halo_ref,
    scale_ref,
    gains_ref,
    turned_ref,
    full_ref,
    others_ref,
    qkv_ref,
    inv_ref,
    wu_ref,
    mq_ref,
    start_ref,
    out0_ref,
    total_ref,
    pad_ref,
    edge_ref,
    pack_send,
    pack_recv,
    edge_send,
    edge_recv,
    turned_send,
    turned_recv,
    full_send,
    full_recv,
    head_send,
    head_recv,
):
    tokens, width = input_ref.shape
    columns = heads * CHUNK
    member = lax.axis_index("seq")
    _, _, near, far = head_peers()
    barrier, stages = greet_seq(members)
    for target in (near, far):
        pl.semaphore_signal(barrier, inc=1, device_id={"head": target}, device_id_type=MESH)

    @pl.when(member > 0)
    def _():
        pl.semaphore_signal(barrier, inc=1, device_id={"seq": member - 1}, device_id_type=MESH)

    pack_ref[0, member, :, :columns] = query_ref[...]
    pack_ref[0, member, :, columns : 2 * columns] = key_ref[...]
    pack_ref[0, member, :, 2 * columns : 3 * columns] = value_ref[...]
    pack_ref[0, member, :, 3 * columns :] = extra_ref[...]
    turned_ref[0, member] = out_weight_ref[...]
    for part in range(full_ref.shape[0]):
        full_ref[part, member] = own_ref[part]
    pack = piece_gather(pack_ref, pack_send, pack_recv, members)
    turned = piece_gather(turned_ref, turned_send, turned_recv, members)
    full = piece_gather(full_ref, full_send, full_recv, members)
    near_copy = push(turned_ref.at[0], others_ref.at[0], head_send.at[0], head_recv.at[0], "head", near)
    far_copy = push(turned_ref.at[0], others_ref.at[1], head_send.at[1], head_recv.at[1], "head", far)
    pass_copy = push(others_ref.at[1], others_ref.at[2], head_send.at[2], head_recv.at[2], "head", near)
    pl.semaphore_wait(barrier, stages + 2 + jnp.minimum(members - 1 - member, 1))
    pack[0]()
    turned[0]()
    full[0](0, [stages - 1, 0])

    last_rows = pl.ds(tokens - 16, 16)

    def edge(target):
        return push(input_ref.at[last_rows], edge_ref, edge_send, edge_recv, "seq", target)

    @pl.when(member + 1 < members)
    def _():
        edge(member + 1).start()

    chunk = 256

    def at(index):
        return pl.ds(pl.multiple_of(index * chunk, chunk), chunk)

    def measure(index):
        block = input_ref[at(index)].astype(F32)
        scale_ref[at(index)] = lax.rsqrt(jnp.mean(block * block, axis=-1, keepdims=True) + 1e-06)

    pl.loop(0, tokens // chunk)(measure)
    for job in pack[2]:
        pack[1](*job)
    for job in turned[2]:
        turned[1](*job)
    full[0](0, range(1, stages - 1))
    pack[3]()
    projection = pack_ref[0].reshape(width, pack_ref.shape[3])
    extras = projection[:, 3 * columns :].astype(F32)
    gains_ref[0:1] = turn_column(extras[:, heads : heads + 1])
    gains_ref[1:2] = turn_column(extras[:, heads + 1 : heads + 2])

    def project(index):
        first = (input_ref[at(index)].astype(F32) * scale_ref[at(index)] * gains_ref[0:1]).astype(BF)
        first_ref[at(index)] = first
        both = nn(first, pack_ref[0].reshape(width, pack_ref.shape[3]))
        pre_ref[at(index)] = both[:, : 3 * columns].astype(BF)
        logits_ref[at(index)] = both[:, 3 * columns :]

    pl.loop(0, tokens // chunk)(project)

    @pl.when(member == 0)
    def _():
        halo_ref[...] = jnp.zeros_like(halo_ref)

    @pl.when(member > 0)
    def _():
        edge(member).wait_recv()
        block = edge_ref[...].astype(F32)
        scale = lax.rsqrt(jnp.mean(block * block, axis=-1, keepdims=True) + 1e-06)
        first = (block * scale * gains_ref[0:1]).astype(BF)
        halo_ref[...] = nn(first, pack_ref[0].reshape(width, pack_ref.shape[3])[:, : 3 * columns]).astype(BF)

    turned[3]()
    near_copy.start()
    far_copy.start()
    rows, cols = grid_indices()
    eye = jnp.where(rows == cols, 1.0, 0.0)
    top = lax.broadcasted_iota(jnp.int32, (CHUNK, 1), 0) < GROUP
    for head in range(heads):
        total_ref[head] = side(eye, jnp.zeros_like(eye))
    batch = pad_ref.shape[0]

    def one(step, carry):
        units = []
        for lane in range(batch):
            chunk = step * batch + lane
            pad = pad_ref.at[lane]
            load_padded(pad, pre_ref, halo_ref, chunk, resets_ref)
            mixed = convolve(pad, taps_ref)
            silued = mixed * sigmoid(mixed)
            keep0 = 1.0 - resets_ref[2 * chunk]
            keep1 = 1.0 - resets_ref[2 * chunk + 1]
            both = keep0 * keep1
            enter = jnp.where(top, keep0, both)
            leave = jnp.where(top, keep1, 1.0)
            at = pl.ds(pl.multiple_of(chunk * CHUNK, CHUNK), CHUNK)
            beta_rows = sigmoid(logits_ref[at, :])
            for head in range(heads):
                window = slice(head * CHUNK, (head + 1) * CHUNK)
                parts = []
                for kind in range(3):
                    part = silued[:, kind * columns + head * CHUNK : kind * columns + (head + 1) * CHUNK]
                    if kind < 2:
                        part = part * lax.rsqrt(jnp.sum(part * part, axis=-1, keepdims=True) + 1e-06)
                    part = part.astype(BF)
                    qkv_ref[at, kind * columns + head * CHUNK : kind * columns + (head + 1) * CHUNK] = part
                    parts.append(part)
                units.append((chunk, head, *parts, beta_rows[:, head : head + 1], keep1, both, enter, leave))
        turned = [u[3].T for u in units]
        strict = [
            jnp.where(rows > cols, u[5] * nn(u[3], t), 0.0) for u, t in zip(units, turned)
        ]
        inverses = [r.astype(BF) for r in inverse_levels(strict, rows, cols, [u[6] for u in units])]
        factors = []
        for u, inverse in zip(units, inverses):
            beta = u[5]
            factors.append(nn(inverse, side(u[3].astype(F32) * beta, u[4].astype(F32) * beta)))
        for u, inverse, factor, t in zip(units, inverses, factors, turned):
            chunk, head, query, key, value, beta, keep1, both, enter, leave = u
            weight, update = factor[:, :CHUNK], factor[:, CHUNK:]
            entering_weight = weight * enter
            inv_ref[chunk, head] = inverse
            wu_ref[chunk, head] = side(entering_weight, update).astype(BF)
            gathered = nn(t, side(weight, update * leave))
            device_map = (both * (eye - gathered[:, :CHUNK])).astype(BF)
            shift = gathered[:, CHUNK:]
            scores = jnp.where(rows >= cols, nn(query, t), 0.0)
            scores = jnp.where((rows >= GROUP) & (cols < GROUP), scores * keep1, scores)
            seen = nn(scores, side(entering_weight, update))
            effective = query.astype(F32) * enter - seen[:, :CHUNK]
            mq_ref[chunk, head] = stack(device_map, effective.astype(BF))
            out0_ref[chunk, head] = seen[:, CHUNK:]
            running = total_ref[head]
            start_ref[chunk, head] = running.astype(BF)
            total_ref[head] = nn(device_map, running) + side(jnp.zeros_like(shift), shift)
        return carry

    count = resets_ref.shape[0] // 2 // batch
    relays = full[2]

    def pumped(step, carry):
        carry = one(step, carry)
        for turn in range(count):
            jobs = [job for place, job in enumerate(relays) if place * count // len(relays) == turn]
            if not jobs and turn != count // 2:
                continue

            @pl.when(step == turn)
            def _():
                for job in jobs:
                    full[1](*job)
                if turn == count // 2:
                    far_copy.wait_recv()
                    pass_copy.start()

        return carry

    lax.fori_loop(0, count, pumped, 0)
    near_copy.wait()
    far_copy.wait_send()
    pass_copy.wait()
    full[3]()

    @pl.when(member + 1 < members)
    def _():
        edge(member + 1).wait_send()

    for gather in (pack, turned, full):
        gather[4]()


def front_stage(resets, inputs, query, key, value, extra, out_weight, own, taps, members, heads, collective):
    tokens, width = inputs.shape
    columns = heads * CHUNK
    chunks = tokens // CHUNK
    whole = pl.BlockSpec(memory_space=pltpu.VMEM)
    piece = width // members

    def units(wide, kind):
        return jax.ShapeDtypeStruct((chunks, heads, *wide), kind)

    def dma(*shape):
        return [pltpu.SemaphoreType.DMA(shape)] * 2

    return pl.pallas_call(
        functools.partial(front_kernel, members, heads),
        name="front",
        out_shape=(
            jax.ShapeDtypeStruct((1, members, piece, 3 * columns + CHUNK), BF),
            jax.ShapeDtypeStruct((tokens, width), BF),
            jax.ShapeDtypeStruct((tokens, 3 * columns), BF),
            jax.ShapeDtypeStruct((tokens, CHUNK), F32),
            jax.ShapeDtypeStruct((16, 3 * columns), BF),
            jax.ShapeDtypeStruct((tokens, 1), F32),
            jax.ShapeDtypeStruct((2, width), F32),
            jax.ShapeDtypeStruct((1, members, *out_weight.shape), BF),
            jax.ShapeDtypeStruct((own.shape[0], members, *own.shape[1:]), BF),
            jax.ShapeDtypeStruct((3, members, *out_weight.shape), BF),
            jax.ShapeDtypeStruct((tokens, 3 * columns), BF),
            units((CHUNK, CHUNK), BF),
            units((CHUNK, 2 * CHUNK), BF),
            units((2 * CHUNK, CHUNK), BF),
            units((CHUNK, 2 * CHUNK), BF),
            units((CHUNK, CHUNK), F32),
            jax.ShapeDtypeStruct((heads, CHUNK, 2 * CHUNK), F32),
        ),
        in_specs=[pl.BlockSpec(memory_space=pltpu.SMEM)] + [whole] * 8,
        out_specs=(whole,) * 17,
        scratch_shapes=[pltpu.VMEM((2, 144, 3 * columns), F32), pltpu.VMEM((16, width), BF)]
        + dma(1, members)
        + dma()
        + dma(1, members)
        + dma(own.shape[0], members)
        + dma(3),
        compiler_params=pltpu.CompilerParams(
            collective_id=collective, has_side_effects=True, vmem_limit_bytes=VMEM_LIMIT
        ),
        cost_estimate=pl.CostEstimate(flops=8 * 10**9, bytes_accessed=40 << 20, transcendentals=2 << 20),
    )(resets, inputs, query, key, value, extra, out_weight, own, taps)


def lanes_whole(pieces):
    places, rows, piece = pieces.shape
    if piece >= 128:
        return pieces
    group = 128 // piece
    return pieces.reshape(places // group, group, rows, piece).transpose(0, 2, 1, 3).reshape(places // group, rows, 128)


def lanes_split(blocks, piece):
    count, rows, lanes = blocks.shape
    if piece >= 128:
        return blocks
    group = 128 // piece
    return blocks.reshape(count, rows, group, piece).transpose(0, 2, 1, 3).reshape(count * group, rows, piece)


def body(
    block_input,
    first_gain,
    query_weight,
    key_weight,
    value_weight,
    beta_weight,
    conv_weight,
    head_gain,
    output_weight,
    second_gain,
    gate_weight,
    up_weight,
    down_weight,
    lengths,
    cotangent,
):
    tokens, width = block_input.shape
    heads = beta_weight.shape[1]
    columns = query_weight.shape[1]
    hidden_columns = gate_weight.shape[1]
    members = lax.axis_size("seq")
    piece = width // members
    seq_place = lax.axis_index("seq")

    extra = jnp.concatenate(
        [beta_weight, first_gain[:, None], second_gain[:, None], jnp.zeros((piece, CHUNK - heads - 2), BF)], 1
    )
    ends = jnp.sum(jnp.where(jnp.arange(4)[:, None] >= jnp.arange(4)[None, :], lengths[None, :], 0), axis=1)
    starts = ends - lengths
    block_starts = seq_place * tokens + GROUP * jnp.arange(tokens // GROUP, dtype=jnp.int32)
    resets = jnp.any(starts[None, :] == block_starts[:, None], axis=1).astype(F32)

    taps = conv_weight.astype(F32).transpose(1, 0, 2).reshape(4, -1)
    own = jnp.stack([gate_weight.T, up_weight.T, down_weight.T])
    split = piece < 128
    (
        mixer_pack,
        first_rows,
        pre,
        logits,
        halo,
        scale_one,
        gains,
        turned,
        full,
        others,
        qkv,
        inv,
        wu,
        mq,
        start,
        out0,
        total,
    ) = front_stage(
        resets,
        block_input,
        query_weight,
        key_weight,
        value_weight,
        extra,
        output_weight.T,
        own[:1, :16] if split else own,
        taps,
        members,
        heads,
        5,
    )
    mixer_pack = mixer_pack.reshape(width, -1)
    if split:
        gathered = lax.all_gather(own, "seq", axis=1)
        full = jnp.stack([lanes_whole(gathered[i]) for i in range(3)])
    turned = lanes_whole(turned[0])
    others = jnp.stack([lanes_whole(others[i]) for i in range(3)]) if split else others
    total_low = total.astype(BF)
    (state,) = exchange(total_low, (), "seq", False, 0)
    gain_head = head_gain.astype(F32)[None, :]
    delta, head_rows, states = mixer_output(state, start, mq, out0, gain_head)

    d_heads, update_part, middle_shard, d_middle_shard, *grads, second_grad = middle_stage(
        head_rows, full, turned, others, block_input, cotangent, gains[1:2], 2
    )
    second_part = jnp.sum(second_grad, 0)
    ddelta, gain_part, shift = mixer_back_state(d_heads, delta, gain_head, mq)
    back_part = jnp.concatenate([total_low[:, :, :CHUNK].transpose(0, 2, 1), shift.astype(BF)], 2)
    if split:
        pieces = jnp.concatenate([part for pair in grads for part in pair], 1)
        whole_sum = lax.psum_scatter(lanes_split(pieces, piece), "seq", scatter_dimension=0, tiled=False).astype(F32)
        grads = [jnp.zeros((1, members, 16, 128), BF)] * 3
    arrive, block_output, third_sum = exchange(back_part, (update_part, middle_shard, grads[2]), "seq", True, 1)
    d_pre, taps_part, first_sum = mixer_backward(
        resets, pre, halo, taps, logits, qkv, inv, wu, mq, states, ddelta, arrive, grads[0], 3
    )
    small = jnp.concatenate(
        [
            jnp.zeros((1, width), F32),
            jnp.pad(jnp.sum(gain_part, 0, keepdims=True), ((0, 0), (0, width - CHUNK))),
            jnp.zeros((6, width), F32),
            jnp.sum(second_grad, 0, keepdims=True),
            jnp.sum(taps_part, 1).reshape(-1, width),
            jnp.zeros((7 - 12 * columns // width, width), F32),
        ]
    )
    input_gradient, mixer_sum, sums, second_sum = final_stage(
        first_rows, d_pre, mixer_pack, block_input, scale_one, gains[0:1], d_middle_shard, small, grads[1], members, 4
    )
    if not split:
        whole_sum = jnp.concatenate([s.reshape(-1, 128) for s in (first_sum, second_sum, third_sum)])
    gain_sum = sums[1, :CHUNK]
    conv_gradient = sums[9 : 9 + 12 * columns // width].reshape(4, 3, columns).transpose(1, 0, 2)
    row_start = seq_place * piece
    first_gradient = lax.dynamic_slice_in_dim(sums[0], row_start, piece, 0)
    second_gradient = lax.dynamic_slice_in_dim(sums[8], row_start, piece, 0)
    beta_gradient = mixer_sum[:, 3 * columns : 3 * columns + heads]
    return (
        block_output,
        input_gradient,
        first_gradient,
        mixer_sum[:, :columns],
        mixer_sum[:, columns : 2 * columns],
        mixer_sum[:, 2 * columns : 3 * columns],
        beta_gradient,
        conv_gradient,
        gain_sum,
        whole_sum[3 * hidden_columns :].T,
        second_gradient,
        whole_sum[:hidden_columns].T,
        whole_sum[hidden_columns : 2 * hidden_columns].T,
        whole_sum[2 * hidden_columns : 3 * hidden_columns].T,
    )


def solution(mesh):
    return jax.shard_map(
        body,
        mesh=mesh,
        in_specs=(
            P("seq", None),
            P("seq"),
            P("seq", "head"),
            P("seq", "head"),
            P("seq", "head"),
            P("seq", "head"),
            P(None, None, "head"),
            P(),
            P("seq", "head"),
            P("seq"),
            P("seq", "head"),
            P("seq", "head"),
            P("seq", "head"),
            P(),
            P("seq", None),
        ),
        out_specs=(
            P("seq", "head"),
            P("seq", "head"),
            P("seq"),
            P("seq", "head"),
            P("seq", "head"),
            P("seq", "head"),
            P("seq", "head"),
            P(None, None, "head"),
            P(),
            P("seq", "head"),
            P("seq"),
            P("seq", "head"),
            P("seq", "head"),
            P("seq", "head"),
        ),
        check_vma=False,
    )
```

time: 455 us -> 401 us (0.88)
  waiting for transfers between devices: 74.5 us -> 0 us
  Pallas kernels: 307 us -> 368 us
  between operations: 14 us -> 0.82 us
  local copies, waits for them, and re-layouts: 30.5 us -> 20.1 us
  matrix products: 9.46 us -> 0 us
  starting transfers between devices: 4.98 us -> 0 us
    all_gather x2 -> x0, waiting for transfers between devices: 74.4 us -> none  [gather_seq(): return lax.all_gather(block, 'seq', axis=0, tiled=True)]
    pallas_call x2, Pallas kernels: 125 us -> 196 us  [the longest x1 101 us: front_stage(): pl.pallas_call(functools.partial(front_kernel, members, heads), name='fro...]
    pallas_call x2, Pallas kernels: 76 us -> 58.6 us  [exchange(): pl.pallas_call(functools.partial(exchange_kernel, axis, count, window, ba...]
    dot_general x3 -> x0, matrix products: 9.46 us -> none  [dot(): return jnp.dot(left, right, preferred_element_type=F32)]
    pallas_call x1, Pallas kernels: 37.5 us -> 44.7 us  [mixer_backward(): pl.pallas_call(functools.partial(mixer_backward_kernel, heads), name='mix...]
    convert_element_type x2 -> x0, other arithmetic: 4.99 us -> none  [the longest x1 2.92 us: body(): first_rows = (inputs * scale_one * gain_one).astype(BF)]
    ppermute x1 -> x0, starting transfers between devices: 4.86 us -> none  [from_behind(): return lax.ppermute(block, axis, route)]
    unnamed x31 -> x17, local copies, waits for them, and re-layouts: 11.5 us -> 7.95 us
  transfers between devices with their start and end apart: 4 -> 0, of which waited for: 2 -> 0; matrix products, arithmetic and copies ran while one was open for 9% -> 0% of each run, Pallas kernels for 41% -> 0%
where the time goes in v4:
time: 401 us; the launch traced here: 400 us
  Pallas kernels  368 us (92%)
  local copies, waits for them, and re-layouts  20.1 us (5%)
  other arithmetic  11.8 us (3%)
    pallas_call x1, Pallas kernels, front_stage(): pl.pallas_call(functools.partial(front_kernel, members, heads), name='fro...  101 us
    pallas_call x1, Pallas kernels, middle_stage(): pl.pallas_call(functools.partial(middle_kernel, steps), name='middle', gr...  94.9 us
    pallas_call x2, Pallas kernels, exchange(): pl.pallas_call(functools.partial(exchange_kernel, axis, count, window, ba...  58.6 us
    pallas_call x1, Pallas kernels, final_stage(): pl.pallas_call(functools.partial(final_kernel, members, chunk), name='fin...  52.1 us
    pallas_call x1, Pallas kernels, mixer_backward(): pl.pallas_call(functools.partial(mixer_backward_kernel, heads), name='mix...  44.7 us
    pallas_call x1, Pallas kernels, mixer_back_state(): pl.pallas_call(functools.partial(mixer_back_state_kernel, heads), name='m...  9.4 us

profile of v4, /device:TPU:0, one launch (start us, length us, event | category | flops | bytes accessed | tf_op | source)
XLA Modules:
  0.0 400.4 jit_solution(10060339924284659346)
XLA Ops:
  0.7 1.2 bitcast_convert_fusion.gain_ref
  1.8 0.8 select_reduce_fusion
  4.0 1.3 reshape.71
  5.2 0.8 copy.48
  6.0 0.8 copy.47
  6.8 0.8 copy.49
  7.6 0.7 maximum_maximum_fusion.extra_ref
  8.3 1.6 copy.50
  9.9 2.0 pad_maximum_fusion.own_ref
  11.8 101.2 %front.1 = (bf16[1,8,128,896]{3,2,1,0:T(8,128)(2,1)}, bf16[2048,1024]{1,0:T(8,128)(2,1)}, bf16[2048,768]{1,0:T(8,128)(2,1)}, f32[2048,128]{1,0:T(8,128)}, bf16[1...) custom-call(f32[32]{0:T(128)} %convert_element_type.13.resets_ref, ...), custom_call_target="tpu_custom_call" | custom-call | flops 8000000000 | bytes 41943040 | tf_op jit(solution)/shard_map/front/pallas_call | solution.py:1557
  113.1 1.1 copy.51
  114.1 1.4 fusion.4
  115.5 0.8 copy.52.refs_0_
  116.3 9.5 %state_forward.1.state_ref = f32[2,128,128]{2,1,0:T(8,128)} custom-call(bf16[2,128,256]{2,1,0:T(8,128)(2,1)} %copy.52.refs_0_), custom_call_target="tpu_custom_call" | custom-call | flops 1000000000 | bytes 20971520 | tf_op jit(solution)/shard_map/state_forward/pallas_call | solution.py:218
  125.8 6.8 %mixer_output.1 = (f32[2048,256]{1,0:T(8,128)}, bf16[2048,256]{1,0:T(8,128)(2,1)}, bf16[16,2,128,128]{3,2,1,0:T(8,128)(2,1)}) custom-call(f32[2,128,128]{2,1,0:T(8,128)} %state_forward.1.state_ref, bf16[16,2,128,256]{3,2,1,0:T(8,128)(2,1)} %get-tuple-element.56.start_ref, bf16[16,2,256,128]{3,2,1,0:T(8,128)(2,1)} %get-tuple-element.57.mq_ref, ...), custom_call_target="tpu_custom_call" | custom-call | flops 300000000 | bytes 10485760 | tf_op jit(solution)/shard_map/mixer_output/pallas_call | solution.py:257
  132.6 94.9 %middle.1 = (bf16[2048,256]{1,0:T(8,128)(2,1)}, bf16[2048,1024]{1,0:T(8,128)(2,1)}, f32[2048,256]{1,0:T(8,128)}, f32[2048,256]{1,0:T(8,128)}, bf16[2,8,576,128]{...) custom-call(bf16[2048,256]{1,0:T(8,128)(2,1)} %get-tuple-element.59.row, ...), custom_call_target="tpu_custom_call" | custom-call | flops 30000001024 | bytes 31457280 | tf_op jit(solution)/shard_map/middle/pallas_call | solution.py:849
  227.5 9.4 %mixer_back_state.1 = (bf16[2048,256]{1,0:T(8,128)(2,1)}, f32[8,128]{1,0:T(8,128)}, f32[2,128,128]{2,1,0:T(8,128)}) custom-call(bf16[2048,256]{1,0:T(8,128)(2,1)} %get-tuple-element.64.dheads_ref, f32[2048,256]{1,0:T(8,128)} %get-tuple-element.65.delta_ref, f32[1,128]{1,0:T(1,128)} %bitcast_convert_fusion.gain_ref, ...), custom_call_target="tpu_custom_call" | custom-call | flops 300000000 | bytes 10485760 | tf_op jit(solution)/shard_map/mixer_back_state/pallas_call | solution.py:298
  236.9 0.9 convert_element_type.15
  238.5 49.1 %state_backward.1 = (f32[2,128,128]{2,1,0:T(8,128)}, bf16[2048,256]{1,0:T(8,128)(2,1)}, f32[2,400,128]{2,1,0:T(8,128)}) custom-call(bf16[2,128,256]{2,1,0:T(8,128)(2,1)} %pad_maximum_fusion.3.refs_0_, bf16[2048,1024]{1,0:T(8,128)(2,1)} %get-tuple-element.67.refs_1_, f32[2048,256]{1,0:T(8,128)} %get-tuple-element.68.refs_2_, ...), custom_call_target="tpu_custom_call" | custom-call | flops 1000000000 | bytes 20971520 | tf_op jit(solution)/shard_map/state_backward/pallas_call | solution.py:218
  287.6 44.7 %mixer_backward.1 = (bf16[2048,896]{1,0:T(8,128)(2,1)}, f32[4,8,768]{2,1,0:T(8,128)}, f32[2,576,128]{2,1,0:T(8,128)}) custom-call(f32[32]{0:T(128)} %convert_element_type.13.resets_ref, bf16[2048,768]{1,0:T(8,128)(2,1)} %get-tuple-element.72.pre_ref, bf16[16,768]{1,0:T(8,128)(2,1)} %get-tuple-element.73.halo_ref, f32[4,768]{1,0:T(4,128)} %bitcast.52, ...), custom_call_target="tpu_custom_call" | custom-call | flops 3000000000 | bytes 20971520 | tf_op jit(solution)/shard_map/mixer_backward/pallas_call | solution.py:559
  332.4 0.9 reduce_sum.39
  333.4 1.3 concatenate.18.small_ref
  334.7 52.1 %final.1 = (f32[2048,256]{1,0:T(8,128)}, f32[128,896]{1,0:T(8,128)}, f32[16,1024]{1,0:T(8,128)}, f32[2,208,128]{2,1,0:T(8,128)}) custom-call(bf16[2048,1024]{1,0:T(8,128)(2,1)} %get-tuple-element.71.rows_ref, bf16[2048,896]{1,0:T(8,128)(2,1)} %get-tuple-element.82.dpre_ref, bf16[1024,896]{1,0:T(8,128)(2,1)} %bitcast.57, bf16[2048,1024]{1,0:T(8,128)(2,1)} %input_ref.5, ...), custom_call_target="tpu_custom_call" | custom-call | flops 8000000000 | bytes 31457280 | tf_op jit(solution)/shard_map/final/pallas_call | solution.py:1211
  386.8 1.2 slice_bitcast_fusion.3
  388.0 0.8 fusion.3
  388.8 0.8 slice.55
  390.7 0.8 slice.54
  391.5 1.8 fusion.2
  394.0 2.1 fusion.1
  396.1 0.8 copy.55
  396.8 2.3 copy.58
  399.1 1.3 copy.59
  (30 shorter events, 3.9 us)
Async XLA Ops:
  287.6 44.8 %copy-start.4 = (f32[8,128]{1,0:T(8,128)S(1)}, f32[8,128]{1,0:T(8,128)}, u32[]{:S(2)}) copy-start(f32[8,128]{1,0:T(8,128)} %get-tuple-element.86) | copy-start | bytes 12292
  287.6 44.8 %copy-start.3 = (f32[8,1024]{1,0:T(8,128)S(1)}, f32[8,1024]{1,0:T(8,128)}, u32[]{:S(2)}) copy-start(f32[8,1024]{1,0:T(8,128)} %get-tuple-element.87) | copy-start | bytes 98308
  334.7 59.3 %copy-start.2 = (f32[2,400,128]{2,1,0:T(8,128)S(1)}, f32[2,400,128]{2,1,0:T(8,128)}, u32[]{:S(2)}) copy-start(f32[2,400,128]{2,1,0:T(8,128)} %get-tuple-element.93) | copy-start | bytes 1228804
  334.7 59.3 %copy-start.1 = (f32[2,576,128]{2,1,0:T(8,128)S(1)}, f32[2,576,128]{2,1,0:T(8,128)}, u32[]{:S(2)}) copy-start(f32[2,576,128]{2,1,0:T(8,128)} %get-tuple-element.94) | copy-start | bytes 1769476
  394.0 5.1 %copy-start = (f32[2048,256]{1,0:T(8,128)S(1)}, f32[2048,256]{1,0:T(8,128)}, u32[]{:S(2)}) copy-start(f32[2048,256]{1,0:T(8,128)} %get-tuple-element.165) | copy-start | bytes 6291460

commit v5 on v4

--- a/solution.py
+++ b/solution.py
@@ -12,7 +12,7 @@
 MESH = pl.DeviceIdType.MESH
 BF = jnp.bfloat16
 F32 = jnp.float32
-VMEM_LIMIT = 56 << 20
+VMEM_LIMIT = 59 << 20
 
 
 def nn(left, right):
@@ -227,44 +227,6 @@
         ),
         cost_estimate=pl.CostEstimate(flops=10**9, bytes_accessed=20 << 20, transcendentals=0),
     )(part, *extras)
-
-
-def mixer_output_kernel(heads, state_ref, start_ref, mq_ref, out0_ref, gain_ref, delta_ref, rows_ref, states_ref):
-    batch = 4
-
-    def one(step, carry):
-        for lane in range(batch):
-            chunk = step * batch + lane
-            at = pl.ds(pl.multiple_of(chunk * CHUNK, CHUNK), CHUNK)
-            for head in range(heads):
-                window = slice(head * CHUNK, (head + 1) * CHUNK)
-                begin = start_ref[chunk, head]
-                state = nn(begin[:, :CHUNK], state_ref[head]) + begin[:, CHUNK:].astype(F32)
-                state = state.astype(BF)
-                states_ref[chunk, head] = state
-                out = out0_ref[chunk, head] + nn(mq_ref[chunk, head, CHUNK:], state)
-                delta_ref[at, window] = out
-                scale = lax.rsqrt(jnp.mean(out * out, axis=-1, keepdims=True) + 1e-05)
-                rows_ref[at, window] = (out * scale * gain_ref[...]).astype(BF)
-        return carry
-
-    lax.fori_loop(0, start_ref.shape[0] // batch, one, 0)
-
-
-def mixer_output(state, start, mq, out0, gain):
-    chunks, heads = start.shape[:2]
-    tokens = chunks * CHUNK
-    return pl.pallas_call(
-        functools.partial(mixer_output_kernel, heads),
-        name="mixer_output",
-        out_shape=(
-            jax.ShapeDtypeStruct((tokens, heads * CHUNK), F32),
-            jax.ShapeDtypeStruct((tokens, heads * CHUNK), BF),
-            jax.ShapeDtypeStruct((chunks, heads, CHUNK, CHUNK), BF),
-        ),
-        compiler_params=pltpu.CompilerParams(vmem_limit_bytes=VMEM_LIMIT),
-        cost_estimate=pl.CostEstimate(flops=3 * 10**8, bytes_accessed=10 << 20, transcendentals=1 << 14),
-    )(state, start, mq, out0, gain)
 
 
 def mixer_back_state_kernel(heads, dheads_ref, delta_ref, gain_ref, mq_ref, ddelta_ref, gain_grad_ref, shift_ref):
@@ -612,6 +574,8 @@
 def middle_kernel(
     steps,
     rows_ref,
+    late_rows_ref,
+    far_rows_ref,
     full_hbm,
     turned_hbm,
     others_hbm,
@@ -633,7 +597,6 @@
     turned_ref,
     others_ref,
     load_sem,
-    full_ref,
     acc_ref,
     part_ref,
     pair_ref,
@@ -642,12 +605,6 @@
     keep_ref,
     scale_ref,
     shard_ref,
-    row_near_send,
-    row_near_recv,
-    row_far_send,
-    row_far_recv,
-    row_pass_send,
-    row_pass_recv,
     pair_send,
     pair_recv,
     far_send,
@@ -665,24 +622,6 @@
     theirs = pl.ds(pl.multiple_of((1 - low) * half, 128), half)
     own_columns = pl.ds(pl.multiple_of(place * columns, 128), columns)
 
-    def at(index):
-        return pl.ds(pl.multiple_of(index * chunk, chunk), chunk)
-
-    def near_rows(index):
-        return push(
-            rows_ref.at[at(index)], full_ref.at[0, at(index)], row_near_send.at[index], row_near_recv.at[index], "head", near
-        )
-
-    def far_rows(index):
-        return push(
-            rows_ref.at[at(index)], full_ref.at[1, at(index)], row_far_send.at[index], row_far_recv.at[index], "head", far
-        )
-
-    def pass_rows(index):
-        return push(
-            full_ref.at[1, at(index)], full_ref.at[2, at(index)], row_pass_send.at[index], row_pass_recv.at[index], "head", near
-        )
-
     def pair(index):
         return push(
             part_ref.at[lax.rem(index, 2), :, theirs], pair_ref.at[index], pair_send.at[index], pair_recv.at[index], "head", near
@@ -715,11 +654,6 @@
             load.start()
         greet("head", (near, far))
 
-        @pl.loop(0, steps)
-        def _(index):
-            far_rows(index).start()
-            near_rows(index).start()
-
         acc_ref[...] = jnp.zeros_like(acc_ref)
         gain_grad_ref[...] = jnp.zeros_like(gain_grad_ref)
         for load in loads():
@@ -730,21 +664,14 @@
         ct = ct_ref[...]
         d_hidden = nt(ct, down_ref[...])
 
-        @pl.when(step == 0)
-        def _():
-            far_rows(step).wait_recv()
-            pass_rows(step).start()
-
-        near_rows(step).wait_recv()
-        pass_rows(step).wait_recv()
-        branch = nn(rows_ref[at(step)], turned_ref[...])
+        branch = nn(rows_ref[...], turned_ref[...])
         for other in range(3):
-            branch = branch + nn(full_ref[other, at(step)], others_ref[other])
+            branch = branch + nn(far_rows_ref[other], others_ref[other])
         middle = input_ref[...].astype(F32) + branch
-        keep_ref[lax.rem(step, 3)] = middle
-        mid_ref[...] = keep_ref[lax.rem(step, 3), :, own_columns]
+        keep_ref[lax.rem(step, 4)] = middle
+        mid_ref[...] = keep_ref[lax.rem(step, 4), :, own_columns]
         scale = lax.rsqrt(jnp.mean(middle * middle, axis=-1, keepdims=True) + 1e-06)
-        scale_ref[lax.rem(step, 3)] = scale
+        scale_ref[lax.rem(step, 4)] = scale
         second = (middle * scale * gain_ref[...]).astype(BF)
         gate, up = nt(second, gate_ref[...]), nt(second, up_ref[...])
         sig = sigmoid(gate)
@@ -760,11 +687,6 @@
         part_ref[lax.rem(step, 2)] = (nn(d_gate, gate_ref[...]) + nn(d_up, up_ref[...])).astype(BF)
         pair(step).start()
 
-        @pl.when(step + 1 < steps)
-        def _():
-            far_rows(step + 1).wait_recv()
-            pass_rows(step + 1).start()
-
         update_ref[...] = nn(active, down_ref[...]).astype(BF)
         acc_ref[:hidden] += tn(d_gate, second)
         acc_ref[hidden : 2 * hidden] += tn(d_up, second)
@@ -777,22 +699,22 @@
         pair_ref[step] = both.astype(BF)
         across(step).start()
 
-    @pl.when((step > 0) & (step <= steps))
+    @pl.when((step > 1) & (step < steps + 2))
     def _():
-        done = step - 1
+        done = step - 2
         across(done).wait_recv()
         across(done).wait_send()
         total = pair_ref[done].astype(F32) + far_ref[done].astype(F32)
         sum_ref[done, :, mine] = total.astype(BF)
         last(done).start()
 
-    @pl.when(step > 1)
+    @pl.when(step > 2)
     def _():
-        done = step - 2
+        done = step - 3
         last(done).wait_recv()
         grad = sum_ref[done].astype(F32)
-        middle = keep_ref[lax.rem(done, 3)]
-        scale = scale_ref[lax.rem(done, 3)]
+        middle = keep_ref[lax.rem(done, 4)]
+        scale = scale_ref[lax.rem(done, 4)]
         unit = middle * scale
         gain_grad_ref[...] += jnp.sum((grad * unit).reshape(chunk // 8, 8, width), 0)
         scaled = grad * gain_ref[...]
@@ -803,9 +725,9 @@
         dmid_ref[...] = shard_ref[:, own_columns]
         d_branch = d_middle.astype(BF)
         dheads_ref[...] = nt(d_branch, turned_ref[...]).astype(BF)
-        acc_ref[3 * hidden :] += tn(rows_ref[at(done)], d_branch)
-
-    @pl.when(step == steps + 1)
+        acc_ref[3 * hidden :] += tn(late_rows_ref[...], d_branch)
+
+    @pl.when(step == steps + 2)
     def _():
         for piece in range(width // 128):
             lanes = slice(piece * 128, (piece + 1) * 128)
@@ -818,16 +740,13 @@
 
         @pl.loop(0, steps)
         def _(index):
-            near_rows(index).wait_send()
-            far_rows(index).wait_send()
-            pass_rows(index).wait_send()
             last(index).wait_send()
 
         for index in range(max(steps - 2, 0), steps):
             pair(index).wait_send()
 
 
-def middle_stage(head_rows, full, turned, others, inputs, cotangent, gain, collective):
+def middle_stage(head_rows, far_rows, full, turned, others, inputs, cotangent, gain, collective):
     tokens, width = inputs.shape
     columns = head_rows.shape[1]
     chunk = min(256, tokens // 2)
@@ -843,13 +762,14 @@
         return pl.BlockSpec((chunk, wide), lambda s: (jnp.minimum(s, steps - 1), 0))
 
     def late(wide):
-        return pl.BlockSpec((chunk, wide), lambda s: (jnp.maximum(s - 2, 0), 0))
-
+        return pl.BlockSpec((chunk, wide), lambda s: (jnp.maximum(s - 3, 0), 0))
+
+    far = pl.BlockSpec((3, chunk, columns), lambda s: (0, jnp.minimum(s, steps - 1), 0))
     dma = pltpu.SemaphoreType.DMA((steps,))
     return pl.pallas_call(
         functools.partial(middle_kernel, steps),
         name="middle",
-        grid=(steps + 2,),
+        grid=(steps + 3,),
         out_shape=(
             jax.ShapeDtypeStruct((tokens, columns), BF),
             jax.ShapeDtypeStruct((tokens, width), BF),
@@ -858,7 +778,7 @@
             *(jax.ShapeDtypeStruct((2, width // 128, rows, 128), BF) for rows in shares),
             jax.ShapeDtypeStruct((8, width), F32),
         ),
-        in_specs=[whole] + [outside] * 3 + [early(width), early(width), late(width), whole],
+        in_specs=[early(columns), late(columns), far] + [outside] * 3 + [early(width), early(width), late(width), whole],
         out_specs=(late(columns), early(width), early(columns), late(columns), whole, whole, whole, whole),
         scratch_shapes=[
             pltpu.VMEM((hidden, width), BF),
@@ -867,17 +787,16 @@
             pltpu.VMEM((columns, width), BF),
             pltpu.VMEM((3, columns, width), BF),
             pltpu.SemaphoreType.DMA((7, width // 128)),
-            pltpu.VMEM((3, tokens, columns), BF),
             pltpu.VMEM((3 * hidden + columns, width), F32),
             pltpu.VMEM((2, chunk, width), BF),
             pltpu.VMEM((steps, chunk, width // 2), BF),
             pltpu.VMEM((steps, chunk, width // 2), BF),
             pltpu.VMEM((steps, chunk, width), BF),
-            pltpu.VMEM((3, chunk, width), F32),
-            pltpu.VMEM((3, chunk, 1), F32),
+            pltpu.VMEM((4, chunk, width), F32),
+            pltpu.VMEM((4, chunk, 1), F32),
             pltpu.VMEM((chunk, width), F32),
         ]
-        + [dma] * 12,
+        + [dma] * 6,
         compiler_params=pltpu.CompilerParams(
             collective_id=collective,
             has_side_effects=True,
@@ -885,7 +804,7 @@
             dimension_semantics=("arbitrary",),
         ),
         cost_estimate=pl.CostEstimate(flops=30 * 10**9, bytes_accessed=30 << 20, transcendentals=2 << 20),
-    )(head_rows, full, turned, others, inputs, cotangent, cotangent, gain)
+    )(head_rows, head_rows, far_rows, full, turned, others, inputs, cotangent, cotangent, gain)
 
 
 def zeros_below(value):
@@ -1331,6 +1250,7 @@
     out_weight_ref,
     own_ref,
     taps_ref,
+    head_gain_ref,
     pack_ref,
     first_ref,
     pre_ref,
@@ -1345,9 +1265,16 @@
     inv_ref,
     wu_ref,
     mq_ref,
+    total_ref,
+    delta_ref,
+    rows_ref,
+    far_rows_ref,
+    states_ref,
     start_ref,
     out0_ref,
-    total_ref,
+    state_ref,
+    part_ref,
+    slots_ref,
     pad_ref,
     edge_ref,
     pack_send,
@@ -1360,6 +1287,14 @@
     full_recv,
     head_send,
     head_recv,
+    state_send,
+    state_recv,
+    row_near_send,
+    row_near_recv,
+    row_far_send,
+    row_far_recv,
+    row_pass_send,
+    row_pass_recv,
 ):
     tokens, width = input_ref.shape
     columns = heads * CHUNK
@@ -1372,6 +1307,19 @@
     @pl.when(member > 0)
     def _():
         pl.semaphore_signal(barrier, inc=1, device_id={"seq": member - 1}, device_id_type=MESH)
+
+    window = slots_ref.shape[0]
+    behind = members - 1 - member
+    for hop in range(1, window + 1):
+
+        @pl.when(member >= hop)
+        def _():
+            pl.semaphore_signal(barrier, inc=1, device_id={"seq": member - hop}, device_id_type=MESH)
+
+    def state_copy(hop):
+        return push(
+            part_ref, slots_ref.at[hop - 1], state_send.at[hop - 1], state_recv.at[hop - 1], "seq", member + hop
+        )
 
     pack_ref[0, member, :, :columns] = query_ref[...]
     pack_ref[0, member, :, columns : 2 * columns] = key_ref[...]
@@ -1386,7 +1334,7 @@
     near_copy = push(turned_ref.at[0], others_ref.at[0], head_send.at[0], head_recv.at[0], "head", near)
     far_copy = push(turned_ref.at[0], others_ref.at[1], head_send.at[1], head_recv.at[1], "head", far)
     pass_copy = push(others_ref.at[1], others_ref.at[2], head_send.at[2], head_recv.at[2], "head", near)
-    pl.semaphore_wait(barrier, stages + 2 + jnp.minimum(members - 1 - member, 1))
+    pl.semaphore_wait(barrier, stages + 2 + jnp.minimum(behind, 1) + jnp.minimum(behind, window))
     pack[0]()
     turned[0]()
     full[0](0, [stages - 1, 0])
@@ -1508,7 +1456,8 @@
         return carry
 
     count = resets_ref.shape[0] // 2 // batch
-    relays = full[2]
+    held = 3 if len(full[2]) > 3 else 0
+    relays = full[2][: len(full[2]) - held]
 
     def pumped(step, carry):
         carry = one(step, carry)
@@ -1528,6 +1477,66 @@
         return carry
 
     lax.fori_loop(0, count, pumped, 0)
+    part_ref[...] = total_ref[...].astype(BF)
+    for hop in range(1, window + 1):
+
+        @pl.when(behind >= hop)
+        def _():
+            state_copy(hop).start()
+
+    for job in full[2][len(full[2]) - held :]:
+        full[1](*job)
+    state_ref[...] = jnp.zeros_like(state_ref)
+    for hop in range(window, 0, -1):
+
+        @pl.when(member >= hop)
+        def _():
+            state_copy(hop).wait_recv()
+            for head in range(heads):
+                part = slots_ref[hop - 1, head]
+                state_ref[head] = nn(part[:, :CHUNK], state_ref[head]) + part[:, CHUNK:].astype(F32)
+
+    def near_rows(index):
+        return push(
+            rows_ref.at[at(index)], far_rows_ref.at[0, at(index)], row_near_send.at[index], row_near_recv.at[index], "head", near
+        )
+
+    def far_rows(index):
+        return push(
+            rows_ref.at[at(index)], far_rows_ref.at[1, at(index)], row_far_send.at[index], row_far_recv.at[index], "head", far
+        )
+
+    def pass_rows(index):
+        return push(
+            far_rows_ref.at[1, at(index)], far_rows_ref.at[2, at(index)], row_pass_send.at[index], row_pass_recv.at[index], "head", near
+        )
+
+    def finished(index):
+        for lane in range(chunk // CHUNK):
+            place_ = index * (chunk // CHUNK) + lane
+            rows_at = pl.ds(pl.multiple_of(place_ * CHUNK, CHUNK), CHUNK)
+            begins = [start_ref[place_, head] for head in range(heads)]
+            states = [
+                (nn(begins[head][:, :CHUNK], state_ref[head]) + begins[head][:, CHUNK:].astype(F32)).astype(BF)
+                for head in range(heads)
+            ]
+            outs = [out0_ref[place_, head] + nn(mq_ref[place_, head, CHUNK:], states[head]) for head in range(heads)]
+            for head in range(heads):
+                lanes = slice(head * CHUNK, (head + 1) * CHUNK)
+                states_ref[place_, head] = states[head]
+                delta_ref[rows_at, lanes] = outs[head]
+                scale = lax.rsqrt(jnp.mean(outs[head] * outs[head], axis=-1, keepdims=True) + 1e-05)
+                rows_ref[rows_at, lanes] = (outs[head] * scale * head_gain_ref[...]).astype(BF)
+        far_rows(index).start()
+        near_rows(index).start()
+
+    pl.loop(0, tokens // chunk)(finished)
+
+    @pl.loop(0, tokens // chunk)
+    def _(index):
+        far_rows(index).wait_recv()
+        pass_rows(index).start()
+
     near_copy.wait()
     far_copy.wait_send()
     pass_copy.wait()
@@ -1537,16 +1546,29 @@
     def _():
         edge(member + 1).wait_send()
 
+    for hop in range(1, window + 1):
+
+        @pl.when(behind >= hop)
+        def _():
+            state_copy(hop).wait_send()
+
+    @pl.loop(0, tokens // chunk)
+    def _(index):
+        near_rows(index).wait()
+        far_rows(index).wait_send()
+        pass_rows(index).wait()
+
     for gather in (pack, turned, full):
         gather[4]()
 
 
-def front_stage(resets, inputs, query, key, value, extra, out_weight, own, taps, members, heads, collective):
+def front_stage(resets, inputs, query, key, value, extra, out_weight, own, taps, head_gain, members, heads, collective):
     tokens, width = inputs.shape
     columns = heads * CHUNK
     chunks = tokens // CHUNK
     whole = pl.BlockSpec(memory_space=pltpu.VMEM)
     piece = width // members
+    window = min(members - 1, members // 2)
 
     def units(wide, kind):
         return jax.ShapeDtypeStruct((chunks, heads, *wide), kind)
@@ -1572,23 +1594,35 @@
             units((CHUNK, CHUNK), BF),
             units((CHUNK, 2 * CHUNK), BF),
             units((2 * CHUNK, CHUNK), BF),
-            units((CHUNK, 2 * CHUNK), BF),
-            units((CHUNK, CHUNK), F32),
             jax.ShapeDtypeStruct((heads, CHUNK, 2 * CHUNK), F32),
+            jax.ShapeDtypeStruct((tokens, columns), F32),
+            jax.ShapeDtypeStruct((tokens, columns), BF),
+            jax.ShapeDtypeStruct((3, tokens, columns), BF),
+            units((CHUNK, CHUNK), BF),
         ),
-        in_specs=[pl.BlockSpec(memory_space=pltpu.SMEM)] + [whole] * 8,
-        out_specs=(whole,) * 17,
-        scratch_shapes=[pltpu.VMEM((2, 144, 3 * columns), F32), pltpu.VMEM((16, width), BF)]
+        in_specs=[pl.BlockSpec(memory_space=pltpu.SMEM)] + [whole] * 9,
+        out_specs=(whole,) * 19,
+        scratch_shapes=[
+            pltpu.VMEM((chunks, heads, CHUNK, 2 * CHUNK), BF),
+            pltpu.VMEM((chunks, heads, CHUNK, CHUNK), F32),
+            pltpu.VMEM((heads, CHUNK, CHUNK), F32),
+            pltpu.VMEM((heads, CHUNK, 2 * CHUNK), BF),
+            pltpu.VMEM((window, heads, CHUNK, 2 * CHUNK), BF),
+            pltpu.VMEM((2, 144, 3 * columns), F32),
+            pltpu.VMEM((16, width), BF),
+        ]
         + dma(1, members)
         + dma()
         + dma(1, members)
         + dma(own.shape[0], members)
-        + dma(3),
+        + dma(3)
+        + dma(window)
+        + dma(tokens // 256) * 3,
         compiler_params=pltpu.CompilerParams(
             collective_id=collective, has_side_effects=True, vmem_limit_bytes=VMEM_LIMIT
         ),
         cost_estimate=pl.CostEstimate(flops=8 * 10**9, bytes_accessed=40 << 20, transcendentals=2 << 20),
-    )(resets, inputs, query, key, value, extra, out_weight, own, taps)
+    )(resets, inputs, query, key, value, extra, out_weight, own, taps, head_gain)
 
 
 def lanes_whole(pieces):
@@ -1641,6 +1675,7 @@
     resets = jnp.any(starts[None, :] == block_starts[:, None], axis=1).astype(F32)
 
     taps = conv_weight.astype(F32).transpose(1, 0, 2).reshape(4, -1)
+    gain_head = head_gain.astype(F32)[None, :]
     own = jnp.stack([gate_weight.T, up_weight.T, down_weight.T])
     split = piece < 128
     (
@@ -1658,9 +1693,11 @@
         inv,
         wu,
         mq,
-        start,
-        out0,
         total,
+        delta,
+        head_rows,
+        far_rows,
+        states,
     ) = front_stage(
         resets,
         block_input,
@@ -1671,6 +1708,7 @@
         output_weight.T,
         own[:1, :16] if split else own,
         taps,
+        gain_head,
         members,
         heads,
         5,
@@ -1682,12 +1720,8 @@
     turned = lanes_whole(turned[0])
     others = jnp.stack([lanes_whole(others[i]) for i in range(3)]) if split else others
     total_low = total.astype(BF)
-    (state,) = exchange(total_low, (), "seq", False, 0)
-    gain_head = head_gain.astype(F32)[None, :]
-    delta, head_rows, states = mixer_output(state, start, mq, out0, gain_head)
-
     d_heads, update_part, middle_shard, d_middle_shard, *grads, second_grad = middle_stage(
-        head_rows, full, turned, others, block_input, cotangent, gains[1:2], 2
+        head_rows, far_rows, full, turned, others, block_input, cotangent, gains[1:2], 2
     )
     second_part = jnp.sum(second_grad, 0)
     ddelta, gain_part, shift = mixer_back_state(d_heads, delta, gain_head, mq)

time: 401 us -> 376 us (0.938)
  Pallas kernels: 368 us -> 343 us
    pallas_call x1, Pallas kernels: 94.9 us -> 74.9 us  [middle_stage(): pl.pallas_call(functools.partial(middle_kernel, steps), name='middle', gr...]
    pallas_call x1, Pallas kernels: 101 us -> 110 us  [front_stage(): pl.pallas_call(functools.partial(front_kernel, members, heads), name='fro...]
    pallas_call x1 -> x0, Pallas kernels: 6.81 us -> none  [mixer_output(): pl.pallas_call(functools.partial(mixer_output_kernel, heads), name='mixer...]
    pallas_call x2 -> x1, Pallas kernels: 58.6 us -> 52.4 us  [exchange(): pl.pallas_call(functools.partial(exchange_kernel, axis, count, window, ba...]
where the time goes in v5:
time: 376 us; the launch traced here: 375 us
  Pallas kernels  343 us (91%)
  local copies, waits for them, and re-layouts  19.3 us (5%)
  other arithmetic  11.8 us (3%)
    pallas_call x1, Pallas kernels, front_stage(): pl.pallas_call(functools.partial(front_kernel, members, heads), name='fro...  110 us
    pallas_call x1, Pallas kernels, middle_stage(): pl.pallas_call(functools.partial(middle_kernel, steps), name='middle', gr...  74.9 us
    pallas_call x1, Pallas kernels, final_stage(): pl.pallas_call(functools.partial(final_kernel, members, chunk), name='fin...  52.5 us
    pallas_call x1, Pallas kernels, exchange(): pl.pallas_call(functools.partial(exchange_kernel, axis, count, window, ba...  52.4 us
    pallas_call x1, Pallas kernels, mixer_backward(): pl.pallas_call(functools.partial(mixer_backward_kernel, heads), name='mix...  44.1 us
    pallas_call x1, Pallas kernels, mixer_back_state(): pl.pallas_call(functools.partial(mixer_back_state_kernel, heads), name='m...  9.4 us
    unnamed x17, local copies, waits for them, and re-layouts  7.95 us

profile of v5, /device:TPU:0, one launch (start us, length us, event | category | flops | bytes accessed | tf_op | source)
XLA Modules:
  0.0 375.2 jit_solution(2695180444610917692)
XLA Ops:
  0.7 1.2 bitcast_convert_fusion.head_gain_ref.gain_ref
  1.8 0.8 select_reduce_fusion
  2.6 0.7 sub.3
  4.0 1.3 reshape.71
  5.2 0.8 copy.46
  6.0 0.8 copy.45
  6.8 0.8 copy.47
  7.6 0.7 maximum_maximum_fusion.extra_ref
  8.3 1.6 copy.48
  9.9 2.0 pad_maximum_fusion.own_ref
  11.8 110.0 %front.1 = (bf16[1,8,128,896]{3,2,1,0:T(8,128)(2,1)}, bf16[2048,1024]{1,0:T(8,128)(2,1)}, bf16[2048,768]{1,0:T(8,128)(2,1)}, f32[2048,128]{1,0:T(8,128)}, bf16[1...) custom-call(f32[32]{0:T(128)} %convert_element_type.13.resets_ref, ...), custom_call_target="tpu_custom_call" | custom-call | flops 8000000000 | bytes 41943040 | tf_op jit(solution)/shard_map/front/pallas_call | solution.py:1579
  121.8 1.1 copy.49
  122.9 1.4 fusion.5
  124.3 74.9 %middle.1 = (bf16[2048,256]{1,0:T(8,128)(2,1)}, bf16[2048,1024]{1,0:T(8,128)(2,1)}, f32[2048,256]{1,0:T(8,128)}, f32[2048,256]{1,0:T(8,128)}, bf16[2,8,576,128]{...) custom-call(bf16[2048,256]{1,0:T(8,128)(2,1)} %get-tuple-element.55.row, ...), custom_call_target="tpu_custom_call" | custom-call | flops 30000001024 | bytes 31457280 | tf_op jit(solution)/shard_map/middle/pallas_call | solution.py:769
  199.1 9.4 %mixer_back_state.1 = (bf16[2048,256]{1,0:T(8,128)(2,1)}, f32[8,128]{1,0:T(8,128)}, f32[2,128,128]{2,1,0:T(8,128)}) custom-call(bf16[2048,256]{1,0:T(8,128)(2,1)} %get-tuple-element.61.dheads_ref, f32[2048,256]{1,0:T(8,128)} %get-tuple-element.62.delta_ref, f32[1,128]{1,0:T(1,128)} %bitcast_convert_fusion.head_gain_ref.gain_ref, ...), custom_call_target="tpu_custom_call" | custom-call | flops 300000000 | bytes 10485760 | tf_op jit(solution)/shard_map/mixer_back_state/pallas_call | solution.py:260
  208.5 0.9 convert_element_type.15
  209.5 0.7 pad_maximum_fusion.3.refs_0_
  210.1 52.4 %state_backward.1 = (f32[2,128,128]{2,1,0:T(8,128)}, bf16[2048,256]{1,0:T(8,128)(2,1)}, f32[2,400,128]{2,1,0:T(8,128)}) custom-call(bf16[2,128,256]{2,1,0:T(8,128)(2,1)} %pad_maximum_fusion.3.refs_0_, bf16[2048,1024]{1,0:T(8,128)(2,1)} %get-tuple-element.65.refs_1_, f32[2048,256]{1,0:T(8,128)} %get-tuple-element.66.refs_2_, ...), custom_call_target="tpu_custom_call" | custom-call | flops 1000000000 | bytes 20971520 | tf_op jit(solution)/shard_map/state_backward/pallas_call | solution.py:218
  262.6 44.1 %mixer_backward.1 = (bf16[2048,896]{1,0:T(8,128)(2,1)}, f32[4,8,768]{2,1,0:T(8,128)}, f32[2,576,128]{2,1,0:T(8,128)}) custom-call(f32[32]{0:T(128)} %convert_element_type.13.resets_ref, bf16[2048,768]{1,0:T(8,128)(2,1)} %get-tuple-element.70.pre_ref, bf16[16,768]{1,0:T(8,128)(2,1)} %get-tuple-element.71.halo_ref, f32[4,768]{1,0:T(4,128)} %bitcast.52, ...), custom_call_target="tpu_custom_call" | custom-call | flops 3000000000 | bytes 20971520 | tf_op jit(solution)/shard_map/mixer_backward/pallas_call | solution.py:521
  306.8 0.9 reduce_sum.39
  307.8 1.3 concatenate.18.small_ref
  309.1 52.5 %final.1 = (f32[2048,256]{1,0:T(8,128)}, f32[128,896]{1,0:T(8,128)}, f32[16,1024]{1,0:T(8,128)}, f32[2,208,128]{2,1,0:T(8,128)}) custom-call(bf16[2048,1024]{1,0:T(8,128)(2,1)} %get-tuple-element.69.rows_ref, bf16[2048,896]{1,0:T(8,128)(2,1)} %get-tuple-element.80.dpre_ref, bf16[1024,896]{1,0:T(8,128)(2,1)} %bitcast.57, bf16[2048,1024]{1,0:T(8,128)(2,1)} %input_ref.5, ...), custom_call_target="tpu_custom_call" | custom-call | flops 8000000000 | bytes 31457280 | tf_op jit(solution)/shard_map/final/pallas_call | solution.py:1130
  361.6 1.2 slice_bitcast_fusion.2
  362.8 0.8 fusion.4
  363.6 0.8 slice.55
  365.5 0.8 slice.54
  366.3 1.8 fusion.3
  368.1 0.6 copy.50
  368.8 2.1 fusion.1
  370.9 0.8 copy.52
  371.6 2.3 copy.55
  373.9 1.3 copy.56
  (27 shorter events, 1.9 us)
Async XLA Ops:
  262.6 44.2 %copy-start.4 = (f32[8,128]{1,0:T(8,128)S(1)}, f32[8,128]{1,0:T(8,128)}, u32[]{:S(2)}) copy-start(f32[8,128]{1,0:T(8,128)} %get-tuple-element.84) | copy-start | bytes 12292
  262.6 44.2 %copy-start.3 = (f32[8,1024]{1,0:T(8,128)S(1)}, f32[8,1024]{1,0:T(8,128)}, u32[]{:S(2)}) copy-start(f32[8,1024]{1,0:T(8,128)} %get-tuple-element.85) | copy-start | bytes 98308
  309.1 59.6 %copy-start.2 = (f32[2,400,128]{2,1,0:T(8,128)S(1)}, f32[2,400,128]{2,1,0:T(8,128)}, u32[]{:S(2)}) copy-start(f32[2,400,128]{2,1,0:T(8,128)} %get-tuple-element.91) | copy-start | bytes 1228804
  309.1 59.7 %copy-start.1 = (f32[2,576,128]{2,1,0:T(8,128)S(1)}, f32[2,576,128]{2,1,0:T(8,128)}, u32[]{:S(2)}) copy-start(f32[2,576,128]{2,1,0:T(8,128)} %get-tuple-element.92) | copy-start | bytes 1769476
  368.8 5.1 %copy-start = (f32[2048,256]{1,0:T(8,128)S(1)}, f32[2048,256]{1,0:T(8,128)}, u32[]{:S(2)}) copy-start(f32[2048,256]{1,0:T(8,128)} %get-tuple-element.163) | copy-start | bytes 6291460

commit v6 on v5

--- a/solution.py
+++ b/solution.py
@@ -47,6 +47,26 @@
     rows = lax.broadcasted_iota(jnp.int32, (CHUNK, CHUNK), 0)
     cols = lax.broadcasted_iota(jnp.int32, (CHUNK, CHUNK), 1)
     return rows, cols
+
+
+def fill_resets(lengths_ref, resets_ref, tokens):
+    base = lax.axis_index("seq") * tokens
+
+    @pl.loop(0, tokens // GROUP)
+    def _(block):
+        position = base + block * GROUP
+        value = jnp.float32(0.0)
+        start = jnp.int32(0)
+        for index in range(lengths_ref.shape[0]):
+            value = jnp.where(start == position, 1.0, value)
+            start = start + lengths_ref[index]
+        resets_ref[block] = value
+
+
+def fill_taps(conv_ref, taps_ref):
+    columns = conv_ref.shape[2]
+    for kind in range(3):
+        taps_ref[:, kind * columns : (kind + 1) * columns] = conv_ref[kind].astype(F32)
 
 
 def load_padded(pad_ref, pre_ref, halo_ref, chunk, resets_ref):
@@ -93,181 +113,180 @@
     return results
 
 
-def exchange_kernel(axis, count, window, backward, *refs):
-    if backward:
-        (
-            part_ref, update_ref, mid_ref, grads_ref, state_ref, block_ref, total_ref, slots_ref, send_sem, recv_sem,
-            near_ref, relay_ref, far_ref, *sems, piece_relay, piece_slots, piece_send, piece_recv,
-        ) = refs
-        begin, receive, jobs, end = piece_scatter(
-            grads_ref, piece_relay, piece_slots, total_ref, piece_send, piece_recv, count
-        )
-        _, _, near, far = head_peers()
-        chunk = 256
-        steps = update_ref.shape[0] // chunk
-        at, _, start_pair, pass_on, own_sum, finish = head_scatter_copies(
-            chunk, update_ref, near_ref, relay_ref, far_ref, sems
-        )
-    else:
-        part_ref, state_ref, slots_ref, send_sem, recv_sem = refs
-    place = lax.axis_index(axis)
-    ahead = count - 1 - place if backward else place
-    behind = count - 1 - ahead
-    sign = -1 if backward else 1
-    barrier = pltpu.get_barrier_semaphore()
-    for hop in range(1, window + 1):
-
-        @pl.when(ahead >= hop)
-        def _():
-            pl.semaphore_signal(
-                barrier, inc=1, device_id={axis: place - sign * hop}, device_id_type=MESH
-            )
-
-    extra = 0
-    if backward:
-        extra = 2 + greet_seq(count)[1]
-        for target in (near, far):
-            pl.semaphore_signal(barrier, inc=1, device_id={"head": target}, device_id_type=MESH)
-
-    if extra:
-        pl.semaphore_wait(barrier, jnp.minimum(behind, window) + extra)
-    else:
-
-        @pl.when(behind > 0)
-        def _():
-            pl.semaphore_wait(barrier, jnp.minimum(behind, window))
-
-    def copy(hop):
-        return push(
-            part_ref,
-            slots_ref.at[hop - 1],
-            send_sem.at[hop - 1],
-            recv_sem.at[hop - 1],
-            axis,
-            place + sign * hop,
-        )
-
+def state_backward_kernel(
+    heads,
+    window,
+    dheads_ref,
+    delta_ref,
+    gain_ref,
+    mq_ref,
+    total_ref,
+    update_ref,
+    mid_ref,
+    grads_ref,
+    ddelta_ref,
+    gain_grad_ref,
+    state_ref,
+    block_ref,
+    sum_ref,
+    shift_ref,
+    part_ref,
+    slots_ref,
+    send_sem,
+    recv_sem,
+    near_ref,
+    relay_ref,
+    far_ref,
+    near_send,
+    near_recv,
+    far_send,
+    far_recv,
+    piece_relay,
+    piece_slots,
+    piece_send,
+    piece_recv,
+):
+    member, members = lax.axis_index("seq"), lax.axis_size("seq")
+    _, _, near, far = head_peers()
+    chunk = 256
+    steps = update_ref.shape[0] // chunk
+    chunks = mq_ref.shape[0]
+    behind = members - 1 - member
+    at, _, start_pair, pass_on, own_sum, finish = head_scatter_copies(
+        chunk, update_ref, near_ref, relay_ref, far_ref, (near_send, near_recv, far_send, far_recv)
+    )
+    begin, receive, jobs, end = piece_scatter(
+        grads_ref, piece_relay, piece_slots, sum_ref, piece_send, piece_recv, members
+    )
+    barrier, stages = greet_seq(members)
     for hop in range(1, window + 1):
 
         @pl.when(behind >= hop)
         def _():
-            copy(hop).start()
-
-    if backward:
-
-        @pl.loop(0, steps)
-        def _(index):
-            start_pair(index)
-
-        begin()
-
-        @pl.loop(0, steps)
-        def _(index):
-            pass_on(index)
-
-        for job in jobs[: len(jobs) // 2]:
-            receive(*job)
-
-    heads = state_ref.shape[0]
-    state_ref[...] = jnp.zeros_like(state_ref)
-    for hop in range(window, 0, -1):
-
-        @pl.when(ahead >= hop)
-        def _():
-            copy(hop).wait_recv()
-            for head in range(heads):
-                part = slots_ref[hop - 1, head]
-                state_ref[head] = nn(part[:, :CHUNK], state_ref[head]) + part[:, CHUNK:].astype(F32)
-
-    if backward:
-        for job in jobs[len(jobs) // 2 :]:
-            receive(*job)
-
-        @pl.loop(0, steps)
-        def _(index):
-            block_ref[at(index)] = (mid_ref[at(index)] + own_sum(index)).astype(BF)
-            finish(index)
-
-        end()
-
-    for hop in range(1, window + 1):
-
-        @pl.when(behind >= hop)
-        def _():
-            copy(hop).wait_send()
-
-
-def exchange(part, extras, axis, backward, collective):
-    count = lax.axis_size(axis)
-    window = min(count - 1, count // 2)
-    heads = part.shape[0]
-    whole = pl.BlockSpec(memory_space=pltpu.VMEM)
-    out_shape = [jax.ShapeDtypeStruct((heads, CHUNK, CHUNK), F32)]
-    scratch = [
-        pltpu.VMEM((window, heads, CHUNK, 2 * CHUNK), BF),
-        pltpu.SemaphoreType.DMA((window,)),
-        pltpu.SemaphoreType.DMA((window,)),
-    ]
-    if backward:
-        tokens, columns = extras[1].shape
-        out_shape.append(jax.ShapeDtypeStruct((tokens, columns), BF))
-        scratch += head_scatter_scratch(tokens, columns, tokens // 256)
-        parts, _, *piece = extras[2].shape
-        out_shape.append(jax.ShapeDtypeStruct((parts, *piece), F32))
-        scratch += piece_scatter_scratch(parts, count, piece)
-    return pl.pallas_call(
-        functools.partial(exchange_kernel, axis, count, window, backward),
-        name="state_backward" if backward else "state_forward",
-        out_shape=out_shape,
-        in_specs=[whole] * (1 + len(extras)),
-        out_specs=[whole] * len(out_shape),
-        scratch_shapes=scratch,
-        compiler_params=pltpu.CompilerParams(
-            collective_id=collective, has_side_effects=True, vmem_limit_bytes=VMEM_LIMIT
-        ),
-        cost_estimate=pl.CostEstimate(flops=10**9, bytes_accessed=20 << 20, transcendentals=0),
-    )(part, *extras)
-
-
-def mixer_back_state_kernel(heads, dheads_ref, delta_ref, gain_ref, mq_ref, ddelta_ref, gain_grad_ref, shift_ref):
-    chunks = mq_ref.shape[0]
+            pl.semaphore_signal(barrier, inc=1, device_id={"seq": member + hop}, device_id_type=MESH)
+
+    for target in (near, far):
+        pl.semaphore_signal(barrier, inc=1, device_id={"head": target}, device_id_type=MESH)
+    pl.semaphore_wait(barrier, stages + 2 + jnp.minimum(member, window))
+
+    @pl.loop(0, steps)
+    def _(index):
+        start_pair(index)
+
+    for head in range(heads):
+        part_ref[0, head] = total_ref[head, :, :CHUNK].T.astype(BF)
+
+    def copy(kind, hop):
+        return push(
+            part_ref.at[kind],
+            slots_ref.at[kind, hop - 1],
+            send_sem.at[kind, hop - 1],
+            recv_sem.at[kind, hop - 1],
+            "seq",
+            member - hop,
+        )
+
+    def send(kind):
+        for hop in range(1, window + 1):
+
+            @pl.when(member >= hop)
+            def _():
+                copy(kind, hop).start()
+
+    send(0)
+    half = len(jobs) // 4
+    begin(jobs[:half])
     shift_ref[...] = jnp.zeros_like(shift_ref)
     gain_grad_ref[...] = jnp.zeros_like(gain_grad_ref)
 
     def one(step, carry):
-        chunk = chunks - 1 - step
-        at = pl.ds(pl.multiple_of(chunk * CHUNK, CHUNK), CHUNK)
+        index = chunks - 1 - step
+        rows = pl.ds(pl.multiple_of(index * CHUNK, CHUNK), CHUNK)
         for head in range(heads):
-            window = slice(head * CHUNK, (head + 1) * CHUNK)
-            out = delta_ref[at, window]
-            grad = dheads_ref[at, window].astype(F32)
+            lanes = slice(head * CHUNK, (head + 1) * CHUNK)
+            out = delta_ref[rows, lanes]
+            grad = dheads_ref[rows, lanes].astype(F32)
             scale = lax.rsqrt(jnp.mean(out * out, axis=-1, keepdims=True) + 1e-05)
             unit = out * scale
             gain_grad_ref[...] += jnp.sum((grad * unit).reshape(CHUNK // 8, 8, CHUNK), 0)
             scaled = grad * gain_ref[...]
             back = scale * (scaled - unit * jnp.mean(scaled * unit, axis=-1, keepdims=True))
             back = back.astype(BF)
-            ddelta_ref[at, window] = back
-            shift_ref[head] = tn(mq_ref[chunk, head], stack(shift_ref[head].astype(BF), back))
+            ddelta_ref[rows, lanes] = back
+            shift_ref[head] = tn(mq_ref[index, head], stack(shift_ref[head].astype(BF), back))
+
+        @pl.when(lax.rem(step, 2) == 1)
+        def _():
+            pass_on(lax.div(step, 2))
+
         return carry
 
     lax.fori_loop(0, chunks, one, 0)
-
-
-def mixer_back_state(dheads, delta, gain, mq):
+    for head in range(heads):
+        part_ref[1, head] = shift_ref[head].astype(BF)
+    send(1)
+    begin(jobs[half:])
+    for job in jobs[: len(jobs) // 2]:
+        receive(*job)
+    state_ref[...] = jnp.zeros_like(state_ref)
+    for hop in range(window, 0, -1):
+
+        @pl.when(behind >= hop)
+        def _():
+            copy(0, hop).wait_recv()
+            copy(1, hop).wait_recv()
+            for head in range(heads):
+                state_ref[head] = nn(slots_ref[0, hop - 1, head], state_ref[head]) + slots_ref[1, hop - 1, head].astype(F32)
+
+    for job in jobs[len(jobs) // 2 :]:
+        receive(*job)
+
+    @pl.loop(0, steps)
+    def _(index):
+        block_ref[at(index)] = (mid_ref[at(index)] + own_sum(index)).astype(BF)
+        finish(index)
+
+    end()
+    for hop in range(1, window + 1):
+
+        @pl.when(member >= hop)
+        def _():
+            copy(0, hop).wait_send()
+            copy(1, hop).wait_send()
+
+
+def state_backward(dheads, delta, gain, mq, total, update, mid, grads, members, collective):
     chunks, heads = mq.shape[:2]
-    tokens = chunks * CHUNK
+    tokens, columns = mid.shape
+    window = min(members - 1, members // 2)
+    whole = pl.BlockSpec(memory_space=pltpu.VMEM)
+    parts, _, *piece = grads.shape
     return pl.pallas_call(
-        functools.partial(mixer_back_state_kernel, heads),
-        name="mixer_back_state",
+        functools.partial(state_backward_kernel, heads, window),
+        name="state_backward",
         out_shape=(
-            jax.ShapeDtypeStruct((tokens, heads * CHUNK), BF),
+            jax.ShapeDtypeStruct((tokens, columns), BF),
             jax.ShapeDtypeStruct((8, CHUNK), F32),
             jax.ShapeDtypeStruct((heads, CHUNK, CHUNK), F32),
+            jax.ShapeDtypeStruct((tokens, columns), BF),
+            jax.ShapeDtypeStruct((parts, *piece), F32),
         ),
-        compiler_params=pltpu.CompilerParams(vmem_limit_bytes=VMEM_LIMIT),
-        cost_estimate=pl.CostEstimate(flops=3 * 10**8, bytes_accessed=10 << 20, transcendentals=1 << 14),
-    )(dheads, delta, gain, mq)
+        in_specs=[whole] * 8,
+        out_specs=(whole,) * 5,
+        scratch_shapes=[
+            pltpu.VMEM((heads, CHUNK, CHUNK), F32),
+            pltpu.VMEM((2, heads, CHUNK, CHUNK), BF),
+            pltpu.VMEM((2, window, heads, CHUNK, CHUNK), BF),
+            pltpu.SemaphoreType.DMA((2, window)),
+            pltpu.SemaphoreType.DMA((2, window)),
+        ]
+        + head_scatter_scratch(tokens, columns, tokens // 256)
+        + piece_scatter_scratch(parts, members, piece),
+        compiler_params=pltpu.CompilerParams(
+            collective_id=collective, has_side_effects=True, vmem_limit_bytes=VMEM_LIMIT
+        ),
+        cost_estimate=pl.CostEstimate(flops=10**9, bytes_accessed=30 << 20, transcendentals=0),
+    )(dheads, delta, gain, mq, total, update, mid, grads)
 
 
 def piece_scatter_scratch(parts, members, piece):
@@ -309,8 +328,8 @@
 
     jobs = [(part, r) for r in order if r % 2 == 0 for part in range(parts)]
 
-    def begin():
-        for part, r in jobs:
+    def begin(some=None):
+        for part, r in jobs if some is None else some:
             give(part, r ^ 1).start()
 
     def receive(part, r):
@@ -335,10 +354,23 @@
 
 def mixer_backward_kernel(
     heads,
-    resets_ref,
+    lengths_ref,
+    pre_hbm,
+    halo_ref,
+    conv_ref,
+    logits_hbm,
+    qkv_hbm,
+    inv_hbm,
+    wu_hbm,
+    mq_hbm,
+    states_hbm,
+    ddelta_hbm,
+    arrive_ref,
+    grads_ref,
+    dpre_ref,
+    taps_grad_ref,
+    total_ref,
     pre_ref,
-    halo_ref,
-    taps_ref,
     logits_ref,
     qkv_ref,
     inv_ref,
@@ -346,11 +378,9 @@
     mq_ref,
     states_ref,
     ddelta_ref,
-    arrive_ref,
-    grads_ref,
-    dpre_ref,
-    taps_grad_ref,
-    total_ref,
+    load_sem,
+    resets_ref,
+    taps_ref,
     carry_ref,
     pad_ref,
     dpad_ref,
@@ -376,6 +406,23 @@
 
     columns = heads * CHUNK
     chunks = mq_ref.shape[0]
+    fill_resets(lengths_ref, resets_ref, pre_ref.shape[0])
+    fill_taps(conv_ref, taps_ref)
+    quarter = chunks // 4
+    sources = (pre_hbm, logits_hbm, qkv_hbm, ddelta_hbm, inv_hbm, wu_hbm, mq_hbm, states_hbm)
+    targets = (pre_ref, logits_ref, qkv_ref, ddelta_ref, inv_ref, wu_ref, mq_ref, states_ref)
+
+    def load(number, turn):
+        unit = CHUNK if number < 4 else 1
+        reach = pl.ds((chunks - (turn + 1) * quarter) * unit, quarter * unit)
+        return pltpu.make_async_copy(
+            sources[number].at[reach], targets[number].at[reach], load_sem.at[number, turn]
+        )
+
+    for turn in range(4):
+        for number in range(8):
+            load(number, turn).start()
+    load(0, 0).wait()
     rows, cols = grid_indices()
     top = lax.broadcasted_iota(jnp.int32, (CHUNK, 1), 0) < GROUP
     pl.semaphore_wait(barrier, stages + jnp.minimum(member, 1))
@@ -387,6 +434,15 @@
     def one(step, carry):
         chunk = chunks - 1 - step
         at = pl.ds(pl.multiple_of(chunk * CHUNK, CHUNK), CHUNK)
+        for turn in range(4):
+
+            @pl.when(step == turn * quarter)
+            def _():
+                for number in range(1, 8):
+                    load(number, turn).wait()
+                if turn < 3:
+                    load(0, turn + 1).wait()
+
         keep0 = 1.0 - resets_ref[2 * chunk]
         keep1 = 1.0 - resets_ref[2 * chunk + 1]
         both = keep0 * keep1
@@ -512,12 +568,14 @@
     finish()
 
 
-def mixer_backward(resets, pre, halo, taps, logits, qkv, inv, wu, mq, states, ddelta, arrive, grads, collective):
+def mixer_backward(lengths, pre, halo, conv, logits, qkv, inv, wu, mq, states, ddelta, arrive, grads, collective):
     chunks, heads = mq.shape[:2]
     tokens = chunks * CHUNK
     columns = heads * CHUNK
     parts, members = grads.shape[:2]
     piece = grads.shape[2:]
+    whole, outside = pl.BlockSpec(memory_space=pltpu.VMEM), pl.BlockSpec(memory_space=pl.ANY)
+    streamed = (pre, logits, qkv, inv, wu, mq, states, ddelta)
     return pl.pallas_call(
         functools.partial(mixer_backward_kernel, heads),
         name="mixer_backward",
@@ -526,9 +584,13 @@
             jax.ShapeDtypeStruct((4, 8, 3 * columns), F32),
             jax.ShapeDtypeStruct((parts, *piece), F32),
         ),
-        in_specs=[pl.BlockSpec(memory_space=pltpu.SMEM)] + [pl.BlockSpec(memory_space=pltpu.VMEM)] * 12,
+        in_specs=[pl.BlockSpec(memory_space=pltpu.SMEM), outside, whole, whole] + [outside] * 7 + [whole] * 2,
         out_specs=tuple([pl.BlockSpec(memory_space=pltpu.VMEM)] * 3),
-        scratch_shapes=[
+        scratch_shapes=[pltpu.VMEM(a.shape, a.dtype) for a in streamed]
+        + [
+            pltpu.SemaphoreType.DMA((8, 4)),
+            pltpu.SMEM((tokens // GROUP,), F32),
+            pltpu.VMEM((4, 3 * columns), F32),
             pltpu.VMEM((heads, CHUNK, CHUNK), F32),
             pltpu.VMEM((144, 3 * columns), F32),
             pltpu.VMEM((144, 3 * columns), F32),
@@ -543,7 +605,7 @@
             collective_id=collective, has_side_effects=True, vmem_limit_bytes=VMEM_LIMIT
         ),
         cost_estimate=pl.CostEstimate(flops=3 * 10**9, bytes_accessed=20 << 20, transcendentals=2 << 20),
-    )(resets, pre, halo, taps, logits, qkv, inv, wu, mq, states, ddelta, arrive, grads)
+    )(lengths, pre, halo, conv, logits, qkv, inv, wu, mq, states, ddelta, arrive, grads)
 
 
 def head_peers():
@@ -672,7 +734,7 @@
         mid_ref[...] = keep_ref[lax.rem(step, 4), :, own_columns]
         scale = lax.rsqrt(jnp.mean(middle * middle, axis=-1, keepdims=True) + 1e-06)
         scale_ref[lax.rem(step, 4)] = scale
-        second = (middle * scale * gain_ref[...]).astype(BF)
+        second = (middle * scale * gain_ref[1:2]).astype(BF)
         gate, up = nt(second, gate_ref[...]), nt(second, up_ref[...])
         sig = sigmoid(gate)
         silu = gate * sig
@@ -717,7 +779,7 @@
         scale = scale_ref[lax.rem(done, 4)]
         unit = middle * scale
         gain_grad_ref[...] += jnp.sum((grad * unit).reshape(chunk // 8, 8, width), 0)
-        scaled = grad * gain_ref[...]
+        scaled = grad * gain_ref[1:2]
         d_middle = late_ct_ref[...].astype(F32) + scale * (
             scaled - unit * jnp.mean(scaled * unit, axis=-1, keepdims=True)
         )
@@ -886,17 +948,24 @@
     chunk,
     rows_ref,
     dpre_ref,
-    pack_ref,
-    input_ref,
-    scale_ref,
+    pack_hbm,
+    input_hbm,
+    scale_hbm,
     gain_ref,
-    dmid_ref,
-    small_ref,
+    dmid_hbm,
+    head_part_ref,
+    second_part_ref,
+    taps_part_ref,
     rest_ref,
     ingrad_ref,
     piece_ref,
     sums_ref,
     total_ref,
+    pack_ref,
+    input_ref,
+    scale_ref,
+    dmid_ref,
+    load_sem,
     acc_ref,
     out_ref,
     slots_ref,
@@ -924,6 +993,14 @@
 ):
     tokens, width = input_ref.shape
     steps = tokens // chunk
+    loads = [
+        pltpu.make_async_copy(source, target, load_sem.at[number])
+        for number, (source, target) in enumerate(
+            ((pack_hbm, pack_ref), (input_hbm, input_ref), (scale_hbm, scale_ref), (dmid_hbm, dmid_ref))
+        )
+    ]
+    for load in loads:
+        load.start()
     place, low, near, far = head_peers()
     member = lax.axis_index("seq")
     rows = width // members
@@ -999,7 +1076,20 @@
             send_piece(r)
         begin()
 
-    small_slots[0] = small_ref[...]
+    small_slots[0] = jnp.zeros_like(small_slots[0])
+    small_slots[0, 1:2, :CHUNK] = jnp.sum(head_part_ref[...], 0, keepdims=True)
+    small_slots[0, 8:9] = jnp.sum(second_part_ref[...], 0, keepdims=True)
+    columns3 = taps_part_ref.shape[2]
+    for tap in range(4):
+        taps_sum = jnp.sum(taps_part_ref[tap], 0, keepdims=True)
+        for block in range(3):
+            flat = tap * columns3 + block * (columns3 // 3)
+            line, lane = 9 + flat // width, flat % width
+            small_slots[0, line : line + 1, lane : lane + columns3 // 3] = taps_sum[
+                :, block * (columns3 // 3) : (block + 1) * (columns3 // 3)
+            ]
+    for load in loads:
+        load.wait()
     diagonal = lax.broadcasted_iota(jnp.int32, (128, 128), 0) == lax.broadcasted_iota(jnp.int32, (128, 128), 1)
 
     def project(index):
@@ -1008,7 +1098,7 @@
         start_pair(index)
         seen = part * (input_ref[at(index)].astype(F32) * scale_ref[at(index)])
         small_slots[0, 0:1] += jnp.sum(seen, 0, keepdims=True)
-        stat = jnp.sum(seen * gain_ref[...], axis=-1, keepdims=True)
+        stat = jnp.sum(seen * gain_ref[0:1], axis=-1, keepdims=True)
         for block in range(chunk // 128):
             line = jnp.where(diagonal, stat[block * 128 : (block + 1) * 128], 0.0)
             stat_ref[index * (chunk // 128) + block] = jnp.sum(line, 0, keepdims=True)
@@ -1085,7 +1175,7 @@
             line = jnp.where(diagonal, stat_ref[index * (chunk // 128) + block], 0.0)
             means.append(jnp.sum(line, axis=-1, keepdims=True))
         mean = jnp.concatenate(means, 0) * (1.0 / width)
-        ingrad_ref[at(index)] = dmid_ref[at(index)] + scale * (grad * gain_ref[:, cols(place)] - unit * mean)
+        ingrad_ref[at(index)] = dmid_ref[at(index)] + scale * (grad * gain_ref[0:1, cols(place)] - unit * mean)
 
     rests = list(rest_jobs)
     for turn in range(stages):
@@ -1118,7 +1208,7 @@
     rest_end()
 
 
-def final_stage(first_rows, dpre, pack, inputs, scale, gain, dmid, small, rest, members, collective):
+def final_stage(first_rows, dpre, pack, inputs, scale, gain, dmid, parts, rest, members, collective):
     tokens, width = inputs.shape
     columns = dmid.shape[1]
     chunk = 256
@@ -1126,19 +1216,21 @@
     stages = (members - 1).bit_length()
     rows = width // members
     wide = dpre.shape[1]
-    whole = pl.BlockSpec(memory_space=pltpu.VMEM)
+    whole, outside = pl.BlockSpec(memory_space=pltpu.VMEM), pl.BlockSpec(memory_space=pl.ANY)
     return pl.pallas_call(
         functools.partial(final_kernel, members, chunk),
         name="final",
         out_shape=(
             jax.ShapeDtypeStruct((tokens, columns), F32),
             jax.ShapeDtypeStruct((rows, wide), F32),
-            jax.ShapeDtypeStruct(small.shape, F32),
+            jax.ShapeDtypeStruct((16, width), F32),
             jax.ShapeDtypeStruct((rest.shape[0], *rest.shape[2:]), F32),
         ),
-        in_specs=[whole] * 9,
+        in_specs=[whole, whole, outside, outside, outside, whole, outside] + [whole] * 4,
         out_specs=(whole,) * 4,
-        scratch_shapes=[
+        scratch_shapes=[pltpu.VMEM(a.shape, a.dtype) for a in (pack, inputs, scale, dmid)]
+        + [
+            pltpu.SemaphoreType.DMA((4,)),
             pltpu.VMEM((members, rows, wide), F32),
             pltpu.VMEM((members, rows, wide), BF),
             pltpu.VMEM((members - 1, rows, wide), BF),
@@ -1148,7 +1240,7 @@
         + [
             pltpu.VMEM((tokens // 128, 1, 128), F32),
             pltpu.VMEM((3, tokens // 128, 1, 128), F32),
-            pltpu.VMEM((5 + 2 * stages, *small.shape), F32),
+            pltpu.VMEM((5 + 2 * stages, 16, width), F32),
             pltpu.SemaphoreType.DMA((members,)),
             pltpu.SemaphoreType.DMA((members - 1,)),
             pltpu.SemaphoreType.DMA((3,)),
@@ -1161,7 +1253,117 @@
             collective_id=collective, has_side_effects=True, vmem_limit_bytes=VMEM_LIMIT
         ),
         cost_estimate=pl.CostEstimate(flops=8 * 10**9, bytes_accessed=30 << 20, transcendentals=0),
-    )(first_rows, dpre, pack, inputs, scale, gain, dmid, small, rest)
+    )(first_rows, dpre, pack, inputs, scale, gain, dmid, *parts, rest)
+
+
+def finish_kernel(
+    hidden,
+    block_ref,
+    ingrad_ref,
+    piece_ref,
+    sums_ref,
+    first_ref,
+    second_ref,
+    third_ref,
+    block_out,
+    ingrad_out,
+    first_gain_out,
+    query_out,
+    key_out,
+    value_out,
+    beta_out,
+    conv_out,
+    head_gain_out,
+    output_out,
+    second_gain_out,
+    gate_out,
+    up_out,
+    down_out,
+    turn_ref,
+    strip_ref,
+    sems,
+):
+    rows, columns = query_out.shape
+    member = lax.axis_index("seq")
+    pieces = [(block_ref, block_out), (ingrad_ref, ingrad_out)]
+    for kind, target in enumerate((query_out, key_out, value_out)):
+        pieces.append((piece_ref.at[:, pl.ds(kind * columns, columns)], target))
+    pieces.append((piece_ref.at[:, pl.ds(3 * columns, CHUNK)], strip_ref))
+    spans = []
+    place = 0
+    for source in (first_ref, second_ref, third_ref):
+        for part in range(2):
+            spans.append((place, source, part))
+            place += source.shape[1]
+    goal = 0
+    for target, count in ((gate_out, hidden), (up_out, hidden), (down_out, hidden), (turn_ref, columns)):
+        for begin, source, part in spans:
+            low, high = max(begin, goal), min(begin + source.shape[1], goal + count)
+            if low < high:
+                pieces.append(
+                    (source.at[part, pl.ds(low - begin, high - low)], target.at[pl.ds(low - goal, high - low)])
+                )
+        goal += count
+    copies = [pltpu.make_async_copy(source, target, sems.at[number]) for number, (source, target) in enumerate(pieces)]
+    for copy in copies:
+        copy.start()
+    window = pl.ds(pl.multiple_of(member * rows, 128), rows)
+    first_gain_out[...] = sums_ref[0:1, window]
+    second_gain_out[...] = sums_ref[8:9, window]
+    head_gain_out[...] = sums_ref[1:2, :CHUNK]
+    width = sums_ref.shape[1]
+    for kind in range(3):
+        for tap in range(4):
+            flat = (3 * tap + kind) * columns
+            line, lane = 9 + flat // width, flat % width
+            conv_out[kind, tap : tap + 1] = sums_ref[line : line + 1, lane : lane + columns]
+    for copy in copies:
+        copy.wait()
+    output_out[...] = turn_ref[...].T
+    beta_out[...] = strip_ref[...].T[: beta_out.shape[0]]
+
+
+def finish_stage(block, ingrad, piece, sums, first, second, third, hidden, heads):
+    tokens, columns = ingrad.shape
+    rows = piece.shape[0]
+    whole, outside = pl.BlockSpec(memory_space=pltpu.VMEM), pl.BlockSpec(memory_space=pl.ANY)
+
+    def made(*shape):
+        return jax.ShapeDtypeStruct(shape, F32)
+
+    return pl.pallas_call(
+        functools.partial(finish_kernel, hidden),
+        name="finish",
+        out_shape=(
+            jax.ShapeDtypeStruct((tokens, columns), BF),
+            made(tokens, columns),
+            made(1, rows),
+            made(rows, columns),
+            made(rows, columns),
+            made(rows, columns),
+            made(heads, rows),
+            made(3, 4, columns),
+            made(1, CHUNK),
+            made(rows, columns),
+            made(1, rows),
+            made(hidden, rows),
+            made(hidden, rows),
+            made(hidden, rows),
+        ),
+        in_specs=[outside] * 3 + [whole] + [outside] * 3,
+        out_specs=(outside,) * 2
+        + (whole,)
+        + (outside,) * 3
+        + (whole,) * 5
+        + (outside,) * 3,
+        scratch_shapes=[
+            pltpu.VMEM((columns, rows), F32),
+            pltpu.VMEM((rows, CHUNK), F32),
+            pltpu.SemaphoreType.DMA((24,)),
+        ],
+        compiler_params=pltpu.CompilerParams(vmem_limit_bytes=VMEM_LIMIT),
+        cost_estimate=pl.CostEstimate(flops=0, bytes_accessed=12 << 20, transcendentals=0),
+    )(block, ingrad, piece, sums, first, second, third)
 def turn_column(column):
     diagonal = lax.broadcasted_iota(jnp.int32, (128, 128), 0) == lax.broadcasted_iota(jnp.int32, (128, 128), 1)
     lines = []
@@ -1238,26 +1440,84 @@
     return barrier, stages
 
 
+FRONT_REFS = 64
+
+
 def front_kernel(
     members,
     heads,
-    resets_ref,
+    lengths_ref,
     input_ref,
     query_ref,
     key_ref,
     value_ref,
-    extra_ref,
+    beta_ref,
+    first_gain_ref,
+    second_gain_ref,
     out_weight_ref,
-    own_ref,
-    taps_ref,
+    conv_ref,
     head_gain_ref,
+    *refs,
+):
+    own_refs, refs = refs[:-FRONT_REFS], refs[-FRONT_REFS:]
+    front_body(
+        members,
+        heads,
+        lengths_ref,
+        input_ref,
+        query_ref,
+        key_ref,
+        value_ref,
+        beta_ref,
+        first_gain_ref,
+        second_gain_ref,
+        out_weight_ref,
+        conv_ref,
+        head_gain_ref,
+        own_refs,
+        *refs,
+    )
+
+
+def front_body(
+    members,
+    heads,
+    lengths_ref,
+    input_ref,
+    query_ref,
+    key_ref,
+    value_ref,
+    beta_ref,
+    first_gain_ref,
+    second_gain_ref,
+    out_weight_ref,
+    conv_ref,
+    head_gain_ref,
+    own_refs,
+    pack_hbm,
+    first_hbm,
+    pre_hbm,
+    logits_hbm,
+    halo_ref,
+    scale_hbm,
+    gains_ref,
+    turned_hbm,
+    full_hbm,
+    others_hbm,
+    qkv_hbm,
+    inv_hbm,
+    wu_hbm,
+    mq_hbm,
+    total_ref,
+    delta_hbm,
+    rows_hbm,
+    far_rows_hbm,
+    states_hbm,
     pack_ref,
     first_ref,
     pre_ref,
     logits_ref,
-    halo_ref,
     scale_ref,
-    gains_ref,
     turned_ref,
     full_ref,
     others_ref,
@@ -1265,11 +1525,14 @@
     inv_ref,
     wu_ref,
     mq_ref,
-    total_ref,
     delta_ref,
     rows_ref,
     far_rows_ref,
     states_ref,
+    store_sem,
+    resets_ref,
+    taps_ref,
+    extra_ref,
     start_ref,
     out0_ref,
     state_ref,
@@ -1298,6 +1561,28 @@
 ):
     tokens, width = input_ref.shape
     columns = heads * CHUNK
+    leaving = (
+        (pack_ref, pack_hbm),
+        (first_ref, first_hbm),
+        (pre_ref, pre_hbm),
+        (logits_ref, logits_hbm),
+        (scale_ref, scale_hbm),
+        (turned_ref, turned_hbm),
+        (qkv_ref, qkv_hbm),
+        (inv_ref, inv_hbm),
+        (wu_ref, wu_hbm),
+        (mq_ref, mq_hbm),
+        (delta_ref, delta_hbm),
+        (rows_ref, rows_hbm),
+        (states_ref, states_hbm),
+        (others_ref, others_hbm),
+        (far_rows_ref, far_rows_hbm),
+        (full_ref, full_hbm),
+    )
+
+    def store(number):
+        return pltpu.make_async_copy(*leaving[number], store_sem.at[number])
+
     member = lax.axis_index("seq")
     _, _, near, far = head_peers()
     barrier, stages = greet_seq(members)
@@ -1324,10 +1609,14 @@
     pack_ref[0, member, :, :columns] = query_ref[...]
     pack_ref[0, member, :, columns : 2 * columns] = key_ref[...]
     pack_ref[0, member, :, 2 * columns : 3 * columns] = value_ref[...]
-    pack_ref[0, member, :, 3 * columns :] = extra_ref[...]
-    turned_ref[0, member] = out_weight_ref[...]
-    for part in range(full_ref.shape[0]):
-        full_ref[part, member] = own_ref[part]
+    extra_ref[...] = jnp.zeros_like(extra_ref)
+    extra_ref[0:heads] = beta_ref[...].astype(F32)
+    extra_ref[heads : heads + 1] = first_gain_ref[...].astype(F32)
+    extra_ref[heads + 1 : heads + 2] = second_gain_ref[...].astype(F32)
+    pack_ref[0, member, :, 3 * columns :] = extra_ref[...].T.astype(BF)
+    turned_ref[0, member] = out_weight_ref[...].T
+    for part, own_ref in enumerate(own_refs):
+        full_ref[part, member] = own_ref[...]
     pack = piece_gather(pack_ref, pack_send, pack_recv, members)
     turned = piece_gather(turned_ref, turned_send, turned_recv, members)
     full = piece_gather(full_ref, full_send, full_recv, members)
@@ -1338,6 +1627,8 @@
     pack[0]()
     turned[0]()
     full[0](0, [stages - 1, 0])
+    fill_resets(lengths_ref, resets_ref, tokens)
+    fill_taps(conv_ref, taps_ref)
 
     last_rows = pl.ds(tokens - 16, 16)
 
@@ -1391,6 +1682,8 @@
         halo_ref[...] = nn(first, pack_ref[0].reshape(width, pack_ref.shape[3])[:, : 3 * columns]).astype(BF)
 
     turned[3]()
+    for number in range(6):
+        store(number).start()
     near_copy.start()
     far_copy.start()
     rows, cols = grid_indices()
@@ -1477,6 +1770,8 @@
         return carry
 
     lax.fori_loop(0, count, pumped, 0)
+    for number in range(6, 10):
+        store(number).start()
     part_ref[...] = total_ref[...].astype(BF)
     for hop in range(1, window + 1):
 
@@ -1531,6 +1826,8 @@
         near_rows(index).start()
 
     pl.loop(0, tokens // chunk)(finished)
+    for number in range(10, 13):
+        store(number).start()
 
     @pl.loop(0, tokens // chunk)
     def _(index):
@@ -1540,7 +1837,7 @@
     near_copy.wait()
     far_copy.wait_send()
     pass_copy.wait()
-    full[3]()
+    store(13).start()
 
     @pl.when(member + 1 < members)
     def _():
@@ -1558,11 +1855,16 @@
         far_rows(index).wait_send()
         pass_rows(index).wait()
 
+    store(14).start()
+    full[3]()
+    store(15).start()
     for gather in (pack, turned, full):
         gather[4]()
-
-
-def front_stage(resets, inputs, query, key, value, extra, out_weight, own, taps, head_gain, members, heads, collective):
+    for number in range(len(leaving)):
+        store(number).wait()
+
+
+def front_stage(lengths, inputs, mixer_weights, conv, head_gain, own, members, heads, collective):
     tokens, width = inputs.shape
     columns = heads * CHUNK
     chunks = tokens // CHUNK
@@ -1576,33 +1878,41 @@
     def dma(*shape):
         return [pltpu.SemaphoreType.DMA(shape)] * 2
 
+    outside = pl.BlockSpec(memory_space=pl.ANY)
+    made = (
+        jax.ShapeDtypeStruct((1, members, piece, 3 * columns + CHUNK), BF),
+        jax.ShapeDtypeStruct((tokens, width), BF),
+        jax.ShapeDtypeStruct((tokens, 3 * columns), BF),
+        jax.ShapeDtypeStruct((tokens, CHUNK), F32),
+        jax.ShapeDtypeStruct((16, 3 * columns), BF),
+        jax.ShapeDtypeStruct((tokens, 1), F32),
+        jax.ShapeDtypeStruct((2, width), F32),
+        jax.ShapeDtypeStruct((1, members, columns, piece), BF),
+        jax.ShapeDtypeStruct((len(own), members, *own[0].shape), BF),
+        jax.ShapeDtypeStruct((3, members, columns, piece), BF),
+        jax.ShapeDtypeStruct((tokens, 3 * columns), BF),
+        units((CHUNK, CHUNK), BF),
+        units((CHUNK, 2 * CHUNK), BF),
+        units((2 * CHUNK, CHUNK), BF),
+        jax.ShapeDtypeStruct((heads, CHUNK, 2 * CHUNK), F32),
+        jax.ShapeDtypeStruct((tokens, columns), F32),
+        jax.ShapeDtypeStruct((tokens, columns), BF),
+        jax.ShapeDtypeStruct((3, tokens, columns), BF),
+        units((CHUNK, CHUNK), BF),
+    )
+    stay = (4, 6, 14)
     return pl.pallas_call(
         functools.partial(front_kernel, members, heads),
         name="front",
-        out_shape=(
-            jax.ShapeDtypeStruct((1, members, piece, 3 * columns + CHUNK), BF),
-            jax.ShapeDtypeStruct((tokens, width), BF),
-            jax.ShapeDtypeStruct((tokens, 3 * columns), BF),
-            jax.ShapeDtypeStruct((tokens, CHUNK), F32),
-            jax.ShapeDtypeStruct((16, 3 * columns), BF),
-            jax.ShapeDtypeStruct((tokens, 1), F32),
-            jax.ShapeDtypeStruct((2, width), F32),
-            jax.ShapeDtypeStruct((1, members, *out_weight.shape), BF),
-            jax.ShapeDtypeStruct((own.shape[0], members, *own.shape[1:]), BF),
-            jax.ShapeDtypeStruct((3, members, *out_weight.shape), BF),
-            jax.ShapeDtypeStruct((tokens, 3 * columns), BF),
-            units((CHUNK, CHUNK), BF),
-            units((CHUNK, 2 * CHUNK), BF),
-            units((2 * CHUNK, CHUNK), BF),
-            jax.ShapeDtypeStruct((heads, CHUNK, 2 * CHUNK), F32),
-            jax.ShapeDtypeStruct((tokens, columns), F32),
-            jax.ShapeDtypeStruct((tokens, columns), BF),
-            jax.ShapeDtypeStruct((3, tokens, columns), BF),
-            units((CHUNK, CHUNK), BF),
-        ),
-        in_specs=[pl.BlockSpec(memory_space=pltpu.SMEM)] + [whole] * 9,
-        out_specs=(whole,) * 19,
-        scratch_shapes=[
+        out_shape=made,
+        in_specs=[pl.BlockSpec(memory_space=pltpu.SMEM)] + [whole] * (3 + len(mixer_weights) + len(own)),
+        out_specs=tuple(whole if number in stay else outside for number in range(len(made))),
+        scratch_shapes=[pltpu.VMEM(a.shape, a.dtype) for number, a in enumerate(made) if number not in stay]
+        + [
+            pltpu.SemaphoreType.DMA((len(made) - len(stay),)),
+            pltpu.SMEM((tokens // GROUP,), F32),
+            pltpu.VMEM((4, 3 * columns), F32),
+            pltpu.VMEM((CHUNK, piece), F32),
             pltpu.VMEM((chunks, heads, CHUNK, 2 * CHUNK), BF),
             pltpu.VMEM((chunks, heads, CHUNK, CHUNK), F32),
             pltpu.VMEM((heads, CHUNK, CHUNK), F32),
@@ -1614,7 +1924,7 @@
         + dma(1, members)
         + dma()
         + dma(1, members)
-        + dma(own.shape[0], members)
+        + dma(len(own), members)
         + dma(3)
         + dma(window)
         + dma(tokens // 256) * 3,
@@ -1622,7 +1932,7 @@
             collective_id=collective, has_side_effects=True, vmem_limit_bytes=VMEM_LIMIT
         ),
         cost_estimate=pl.CostEstimate(flops=8 * 10**9, bytes_accessed=40 << 20, transcendentals=2 << 20),
-    )(resets, inputs, query, key, value, extra, out_weight, own, taps, head_gain)
+    )(lengths, inputs, *mixer_weights, conv, head_gain, *own)
 
 
 def lanes_whole(pieces):
@@ -1666,17 +1976,8 @@
     piece = width // members
     seq_place = lax.axis_index("seq")
 
-    extra = jnp.concatenate(
-        [beta_weight, first_gain[:, None], second_gain[:, None], jnp.zeros((piece, CHUNK - heads - 2), BF)], 1
-    )
-    ends = jnp.sum(jnp.where(jnp.arange(4)[:, None] >= jnp.arange(4)[None, :], lengths[None, :], 0), axis=1)
-    starts = ends - lengths
-    block_starts = seq_place * tokens + GROUP * jnp.arange(tokens // GROUP, dtype=jnp.int32)
-    resets = jnp.any(starts[None, :] == block_starts[:, None], axis=1).astype(F32)
-
-    taps = conv_weight.astype(F32).transpose(1, 0, 2).reshape(4, -1)
     gain_head = head_gain.astype(F32)[None, :]
-    own = jnp.stack([gate_weight.T, up_weight.T, down_weight.T])
+    own = [gate_weight.T, up_weight.T, down_weight.T]
     split = piece < 128
     (
         mixer_pack,
@@ -1699,56 +2000,66 @@
         far_rows,
         states,
     ) = front_stage(
-        resets,
+        lengths,
         block_input,
-        query_weight,
-        key_weight,
-        value_weight,
-        extra,
-        output_weight.T,
-        own[:1, :16] if split else own,
-        taps,
+        (
+            query_weight,
+            key_weight,
+            value_weight,
+            beta_weight.T,
+            first_gain[None, :],
+            second_gain[None, :],
+            output_weight,
+        ),
+        conv_weight,
         gain_head,
+        [own[0][:16]] if split else own,
         members,
         heads,
         5,
     )
     mixer_pack = mixer_pack.reshape(width, -1)
     if split:
-        gathered = lax.all_gather(own, "seq", axis=1)
+        gathered = lax.all_gather(jnp.stack(own), "seq", axis=1)
         full = jnp.stack([lanes_whole(gathered[i]) for i in range(3)])
     turned = lanes_whole(turned[0])
     others = jnp.stack([lanes_whole(others[i]) for i in range(3)]) if split else others
-    total_low = total.astype(BF)
     d_heads, update_part, middle_shard, d_middle_shard, *grads, second_grad = middle_stage(
-        head_rows, far_rows, full, turned, others, block_input, cotangent, gains[1:2], 2
+        head_rows, far_rows, full, turned, others, block_input, cotangent, gains, 2
     )
     second_part = jnp.sum(second_grad, 0)
-    ddelta, gain_part, shift = mixer_back_state(d_heads, delta, gain_head, mq)
-    back_part = jnp.concatenate([total_low[:, :, :CHUNK].transpose(0, 2, 1), shift.astype(BF)], 2)
     if split:
         pieces = jnp.concatenate([part for pair in grads for part in pair], 1)
         whole_sum = lax.psum_scatter(lanes_split(pieces, piece), "seq", scatter_dimension=0, tiled=False).astype(F32)
         grads = [jnp.zeros((1, members, 16, 128), BF)] * 3
-    arrive, block_output, third_sum = exchange(back_part, (update_part, middle_shard, grads[2]), "seq", True, 1)
+    ddelta, gain_part, arrive, block_output, third_sum = state_backward(
+        d_heads, delta, gain_head, mq, total, update_part, middle_shard, grads[2], members, 1
+    )
     d_pre, taps_part, first_sum = mixer_backward(
-        resets, pre, halo, taps, logits, qkv, inv, wu, mq, states, ddelta, arrive, grads[0], 3
-    )
-    small = jnp.concatenate(
-        [
-            jnp.zeros((1, width), F32),
-            jnp.pad(jnp.sum(gain_part, 0, keepdims=True), ((0, 0), (0, width - CHUNK))),
-            jnp.zeros((6, width), F32),
-            jnp.sum(second_grad, 0, keepdims=True),
-            jnp.sum(taps_part, 1).reshape(-1, width),
-            jnp.zeros((7 - 12 * columns // width, width), F32),
-        ]
+        lengths, pre, halo, conv_weight, logits, qkv, inv, wu, mq, states, ddelta, arrive, grads[0], 3
     )
     input_gradient, mixer_sum, sums, second_sum = final_stage(
-        first_rows, d_pre, mixer_pack, block_input, scale_one, gains[0:1], d_middle_shard, small, grads[1], members, 4
+        first_rows, d_pre, mixer_pack, block_input, scale_one, gains, d_middle_shard, (gain_part, second_grad, taps_part), grads[1], members, 4
     )
     if not split:
-        whole_sum = jnp.concatenate([s.reshape(-1, 128) for s in (first_sum, second_sum, third_sum)])
+        done = finish_stage(
+            block_output, input_gradient, mixer_sum, sums, first_sum, second_sum, third_sum, hidden_columns, heads
+        )
+        block, ingrad, gain_1, grad_q, grad_k, grad_v, grad_b, grad_c, gain_h, grad_o, gain_2, *rest = done
+        return (
+            block,
+            ingrad,
+            gain_1.reshape(-1),
+            grad_q,
+            grad_k,
+            grad_v,
+            grad_b.T,
+            grad_c,
+            gain_h.reshape(-1),
+            grad_o,
+            gain_2.reshape(-1),
+            *(grad.T for grad in rest),
+        )
     gain_sum = sums[1, :CHUNK]
     conv_gradient = sums[9 : 9 + 12 * columns // width].reshape(4, 3, columns).transpose(1, 0, 2)
     row_start = seq_place * piece

time: 376 us -> 472 us (1.26)
  Pallas kernels: 343 us -> 470 us
  local copies, waits for them, and re-layouts: 19.3 us -> 0 us
  other arithmetic: 11.8 us -> 1.17 us
    pallas_call x2, Pallas kernels: 61.8 us -> 199 us  [the longest x1 143 us: finish_stage(): pl.pallas_call(functools.partial(finish_kernel, hidden), name='finish', o...]
    unnamed x17 -> x0, local copies, waits for them, and re-layouts: 7.95 us -> none
    pallas_call x1, Pallas kernels: 110 us -> 103 us  [front_stage(): pl.pallas_call(functools.partial(front_kernel, members, heads), name='fro...]
    slice x5 -> x0, local copies, waits for them, and re-layouts: 5.54 us -> none  [the longest x1 1.78 us: body(): mixer_sum[:, 2 * columns:3 * columns]]
where the time goes in v6:
time: 472 us
  Pallas kernels  470 us (100%)
    pallas_call x1, Pallas kernels, finish_stage(): pl.pallas_call(functools.partial(finish_kernel, hidden), name='finish', o...  143 us
    pallas_call x1, Pallas kernels, front_stage(): pl.pallas_call(functools.partial(front_kernel, members, heads), name='fro...  103 us
    pallas_call x1, Pallas kernels, middle_stage(): pl.pallas_call(functools.partial(middle_kernel, steps), name='middle', gr...  74.9 us
    pallas_call x1, Pallas kernels, state_backward(): pl.pallas_call(functools.partial(state_backward_kernel, heads, window), n...  55.9 us
    pallas_call x1, Pallas kernels, final_stage(): pl.pallas_call(functools.partial(final_kernel, members, chunk), name='fin...  53.5 us
    pallas_call x1, Pallas kernels, mixer_backward(): pl.pallas_call(functools.partial(mixer_backward_kernel, heads), name='mix...  39.7 us

profile of v6, /device:TPU:0, one launch (start us, length us, event | category | flops | bytes accessed | tf_op | source)
XLA Modules:
  0.0 472.0 jit_solution(17685584962705299147)
XLA Ops:
  0.6 1.2 bitcast_convert_fusion.head_gain_ref.gain_ref
  1.8 103.0 %front.1 = (bf16[1,8,128,896]{3,2,1,0:T(8,128)(2,1)}, bf16[2048,1024]{1,0:T(8,128)(2,1)}, bf16[2048,768]{1,0:T(8,128)(2,1)}, f32[2048,128]{1,0:T(8,128)}, bf16[1...) custom-call(s32[4]{0:T(128)} %lengths_ref.3, ...), custom_call_target="tpu_custom_call" | custom-call | flops 8000000000 | bytes 41943040 | tf_op jit(solution)/shard_map/front/pallas_call | solution.py:1904
  104.8 74.9 %middle.1 = (bf16[2048,256]{1,0:T(8,128)(2,1)}, bf16[2048,1024]{1,0:T(8,128)(2,1)}, f32[2048,256]{1,0:T(8,128)}, f32[2048,256]{1,0:T(8,128)}, bf16[2,8,576,128]{...) custom-call(bf16[2048,256]{1,0:T(8,128)(2,1)} %get-tuple-element.67.row, ...), custom_call_target="tpu_custom_call" | custom-call | flops 30000001024 | bytes 31457280 | tf_op jit(solution)/shard_map/middle/pallas_call | solution.py:831
  179.8 55.9 %state_backward.1 = (bf16[2048,256]{1,0:T(8,128)(2,1)}, f32[8,128]{1,0:T(8,128)}, f32[2,128,128]{2,1,0:T(8,128)}, bf16[2048,256]{1,0:T(8,128)(2,1)}, f32[2,400,128]{2,1,0:T(8,128)}) custom-call(bf16[2048,256]{1,0:T(8,128)(2,1)} %get-tuple-element.73.dheads_ref, f32[2048,256]{1,0:T(8,128)} %get-tuple-element.74.delta_ref, ...), custom_call_target="tpu_custom_call" | custom-call | flops 1000000000 | bytes 31457280 | tf_op jit(solution)/shard_map/state_backward/pallas_call | solution.py:264
  235.7 39.7 %mixer_backward.1 = (bf16[2048,896]{1,0:T(8,128)(2,1)}, f32[4,8,768]{2,1,0:T(8,128)}, f32[2,576,128]{2,1,0:T(8,128)}) custom-call(s32[4]{0:T(128)} %lengths_ref.3, bf16[2048,768]{1,0:T(8,128)(2,1)} %get-tuple-element.82.pre_hbm, bf16[16,768]{1,0:T(8,128)(2,1)} %get-tuple-element.83.halo_ref, bf16[3,4,256]{2,1,0:T(4,128)(2,1)} %conv_ref.3, ...), custom_call_target="tpu_custom_call" | custom-call | flops 3000000000 | bytes 20971520 | tf_op jit(solution)/shard_map/mixer_backward/pallas_call | solution.py:579
  275.4 53.5 %final.1 = (f32[2048,256]{1,0:T(8,128)}, f32[128,896]{1,0:T(8,128)}, f32[16,1024]{1,0:T(8,128)}, f32[2,208,128]{2,1,0:T(8,128)}) custom-call(bf16[2048,1024]{1,0:T(8,128)(2,1)} %get-tuple-element.81.rows_ref, bf16[2048,896]{1,0:T(8,128)(2,1)} %get-tuple-element.92.dpre_ref, bf16[1024,896]{1,0:T(8,128)(2,1)} %bitcast.31, bf16[2048,1024]{1,0:T(8,128)(2,1)} %input_hbm.1, ...), custom_call_target="tpu_custom_call" | custom-call | flops 8000000000 | bytes 31457280 | tf_op jit(solution)/shard_map/final/pallas_call | solution.py:1220
  328.9 142.9 %finish.1 = (bf16[2048,256]{1,0:T(8,128)(2,1)}, f32[2048,256]{1,0:T(8,128)}, f32[1,128]{1,0:T(1,128)}, f32[128,256]{1,0:T(8,128)}, f32[128,256]{1,0:T(8,128)}, /...) custom-call(bf16[2048,256]{1,0:T(8,128)(2,1)} %get-tuple-element.80., ...), custom_call_target="tpu_custom_call" | custom-call | bytes 12582912 | tf_op jit(solution)/shard_map/finish/pallas_call | solution.py:1334

commit v7 on v6

--- a/solution.py
+++ b/solution.py
@@ -1350,7 +1350,7 @@
             made(hidden, rows),
             made(hidden, rows),
         ),
-        in_specs=[outside] * 3 + [whole] + [outside] * 3,
+        in_specs=[whole] * 7,
         out_specs=(outside,) * 2
         + (whole,)
         + (outside,) * 3

time: 472 us -> 335 us (0.71)
  Pallas kernels: 470 us -> 333 us
    pallas_call x1, Pallas kernels: 143 us -> 5.46 us  [finish_stage(): pl.pallas_call(functools.partial(finish_kernel, hidden), name='finish', o...]
where the time goes in v7:
time: 335 us
  Pallas kernels  333 us (99%)
    pallas_call x1, Pallas kernels, front_stage(): pl.pallas_call(functools.partial(front_kernel, members, heads), name='fro...  103 us
    pallas_call x1, Pallas kernels, middle_stage(): pl.pallas_call(functools.partial(middle_kernel, steps), name='middle', gr...  74.9 us
    pallas_call x1, Pallas kernels, state_backward(): pl.pallas_call(functools.partial(state_backward_kernel, heads, window), n...  55.9 us
    pallas_call x1, Pallas kernels, final_stage(): pl.pallas_call(functools.partial(final_kernel, members, chunk), name='fin...  53.5 us
    pallas_call x1, Pallas kernels, mixer_backward(): pl.pallas_call(functools.partial(mixer_backward_kernel, heads), name='mix...  39.7 us

profile of v7, /device:TPU:0, one launch (start us, length us, event | category | flops | bytes accessed | tf_op | source)
XLA Modules:
  0.0 334.6 jit_solution(8561769998485215536)
XLA Ops:
  0.6 1.2 bitcast_convert_fusion.head_gain_ref.gain_ref
  1.8 103.0 %front.1 = (bf16[1,8,128,896]{3,2,1,0:T(8,128)(2,1)}, bf16[2048,1024]{1,0:T(8,128)(2,1)}, bf16[2048,768]{1,0:T(8,128)(2,1)}, f32[2048,128]{1,0:T(8,128)}, bf16[1...) custom-call(s32[4]{0:T(128)} %lengths_ref.3, ...), custom_call_target="tpu_custom_call" | custom-call | flops 8000000000 | bytes 41943040 | tf_op jit(solution)/shard_map/front/pallas_call | solution.py:1904
  104.8 74.9 %middle.1 = (bf16[2048,256]{1,0:T(8,128)(2,1)}, bf16[2048,1024]{1,0:T(8,128)(2,1)}, f32[2048,256]{1,0:T(8,128)}, f32[2048,256]{1,0:T(8,128)}, bf16[2,8,576,128]{...) custom-call(bf16[2048,256]{1,0:T(8,128)(2,1)} %get-tuple-element.67.row, ...), custom_call_target="tpu_custom_call" | custom-call | flops 30000001024 | bytes 31457280 | tf_op jit(solution)/shard_map/middle/pallas_call | solution.py:831
  179.8 55.9 %state_backward.1 = (bf16[2048,256]{1,0:T(8,128)(2,1)}, f32[8,128]{1,0:T(8,128)}, f32[2,128,128]{2,1,0:T(8,128)}, bf16[2048,256]{1,0:T(8,128)(2,1)}, f32[2,400,128]{2,1,0:T(8,128)}) custom-call(bf16[2048,256]{1,0:T(8,128)(2,1)} %get-tuple-element.73.dheads_ref, f32[2048,256]{1,0:T(8,128)} %get-tuple-element.74.delta_ref, ...), custom_call_target="tpu_custom_call" | custom-call | flops 1000000000 | bytes 31457280 | tf_op jit(solution)/shard_map/state_backward/pallas_call | solution.py:264
  235.7 39.7 %mixer_backward.1 = (bf16[2048,896]{1,0:T(8,128)(2,1)}, f32[4,8,768]{2,1,0:T(8,128)}, f32[2,576,128]{2,1,0:T(8,128)}) custom-call(s32[4]{0:T(128)} %lengths_ref.3, bf16[2048,768]{1,0:T(8,128)(2,1)} %get-tuple-element.82.pre_hbm, bf16[16,768]{1,0:T(8,128)(2,1)} %get-tuple-element.83.halo_ref, bf16[3,4,256]{2,1,0:T(4,128)(2,1)} %conv_ref.3, ...), custom_call_target="tpu_custom_call" | custom-call | flops 3000000000 | bytes 20971520 | tf_op jit(solution)/shard_map/mixer_backward/pallas_call | solution.py:579
  275.4 53.5 %final.1 = (f32[2048,256]{1,0:T(8,128)}, f32[128,896]{1,0:T(8,128)}, f32[16,1024]{1,0:T(8,128)}, f32[2,208,128]{2,1,0:T(8,128)}) custom-call(bf16[2048,1024]{1,0:T(8,128)(2,1)} %get-tuple-element.81.rows_ref, bf16[2048,896]{1,0:T(8,128)(2,1)} %get-tuple-element.92.dpre_ref, bf16[1024,896]{1,0:T(8,128)(2,1)} %bitcast.31, bf16[2048,1024]{1,0:T(8,128)(2,1)} %input_hbm.1, ...), custom_call_target="tpu_custom_call" | custom-call | flops 8000000000 | bytes 31457280 | tf_op jit(solution)/shard_map/final/pallas_call | solution.py:1220
  328.9 5.5 %finish.1 = (bf16[2048,256]{1,0:T(8,128)(2,1)}, f32[2048,256]{1,0:T(8,128)}, f32[1,128]{1,0:T(1,128)}, f32[128,256]{1,0:T(8,128)}, f32[128,256]{1,0:T(8,128)}, /...) custom-call(bf16[2048,256]{1,0:T(8,128)(2,1)} %get-tuple-element.80., ...), custom_call_target="tpu_custom_call" | custom-call | bytes 12582912 | tf_op jit(solution)/shard_map/finish/pallas_call | solution.py:1334

commit v8 on v7

--- a/solution.py
+++ b/solution.py
@@ -636,7 +636,6 @@
 def middle_kernel(
     steps,
     rows_ref,
-    late_rows_ref,
     far_rows_ref,
     full_hbm,
     turned_hbm,
@@ -659,6 +658,8 @@
     turned_ref,
     others_ref,
     load_sem,
+    own_rows_ref,
+    stage_ref,
     acc_ref,
     part_ref,
     pair_ref,
@@ -673,6 +674,12 @@
     far_recv,
     last_send,
     last_recv,
+    row_near_send,
+    row_near_recv,
+    row_far_send,
+    row_far_recv,
+    row_pass_send,
+    row_pass_recv,
 ):
     step = pl.program_id(0)
     place, low, near, far = head_peers()
@@ -683,6 +690,29 @@
     mine = pl.ds(pl.multiple_of(low * half, 128), half)
     theirs = pl.ds(pl.multiple_of((1 - low) * half, 128), half)
     own_columns = pl.ds(pl.multiple_of(place * columns, 128), columns)
+
+    known = steps // 2
+
+    def at(index):
+        return pl.ds(pl.multiple_of(index * chunk, chunk), chunk)
+
+    def near_rows(index):
+        place_ = at(index - known)
+        return push(
+            rows_ref.at[at(index)], own_rows_ref.at[0, place_], row_near_send.at[index], row_near_recv.at[index], "head", near
+        )
+
+    def far_rows(index):
+        place_ = at(index - known)
+        return push(
+            rows_ref.at[at(index)], own_rows_ref.at[1, place_], row_far_send.at[index], row_far_recv.at[index], "head", far
+        )
+
+    def pass_rows(index):
+        place_ = at(index - known)
+        return push(
+            own_rows_ref.at[1, place_], own_rows_ref.at[2, place_], row_pass_send.at[index], row_pass_recv.at[index], "head", near
+        )
 
     def pair(index):
         return push(
@@ -716,6 +746,12 @@
             load.start()
         greet("head", (near, far))
 
+        @pl.loop(known, steps)
+        def _(index):
+            far_rows(index).start()
+            near_rows(index).start()
+
+
         acc_ref[...] = jnp.zeros_like(acc_ref)
         gain_grad_ref[...] = jnp.zeros_like(gain_grad_ref)
         for load in loads():
@@ -726,9 +762,19 @@
         ct = ct_ref[...]
         d_hidden = nt(ct, down_ref[...])
 
-        branch = nn(rows_ref[...], turned_ref[...])
+        @pl.when(step < known)
+        def _():
+            stage_ref[...] = far_rows_ref[...]
+
+        @pl.when(step >= known)
+        def _():
+            near_rows(step).wait_recv()
+            pass_rows(step).wait_recv()
+            stage_ref[...] = own_rows_ref[:, at(step - known)]
+
+        branch = nn(rows_ref[at(step)], turned_ref[...])
         for other in range(3):
-            branch = branch + nn(far_rows_ref[other], others_ref[other])
+            branch = branch + nn(stage_ref[other], others_ref[other])
         middle = input_ref[...].astype(F32) + branch
         keep_ref[lax.rem(step, 4)] = middle
         mid_ref[...] = keep_ref[lax.rem(step, 4), :, own_columns]
@@ -749,6 +795,11 @@
         part_ref[lax.rem(step, 2)] = (nn(d_gate, gate_ref[...]) + nn(d_up, up_ref[...])).astype(BF)
         pair(step).start()
 
+        @pl.when((step + 2 >= known) & (step + 2 < steps))
+        def _():
+            far_rows(step + 2).wait_recv()
+            pass_rows(step + 2).start()
+
         update_ref[...] = nn(active, down_ref[...]).astype(BF)
         acc_ref[:hidden] += tn(d_gate, second)
         acc_ref[hidden : 2 * hidden] += tn(d_up, second)
@@ -787,7 +838,7 @@
         dmid_ref[...] = shard_ref[:, own_columns]
         d_branch = d_middle.astype(BF)
         dheads_ref[...] = nt(d_branch, turned_ref[...]).astype(BF)
-        acc_ref[3 * hidden :] += tn(late_rows_ref[...], d_branch)
+        acc_ref[3 * hidden :] += tn(rows_ref[at(done)], d_branch)
 
     @pl.when(step == steps + 2)
     def _():
@@ -803,6 +854,12 @@
         @pl.loop(0, steps)
         def _(index):
             last(index).wait_send()
+
+        @pl.loop(known, steps)
+        def _(index):
+            near_rows(index).wait_send()
+            far_rows(index).wait_send()
+            pass_rows(index).wait_send()
 
         for index in range(max(steps - 2, 0), steps):
             pair(index).wait_send()
@@ -826,7 +883,7 @@
     def late(wide):
         return pl.BlockSpec((chunk, wide), lambda s: (jnp.maximum(s - 3, 0), 0))
 
-    far = pl.BlockSpec((3, chunk, columns), lambda s: (0, jnp.minimum(s, steps - 1), 0))
+    far = pl.BlockSpec((3, chunk, columns), lambda s: (0, jnp.minimum(s, steps // 2 - 1), 0))
     dma = pltpu.SemaphoreType.DMA((steps,))
     return pl.pallas_call(
         functools.partial(middle_kernel, steps),
@@ -840,7 +897,7 @@
             *(jax.ShapeDtypeStruct((2, width // 128, rows, 128), BF) for rows in shares),
             jax.ShapeDtypeStruct((8, width), F32),
         ),
-        in_specs=[early(columns), late(columns), far] + [outside] * 3 + [early(width), early(width), late(width), whole],
+        in_specs=[whole, far] + [outside] * 3 + [early(width), early(width), late(width), whole],
         out_specs=(late(columns), early(width), early(columns), late(columns), whole, whole, whole, whole),
         scratch_shapes=[
             pltpu.VMEM((hidden, width), BF),
@@ -849,6 +906,8 @@
             pltpu.VMEM((columns, width), BF),
             pltpu.VMEM((3, columns, width), BF),
             pltpu.SemaphoreType.DMA((7, width // 128)),
+            pltpu.VMEM((3, tokens // 2, columns), BF),
+            pltpu.VMEM((3, chunk, columns), BF),
             pltpu.VMEM((3 * hidden + columns, width), F32),
             pltpu.VMEM((2, chunk, width), BF),
             pltpu.VMEM((steps, chunk, width // 2), BF),
@@ -858,7 +917,7 @@
             pltpu.VMEM((4, chunk, 1), F32),
             pltpu.VMEM((chunk, width), F32),
         ]
-        + [dma] * 6,
+        + [dma] * 12,
         compiler_params=pltpu.CompilerParams(
             collective_id=collective,
             has_side_effects=True,
@@ -866,7 +925,7 @@
             dimension_semantics=("arbitrary",),
         ),
         cost_estimate=pl.CostEstimate(flops=30 * 10**9, bytes_accessed=30 << 20, transcendentals=2 << 20),
-    )(head_rows, head_rows, far_rows, full, turned, others, inputs, cotangent, cotangent, gain)
+    )(head_rows, far_rows, full, turned, others, inputs, cotangent, cotangent, gain)
 
 
 def zeros_below(value):
@@ -1625,7 +1684,6 @@
     pass_copy = push(others_ref.at[1], others_ref.at[2], head_send.at[2], head_recv.at[2], "head", near)
     pl.semaphore_wait(barrier, stages + 2 + jnp.minimum(behind, 1) + jnp.minimum(behind, window))
     pack[0]()
-    turned[0]()
     full[0](0, [stages - 1, 0])
     fill_resets(lengths_ref, resets_ref, tokens)
     fill_taps(conv_ref, taps_ref)
@@ -1651,9 +1709,8 @@
     pl.loop(0, tokens // chunk)(measure)
     for job in pack[2]:
         pack[1](*job)
-    for job in turned[2]:
-        turned[1](*job)
     full[0](0, range(1, stages - 1))
+    turned[0]()
     pack[3]()
     projection = pack_ref[0].reshape(width, pack_ref.shape[3])
     extras = projection[:, 3 * columns :].astype(F32)
@@ -1681,11 +1738,8 @@
         first = (block * scale * gains_ref[0:1]).astype(BF)
         halo_ref[...] = nn(first, pack_ref[0].reshape(width, pack_ref.shape[3])[:, : 3 * columns]).astype(BF)
 
-    turned[3]()
-    for number in range(6):
+    for number in range(5):
         store(number).start()
-    near_copy.start()
-    far_copy.start()
     rows, cols = grid_indices()
     eye = jnp.where(rows == cols, 1.0, 0.0)
     top = lax.broadcasted_iota(jnp.int32, (CHUNK, 1), 0) < GROUP
@@ -1756,14 +1810,22 @@
         carry = one(step, carry)
         for turn in range(count):
             jobs = [job for place, job in enumerate(relays) if place * count // len(relays) == turn]
-            if not jobs and turn != count // 2:
+            if not jobs and turn not in (0, 2, count - 2):
                 continue
 
             @pl.when(step == turn)
             def _():
+                if turn == 0:
+                    for job in turned[2]:
+                        turned[1](*job)
                 for job in jobs:
                     full[1](*job)
-                if turn == count // 2:
+                if turn == 2:
+                    turned[3]()
+                    store(5).start()
+                    near_copy.start()
+                    far_copy.start()
+                if turn == count - 2:
                     far_copy.wait_recv()
                     pass_copy.start()
 
@@ -1822,14 +1884,20 @@
                 delta_ref[rows_at, lanes] = outs[head]
                 scale = lax.rsqrt(jnp.mean(outs[head] * outs[head], axis=-1, keepdims=True) + 1e-05)
                 rows_ref[rows_at, lanes] = (outs[head] * scale * head_gain_ref[...]).astype(BF)
+
+    sent = far_rows_ref.shape[1] // chunk
+
+    def finished_and_sent(index):
+        finished(index)
         far_rows(index).start()
         near_rows(index).start()
 
-    pl.loop(0, tokens // chunk)(finished)
+    pl.loop(0, sent)(finished_and_sent)
+    pl.loop(sent, tokens // chunk)(finished)
     for number in range(10, 13):
         store(number).start()
 
-    @pl.loop(0, tokens // chunk)
+    @pl.loop(0, sent)
     def _(index):
         far_rows(index).wait_recv()
         pass_rows(index).start()
@@ -1849,7 +1917,7 @@
         def _():
             state_copy(hop).wait_send()
 
-    @pl.loop(0, tokens // chunk)
+    @pl.loop(0, sent)
     def _(index):
         near_rows(index).wait()
         far_rows(index).wait_send()
@@ -1897,7 +1965,7 @@
         jax.ShapeDtypeStruct((heads, CHUNK, 2 * CHUNK), F32),
         jax.ShapeDtypeStruct((tokens, columns), F32),
         jax.ShapeDtypeStruct((tokens, columns), BF),
-        jax.ShapeDtypeStruct((3, tokens, columns), BF),
+        jax.ShapeDtypeStruct((3, tokens // 2, columns), BF),
         units((CHUNK, CHUNK), BF),
     )
     stay = (4, 6, 14)

time: 335 us -> 330 us (0.985)
  Pallas kernels: 333 us -> 326 us
    pallas_call x1, Pallas kernels: 55.9 us -> 50.1 us  [state_backward(): pl.pallas_call(functools.partial(state_backward_kernel, heads, window), n...]
    pallas_call x1, Pallas kernels: 74.9 us -> 80.6 us  [middle_stage(): pl.pallas_call(functools.partial(middle_kernel, steps), name='middle', gr...]
    pallas_call x1, Pallas kernels: 103 us -> 98.9 us  [front_stage(): pl.pallas_call(functools.partial(front_kernel, members, heads), name='fro...]
where the time goes in v8:
time: 330 us; the launch traced here: 328 us
  Pallas kernels  326 us (99%)
    pallas_call x1, Pallas kernels, front_stage(): pl.pallas_call(functools.partial(front_kernel, members, heads), name='fro...  98.9 us
    pallas_call x1, Pallas kernels, middle_stage(): pl.pallas_call(functools.partial(middle_kernel, steps), name='middle', gr...  80.6 us
    pallas_call x1, Pallas kernels, final_stage(): pl.pallas_call(functools.partial(final_kernel, members, chunk), name='fin...  50.6 us
    pallas_call x1, Pallas kernels, state_backward(): pl.pallas_call(functools.partial(state_backward_kernel, heads, window), n...  50.1 us
    pallas_call x1, Pallas kernels, mixer_backward(): pl.pallas_call(functools.partial(mixer_backward_kernel, heads), name='mix...  39.8 us

profile of v8, /device:TPU:0, one launch (start us, length us, event | category | flops | bytes accessed | tf_op | source)
XLA Modules:
  0.0 327.5 jit_solution(16674533374344355468)
XLA Ops:
  0.6 1.2 bitcast_convert_fusion.head_gain_ref.gain_ref
  1.8 98.9 %front.1 = (bf16[1,8,128,896]{3,2,1,0:T(8,128)(2,1)}, bf16[2048,1024]{1,0:T(8,128)(2,1)}, bf16[2048,768]{1,0:T(8,128)(2,1)}, f32[2048,128]{1,0:T(8,128)}, bf16[1...) custom-call(s32[4]{0:T(128)} %lengths_ref.3, ...), custom_call_target="tpu_custom_call" | custom-call | flops 8000000000 | bytes 41943040 | tf_op jit(solution)/shard_map/front/pallas_call | solution.py:1972
  100.8 80.6 %middle.1 = (bf16[2048,256]{1,0:T(8,128)(2,1)}, bf16[2048,1024]{1,0:T(8,128)(2,1)}, f32[2048,256]{1,0:T(8,128)}, f32[2048,256]{1,0:T(8,128)}, bf16[2,8,576,128]{...) custom-call(bf16[2048,256]{1,0:T(8,128)(2,1)} %get-tuple-element.67.row, ...), custom_call_target="tpu_custom_call" | custom-call | flops 30000001024 | bytes 31457280 | tf_op jit(solution)/shard_map/middle/pallas_call | solution.py:888
  181.3 50.1 %state_backward.1 = (bf16[2048,256]{1,0:T(8,128)(2,1)}, f32[8,128]{1,0:T(8,128)}, f32[2,128,128]{2,1,0:T(8,128)}, bf16[2048,256]{1,0:T(8,128)(2,1)}, f32[2,400,128]{2,1,0:T(8,128)}) custom-call(bf16[2048,256]{1,0:T(8,128)(2,1)} %get-tuple-element.73.dheads_ref, f32[2048,256]{1,0:T(8,128)} %get-tuple-element.74.delta_ref, ...), custom_call_target="tpu_custom_call" | custom-call | flops 1000000000 | bytes 31457280 | tf_op jit(solution)/shard_map/state_backward/pallas_call | solution.py:264
  231.4 39.8 %mixer_backward.1 = (bf16[2048,896]{1,0:T(8,128)(2,1)}, f32[4,8,768]{2,1,0:T(8,128)}, f32[2,576,128]{2,1,0:T(8,128)}) custom-call(s32[4]{0:T(128)} %lengths_ref.3, bf16[2048,768]{1,0:T(8,128)(2,1)} %get-tuple-element.82.pre_hbm, bf16[16,768]{1,0:T(8,128)(2,1)} %get-tuple-element.83.halo_ref, bf16[3,4,256]{2,1,0:T(4,128)(2,1)} %conv_ref.3, ...), custom_call_target="tpu_custom_call" | custom-call | flops 3000000000 | bytes 20971520 | tf_op jit(solution)/shard_map/mixer_backward/pallas_call | solution.py:579
  271.2 50.6 %final.1 = (f32[2048,256]{1,0:T(8,128)}, f32[128,896]{1,0:T(8,128)}, f32[16,1024]{1,0:T(8,128)}, f32[2,208,128]{2,1,0:T(8,128)}) custom-call(bf16[2048,1024]{1,0:T(8,128)(2,1)} %get-tuple-element.81.rows_ref, bf16[2048,896]{1,0:T(8,128)(2,1)} %get-tuple-element.92.dpre_ref, bf16[1024,896]{1,0:T(8,128)(2,1)} %bitcast.31, bf16[2048,1024]{1,0:T(8,128)(2,1)} %input_hbm.1, ...), custom_call_target="tpu_custom_call" | custom-call | flops 8000000000 | bytes 31457280 | tf_op jit(solution)/shard_map/final/pallas_call | solution.py:1279
  321.9 5.5 %finish.1 = (bf16[2048,256]{1,0:T(8,128)(2,1)}, f32[2048,256]{1,0:T(8,128)}, f32[1,128]{1,0:T(1,128)}, f32[128,256]{1,0:T(8,128)}, f32[128,256]{1,0:T(8,128)}, /...) custom-call(bf16[2048,256]{1,0:T(8,128)(2,1)} %get-tuple-element.80., ...), custom_call_target="tpu_custom_call" | custom-call | bytes 12582912 | tf_op jit(solution)/shard_map/finish/pallas_call | solution.py:1393

commit v9 on v8

--- a/solution.py
+++ b/solution.py
@@ -431,113 +431,130 @@
     taps_grad_ref[...] = jnp.zeros_like(taps_grad_ref)
     dpad_ref[136:144] = jnp.zeros_like(dpad_ref[136:144])
 
+    lanes_ = 2
+    cross = (rows >= GROUP) & (cols < GROUP)
+    columns_of = lax.broadcasted_iota(jnp.int32, (CHUNK, CHUNK), 1)
+
+    def part(kind, head):
+        return slice(kind * columns + head * CHUNK, kind * columns + (head + 1) * CHUNK)
+
     def one(step, carry):
-        chunk = chunks - 1 - step
-        at = pl.ds(pl.multiple_of(chunk * CHUNK, CHUNK), CHUNK)
         for turn in range(4):
 
-            @pl.when(step == turn * quarter)
+            @pl.when(step * lanes_ == turn * quarter)
             def _():
                 for number in range(1, 8):
                     load(number, turn).wait()
                 if turn < 3:
                     load(0, turn + 1).wait()
 
-        keep0 = 1.0 - resets_ref[2 * chunk]
-        keep1 = 1.0 - resets_ref[2 * chunk + 1]
-        both = keep0 * keep1
-        enter = jnp.where(top, keep0, both)
-        leave = jnp.where(top, keep1, 1.0)
-        load_padded(pad_ref, pre_ref, halo_ref, chunk, resets_ref)
-        mixed = convolve(pad_ref, taps_ref)
-        gate = sigmoid(mixed)
-        slope = gate * (1.0 + mixed * (1.0 - gate))
-        silued = mixed * gate
-        beta_rows = sigmoid(logits_ref[at, :])
-        grads = [[None] * heads for _ in range(3)]
-        dlogits = []
-        cross = (rows >= GROUP) & (cols < GROUP)
-
-        def part(kind, head):
-            return slice(kind * columns + head * CHUNK, kind * columns + (head + 1) * CHUNK)
-
-        def masked(product, keep):
+        at, keep0, keep1, enter, leave, slope, silued, beta_rows, place = [], [], [], [], [], [], [], [], []
+        for lane in range(lanes_):
+            chunk = chunks - 1 - lanes_ * step - lane
+            place.append(chunk)
+            at.append(pl.ds(pl.multiple_of(chunk * CHUNK, CHUNK), CHUNK))
+            keep0.append(1.0 - resets_ref[2 * chunk])
+            keep1.append(1.0 - resets_ref[2 * chunk + 1])
+            enter.append(jnp.where(top, keep0[lane], keep0[lane] * keep1[lane]))
+            leave.append(jnp.where(top, keep1[lane], 1.0))
+            load_padded(pad_ref.at[lane], pre_ref, halo_ref, chunk, resets_ref)
+            mixed = convolve(pad_ref.at[lane], taps_ref)
+            gate = sigmoid(mixed)
+            slope.append(gate * (1.0 + mixed * (1.0 - gate)))
+            silued.append(mixed * gate)
+            beta_rows.append(sigmoid(logits_ref[at[lane], :]))
+
+        units = [(lane, h) for lane in range(lanes_) for h in range(heads)]
+        every = range(len(units))
+
+        def masked(product, keep, u):
             lower = jnp.where(keep, product, 0.0)
-            return jnp.where(cross, lower * keep1, lower).astype(BF)
-
-        every = range(heads)
-        query = [qkv_ref[at, part(0, h)] for h in every]
-        key = [qkv_ref[at, part(1, h)] for h in every]
-        value = [qkv_ref[at, part(2, h)] for h in every]
+            return jnp.where(cross, lower * keep1[units[u][0]], lower).astype(BF)
+
+        query = [qkv_ref[at[l], part(0, h)] for l, h in units]
+        key = [qkv_ref[at[l], part(1, h)] for l, h in units]
+        value = [qkv_ref[at[l], part(2, h)] for l, h in units]
         key32 = [k.astype(F32) for k in key]
-        beta = [beta_rows[:, h : h + 1] for h in every]
-        inverse = [inv_ref[chunk, h] for h in every]
-        weight = [wu_ref[chunk, h, :, :CHUNK] for h in every]
-        factors = [wu_ref[chunk, h] for h in every]
-        update = [wu_ref[chunk, h, :, CHUNK:] for h in every]
-        state = [states_ref[chunk, h] for h in every]
-        out_grad = [ddelta_ref[at, h * CHUNK : (h + 1) * CHUNK] for h in every]
-        later = [carry_ref[h].astype(BF) for h in every]
-        carried = [tn(mq_ref[chunk, h], stack(later[h], out_grad[h])) for h in every]
-        scores = [masked(nt(query[h], key[h]), rows >= cols) for h in every]
-        fresh = [(update[h].astype(F32) - nn(weight[h], state[h])).astype(BF) for h in every]
-        fresh_low = [(tn(scores[h], out_grad[h]) + leave * nn(key[h], later[h])).astype(BF) for h in every]
-        score_grad = [masked(nt(out_grad[h], fresh[h]), rows >= cols) for h in every]
-        through = [nt(stack(out_grad[h], fresh_low[h]), state[h]) for h in every]
-        weight_grad = [(-enter * through[h][CHUNK:]).astype(BF) for h in every]
-        back = [tn(inverse[h], side(weight_grad[h], fresh_low[h])) for h in every]
-        query_grad = [enter * through[h][:CHUNK] + nn(score_grad[h], key[h]) for h in every]
-        key_grad = [tn(score_grad[h], query[h]) + leave * nt(fresh[h], later[h]) for h in every]
-        strict = [masked(-nt(back[h].astype(BF), factors[h]), rows > cols) for h in every]
-        strict_key = [nn(strict[h], key[h]) for h in every]
-        turned = [tn(strict[h], (beta[h] * key32[h]).astype(BF)) for h in every]
-        for h in every:
+        beta = [beta_rows[l][:, h : h + 1] for l, h in units]
+        inverse = [inv_ref[place[l], h] for l, h in units]
+        factors = [wu_ref[place[l], h] for l, h in units]
+        weight = [f[:, :CHUNK] for f in factors]
+        update = [f[:, CHUNK:] for f in factors]
+        state = [states_ref[place[l], h] for l, h in units]
+        out_grad = [ddelta_ref[at[l], h * CHUNK : (h + 1) * CHUNK] for l, h in units]
+        later = []
+        carried = [carry_ref[h] for h in range(heads)]
+        for u, (l, h) in enumerate(units):
+            later.append(carried[h].astype(BF))
+            carried[h] = tn(mq_ref[place[l], h], stack(later[u], out_grad[u]))
+        scores = [masked(nt(query[u], key[u]), rows >= cols, u) for u in every]
+        fresh = [(update[u].astype(F32) - nn(weight[u], state[u])).astype(BF) for u in every]
+        fresh_low = [
+            (tn(scores[u], out_grad[u]) + leave[units[u][0]] * nn(key[u], later[u])).astype(BF) for u in every
+        ]
+        score_grad = [masked(nt(out_grad[u], fresh[u]), rows >= cols, u) for u in every]
+        through = [nt(stack(out_grad[u], fresh_low[u]), state[u]) for u in every]
+        weight_grad = [(-enter[units[u][0]] * through[u][CHUNK:]).astype(BF) for u in every]
+        back = [tn(inverse[u], side(weight_grad[u], fresh_low[u])) for u in every]
+        query_grad = [enter[units[u][0]] * through[u][:CHUNK] + nn(score_grad[u], key[u]) for u in every]
+        key_grad = [tn(score_grad[u], query[u]) + leave[units[u][0]] * nt(fresh[u], later[u]) for u in every]
+        strict = [masked(-nt(back[u].astype(BF), factors[u]), rows > cols, u) for u in every]
+        strict_key = [nn(strict[u], key[u]) for u in every]
+        turned = [tn(strict[u], (beta[u] * key32[u]).astype(BF)) for u in every]
+        for h in range(heads):
             carry_ref[h] = carried[h]
-            yk, zv = back[h][:, :CHUNK], back[h][:, CHUNK:]
-            both_key = yk + strict_key[h]
-            key_grad[h] = key_grad[h] + beta[h] * both_key + turned[h]
-            grads[2][h] = beta[h] * zv
-            beta_grad = jnp.sum(both_key * key32[h] + zv * value[h].astype(F32), axis=-1, keepdims=True)
-            dlogits.append(beta_grad * beta[h] * (1.0 - beta[h]))
+        value_grad, dlogits = [], []
+        for u in every:
+            yk, zv = back[u][:, :CHUNK], back[u][:, CHUNK:]
+            both_key = yk + strict_key[u]
+            key_grad[u] = key_grad[u] + beta[u] * both_key + turned[u]
+            value_grad.append(beta[u] * zv)
+            beta_grad = jnp.sum(both_key * key32[u] + zv * value[u].astype(F32), axis=-1, keepdims=True)
+            dlogits.append(beta_grad * beta[u] * (1.0 - beta[u]))
+        unit_grads = []
         for kind, grad in ((0, query_grad), (1, key_grad)):
-            raw = [silued[:, part(kind, h)] for h in every]
-            norm = [lax.rsqrt(jnp.sum(raw[h] * raw[h], axis=-1, keepdims=True) + 1e-06) for h in every]
-            unit = [raw[h] * norm[h] for h in every]
-            inner = [jnp.sum(unit[h] * grad[h], axis=-1, keepdims=True) for h in every]
-            grads[kind] = [(grad[h] - unit[h] * inner[h]) * norm[h] for h in every]
-        lanes = lax.broadcasted_iota(jnp.int32, (CHUNK, CHUNK), 1)
-        spread = jnp.zeros((CHUNK, CHUNK), F32)
-        for head in range(heads):
-            spread = jnp.where(lanes == head, dlogits[head], spread)
-        dpre_ref[at, 3 * columns :] = spread.astype(BF)
-        dmixed = jnp.concatenate([g for kind in grads for g in kind], 1) * slope
-        dpad_ref[0:GROUP] = dmixed[:GROUP]
-        dpad_ref[GROUP : GROUP + 8] = dmixed[GROUP : GROUP + 8] * keep1
-        dpad_ref[72 : 72 + GROUP] = dmixed[GROUP:]
-        dpre = None
-        for tap in range(4):
-            back = 3 - tap
-            shifted = stack(dpad_ref[back : back + GROUP], dpad_ref[72 + back : 72 + back + GROUP])
-            term = taps_ref[tap : tap + 1] * shifted
-            dpre = term if dpre is None else dpre + term
-            seen = (dmixed * tap_rows(pad_ref, tap)).reshape(CHUNK // 8, 8, 3 * columns)
-            taps_grad_ref[tap] += jnp.sum(seen, 0)
-        dpre_ref[at, : 3 * columns] = dpre.astype(BF)
-
-        @pl.when(step == 0)
-        def _():
-            tail_ref[...] = dpre[CHUNK - 16 :]
-
-        dpad_ref[136:144] = dmixed[:8] * keep0
-        for place, job in enumerate(order):
-
-            @pl.when(step == (place + 1) * (chunks - 1) // len(order))
+            raw = [silued[l][:, part(kind, h)] for l, h in units]
+            norm = [lax.rsqrt(jnp.sum(r * r, axis=-1, keepdims=True) + 1e-06) for r in raw]
+            unit = [raw[u] * norm[u] for u in every]
+            inner = [jnp.sum(unit[u] * grad[u], axis=-1, keepdims=True) for u in every]
+            unit_grads.append([(grad[u] - unit[u] * inner[u]) * norm[u] for u in every])
+        unit_grads.append(value_grad)
+        for lane in range(lanes_):
+            spread = jnp.zeros((CHUNK, CHUNK), F32)
+            for head in range(heads):
+                spread = jnp.where(columns_of == head, dlogits[lane * heads + head], spread)
+            dpre_ref[at[lane], 3 * columns :] = spread.astype(BF)
+            mine = [g[lane * heads + head] for g in unit_grads for head in range(heads)]
+            dmixed = jnp.concatenate(mine, 1) * slope[lane]
+            dpad_ref[0:GROUP] = dmixed[:GROUP]
+            dpad_ref[GROUP : GROUP + 8] = dmixed[GROUP : GROUP + 8] * keep1[lane]
+            dpad_ref[72 : 72 + GROUP] = dmixed[GROUP:]
+            dpre = None
+            for tap in range(4):
+                reach = 3 - tap
+                shifted = stack(dpad_ref[reach : reach + GROUP], dpad_ref[72 + reach : 72 + reach + GROUP])
+                term = taps_ref[tap : tap + 1] * shifted
+                dpre = term if dpre is None else dpre + term
+                seen = (dmixed * tap_rows(pad_ref.at[lane], tap)).reshape(CHUNK // 8, 8, 3 * columns)
+                taps_grad_ref[tap] += jnp.sum(seen, 0)
+            dpre_ref[at[lane], : 3 * columns] = dpre.astype(BF)
+            if lane == 0:
+
+                @pl.when(step == 0)
+                def _():
+                    tail_ref[...] = dpre[CHUNK - 16 :]
+
+            dpad_ref[136:144] = dmixed[:8] * keep0[lane]
+        turns = chunks // lanes_
+        for number, job in enumerate(order):
+
+            @pl.when(step == (number + 1) * (turns - 1) // len(order))
             def _():
                 receive(*job)
 
         return carry
 
-    lax.fori_loop(0, chunks, one, 0)
+    lax.fori_loop(0, chunks // lanes_, one, 0)
     index = lax.broadcasted_iota(jnp.int32, (8, 1), 0)
     lead = jnp.zeros((8, 3 * columns), F32)
     dpad_ref[0:128] = jnp.zeros_like(dpad_ref[0:128])
@@ -592,7 +609,7 @@
             pltpu.SMEM((tokens // GROUP,), F32),
             pltpu.VMEM((4, 3 * columns), F32),
             pltpu.VMEM((heads, CHUNK, CHUNK), F32),
-            pltpu.VMEM((144, 3 * columns), F32),
+            pltpu.VMEM((2, 144, 3 * columns), F32),
             pltpu.VMEM((144, 3 * columns), F32),
             pltpu.VMEM((16, 3 * columns), F32),
             pltpu.VMEM((8, 3 * columns), F32),
@@ -1684,7 +1701,6 @@
     pass_copy = push(others_ref.at[1], others_ref.at[2], head_send.at[2], head_recv.at[2], "head", near)
     pl.semaphore_wait(barrier, stages + 2 + jnp.minimum(behind, 1) + jnp.minimum(behind, window))
     pack[0]()
-    full[0](0, [stages - 1, 0])
     fill_resets(lengths_ref, resets_ref, tokens)
     fill_taps(conv_ref, taps_ref)
 
@@ -1709,7 +1725,7 @@
     pl.loop(0, tokens // chunk)(measure)
     for job in pack[2]:
         pack[1](*job)
-    full[0](0, range(1, stages - 1))
+    full[0](0)
     turned[0]()
     pack[3]()
     projection = pack_ref[0].reshape(width, pack_ref.shape[3])
@@ -1803,7 +1819,7 @@
         return carry
 
     count = resets_ref.shape[0] // 2 // batch
-    held = 3 if len(full[2]) > 3 else 0
+    held = 4 if len(full[2]) > 4 else 0
     relays = full[2][: len(full[2]) - held]
 
     def pumped(step, carry):

time: 330 us -> 324 us (0.982)
  Pallas kernels: 326 us -> 322 us
where the time goes in v9:
time: 324 us
  Pallas kernels  322 us (99%)
    pallas_call x1, Pallas kernels, front_stage(): pl.pallas_call(functools.partial(front_kernel, members, heads), name='fro...  98.2 us
    pallas_call x1, Pallas kernels, middle_stage(): pl.pallas_call(functools.partial(middle_kernel, steps), name='middle', gr...  80.5 us
    pallas_call x1, Pallas kernels, final_stage(): pl.pallas_call(functools.partial(final_kernel, members, chunk), name='fin...  49 us
    pallas_call x1, Pallas kernels, state_backward(): pl.pallas_call(functools.partial(state_backward_kernel, heads, window), n...  48 us
    pallas_call x1, Pallas kernels, mixer_backward(): pl.pallas_call(functools.partial(mixer_backward_kernel, heads), name='mix...  40.8 us

profile of v9, /device:TPU:0, one launch (start us, length us, event | category | flops | bytes accessed | tf_op | source)
XLA Modules:
  0.0 324.1 jit_solution(8890417697913401164)
XLA Ops:
  0.6 1.2 bitcast_convert_fusion.head_gain_ref.gain_ref
  1.8 98.2 %front.1 = (bf16[1,8,128,896]{3,2,1,0:T(8,128)(2,1)}, bf16[2048,1024]{1,0:T(8,128)(2,1)}, bf16[2048,768]{1,0:T(8,128)(2,1)}, f32[2048,128]{1,0:T(8,128)}, bf16[1...) custom-call(s32[4]{0:T(128)} %lengths_ref.3, ...), custom_call_target="tpu_custom_call" | custom-call | flops 8000000000 | bytes 41943040 | tf_op jit(solution)/shard_map/front/pallas_call | solution.py:1988
  100.0 80.5 %middle.1 = (bf16[2048,256]{1,0:T(8,128)(2,1)}, bf16[2048,1024]{1,0:T(8,128)(2,1)}, f32[2048,256]{1,0:T(8,128)}, f32[2048,256]{1,0:T(8,128)}, bf16[2,8,576,128]{...) custom-call(bf16[2048,256]{1,0:T(8,128)(2,1)} %get-tuple-element.67.row, ...), custom_call_target="tpu_custom_call" | custom-call | flops 30000001024 | bytes 31457280 | tf_op jit(solution)/shard_map/middle/pallas_call | solution.py:905
  180.6 48.0 %state_backward.1 = (bf16[2048,256]{1,0:T(8,128)(2,1)}, f32[8,128]{1,0:T(8,128)}, f32[2,128,128]{2,1,0:T(8,128)}, bf16[2048,256]{1,0:T(8,128)(2,1)}, f32[2,400,128]{2,1,0:T(8,128)}) custom-call(bf16[2048,256]{1,0:T(8,128)(2,1)} %get-tuple-element.73.dheads_ref, f32[2048,256]{1,0:T(8,128)} %get-tuple-element.74.delta_ref, ...), custom_call_target="tpu_custom_call" | custom-call | flops 1000000000 | bytes 31457280 | tf_op jit(solution)/shard_map/state_backward/pallas_call | solution.py:264
  228.6 40.8 %mixer_backward.1 = (bf16[2048,896]{1,0:T(8,128)(2,1)}, f32[4,8,768]{2,1,0:T(8,128)}, f32[2,576,128]{2,1,0:T(8,128)}) custom-call(s32[4]{0:T(128)} %lengths_ref.3, bf16[2048,768]{1,0:T(8,128)(2,1)} %get-tuple-element.82.pre_hbm, bf16[16,768]{1,0:T(8,128)(2,1)} %get-tuple-element.83.halo_ref, bf16[3,4,256]{2,1,0:T(4,128)(2,1)} %conv_ref.3, ...), custom_call_target="tpu_custom_call" | custom-call | flops 3000000000 | bytes 20971520 | tf_op jit(solution)/shard_map/mixer_backward/pallas_call | solution.py:596
  269.4 49.0 %final.1 = (f32[2048,256]{1,0:T(8,128)}, f32[128,896]{1,0:T(8,128)}, f32[16,1024]{1,0:T(8,128)}, f32[2,208,128]{2,1,0:T(8,128)}) custom-call(bf16[2048,1024]{1,0:T(8,128)(2,1)} %get-tuple-element.81.rows_ref, bf16[2048,896]{1,0:T(8,128)(2,1)} %get-tuple-element.92.dpre_ref, bf16[1024,896]{1,0:T(8,128)(2,1)} %bitcast.31, bf16[2048,1024]{1,0:T(8,128)(2,1)} %input_hbm.1, ...), custom_call_target="tpu_custom_call" | custom-call | flops 8000000000 | bytes 31457280 | tf_op jit(solution)/shard_map/final/pallas_call | solution.py:1296
  318.4 5.5 %finish.1 = (bf16[2048,256]{1,0:T(8,128)(2,1)}, f32[2048,256]{1,0:T(8,128)}, f32[1,128]{1,0:T(1,128)}, f32[128,256]{1,0:T(8,128)}, f32[128,256]{1,0:T(8,128)}, /...) custom-call(bf16[2048,256]{1,0:T(8,128)(2,1)} %get-tuple-element.80., ...), custom_call_target="tpu_custom_call" | custom-call | bytes 12582912 | tf_op jit(solution)/shard_map/finish/pallas_call | solution.py:1410

commit v10 on v9

--- a/solution.py
+++ b/solution.py
@@ -209,7 +209,7 @@
             scale = lax.rsqrt(jnp.mean(out * out, axis=-1, keepdims=True) + 1e-05)
             unit = out * scale
             gain_grad_ref[...] += jnp.sum((grad * unit).reshape(CHUNK // 8, 8, CHUNK), 0)
-            scaled = grad * gain_ref[...]
+            scaled = grad * gain_ref[...].astype(F32)
             back = scale * (scaled - unit * jnp.mean(scaled * unit, axis=-1, keepdims=True))
             back = back.astype(BF)
             ddelta_ref[rows, lanes] = back
@@ -1899,7 +1899,7 @@
                 states_ref[place_, head] = states[head]
                 delta_ref[rows_at, lanes] = outs[head]
                 scale = lax.rsqrt(jnp.mean(outs[head] * outs[head], axis=-1, keepdims=True) + 1e-05)
-                rows_ref[rows_at, lanes] = (outs[head] * scale * head_gain_ref[...]).astype(BF)
+                rows_ref[rows_at, lanes] = (outs[head] * scale * head_gain_ref[...].astype(F32)).astype(BF)
 
     sent = far_rows_ref.shape[1] // chunk
 
@@ -2060,7 +2060,7 @@
     piece = width // members
     seq_place = lax.axis_index("seq")
 
-    gain_head = head_gain.astype(F32)[None, :]
+    gain_head = head_gain[None, :]
     own = [gate_weight.T, up_weight.T, down_weight.T]
     split = piece < 128
     (

time: 324 us -> 323 us (level)
  no operation moved by 1% of the time
where the time goes in v10:
time: 323 us
  Pallas kernels  322 us (100%)
    pallas_call x1, Pallas kernels, front_stage(): pl.pallas_call(functools.partial(front_kernel, members, heads), name='fro...  98.3 us
    pallas_call x1, Pallas kernels, middle_stage(): pl.pallas_call(functools.partial(middle_kernel, steps), name='middle', gr...  80.6 us
    pallas_call x1, Pallas kernels, final_stage(): pl.pallas_call(functools.partial(final_kernel, members, chunk), name='fin...  49.4 us
    pallas_call x1, Pallas kernels, state_backward(): pl.pallas_call(functools.partial(state_backward_kernel, heads, window), n...  47.3 us
    pallas_call x1, Pallas kernels, mixer_backward(): pl.pallas_call(functools.partial(mixer_backward_kernel, heads), name='mix...  40.8 us

profile of v10, /device:TPU:0, one launch (start us, length us, event | category | flops | bytes accessed | tf_op | source)
XLA Modules:
  0.0 322.7 jit_solution(3416553341484728387)
XLA Ops:
  0.6 98.3 %front.1 = (bf16[1,8,128,896]{3,2,1,0:T(8,128)(2,1)}, bf16[2048,1024]{1,0:T(8,128)(2,1)}, bf16[2048,768]{1,0:T(8,128)(2,1)}, f32[2048,128]{1,0:T(8,128)}, bf16[1...) custom-call(s32[4]{0:T(128)} %lengths_ref.3, ...), custom_call_target="tpu_custom_call" | custom-call | flops 8000000000 | bytes 41943040 | tf_op jit(solution)/shard_map/front/pallas_call | solution.py:1988
  98.9 80.6 %middle.1 = (bf16[2048,256]{1,0:T(8,128)(2,1)}, bf16[2048,1024]{1,0:T(8,128)(2,1)}, f32[2048,256]{1,0:T(8,128)}, f32[2048,256]{1,0:T(8,128)}, bf16[2,8,576,128]{...) custom-call(bf16[2048,256]{1,0:T(8,128)(2,1)} %get-tuple-element.67.row, ...), custom_call_target="tpu_custom_call" | custom-call | flops 30000001024 | bytes 31457280 | tf_op jit(solution)/shard_map/middle/pallas_call | solution.py:905
  179.5 47.3 %state_backward.1 = (bf16[2048,256]{1,0:T(8,128)(2,1)}, f32[8,128]{1,0:T(8,128)}, f32[2,128,128]{2,1,0:T(8,128)}, bf16[2048,256]{1,0:T(8,128)(2,1)}, f32[2,400,128]{2,1,0:T(8,128)}) custom-call(bf16[2048,256]{1,0:T(8,128)(2,1)} %get-tuple-element.73.dheads_ref, f32[2048,256]{1,0:T(8,128)} %get-tuple-element.74.delta_ref, bf16[1,128]{1,0:T(2,128)(2,1)} %bitcast.17, ...), custom_call_target="tpu_custom_call" | custom-call | flops 1000000000 | bytes 31457280 | tf_op jit(solution)/shard_map/state_backward/pallas_call | solution.py:264
  226.8 40.8 %mixer_backward.1 = (bf16[2048,896]{1,0:T(8,128)(2,1)}, f32[4,8,768]{2,1,0:T(8,128)}, f32[2,576,128]{2,1,0:T(8,128)}) custom-call(s32[4]{0:T(128)} %lengths_ref.3, bf16[2048,768]{1,0:T(8,128)(2,1)} %get-tuple-element.82.pre_hbm, bf16[16,768]{1,0:T(8,128)(2,1)} %get-tuple-element.83.halo_ref, bf16[3,4,256]{2,1,0:T(4,128)(2,1)} %conv_ref.3, ...), custom_call_target="tpu_custom_call" | custom-call | flops 3000000000 | bytes 20971520 | tf_op jit(solution)/shard_map/mixer_backward/pallas_call | solution.py:596
  267.7 49.4 %final.1 = (f32[2048,256]{1,0:T(8,128)}, f32[128,896]{1,0:T(8,128)}, f32[16,1024]{1,0:T(8,128)}, f32[2,208,128]{2,1,0:T(8,128)}) custom-call(bf16[2048,1024]{1,0:T(8,128)(2,1)} %get-tuple-element.81.rows_ref, bf16[2048,896]{1,0:T(8,128)(2,1)} %get-tuple-element.92.dpre_ref, bf16[1024,896]{1,0:T(8,128)(2,1)} %bitcast.31, bf16[2048,1024]{1,0:T(8,128)(2,1)} %input_hbm.1, ...), custom_call_target="tpu_custom_call" | custom-call | flops 8000000000 | bytes 31457280 | tf_op jit(solution)/shard_map/final/pallas_call | solution.py:1296
  317.1 5.5 %finish.1 = (bf16[2048,256]{1,0:T(8,128)(2,1)}, f32[2048,256]{1,0:T(8,128)}, f32[1,128]{1,0:T(1,128)}, f32[128,256]{1,0:T(8,128)}, f32[128,256]{1,0:T(8,128)}, /...) custom-call(bf16[2048,256]{1,0:T(8,128)(2,1)} %get-tuple-element.80., ...), custom_call_target="tpu_custom_call" | custom-call | bytes 12582912 | tf_op jit(solution)/shard_map/finish/pallas_call | solution.py:1410
